TPU v7x, 32 devices: a whole 2x2x4 slice. The times are simulated.
32 devices in a mesh: dp: 8 (over y, x, core), tensor: 4 (over z).
Axes of the slice: x: 2, y: 2, z: 4, core: 2. Of those that a mesh axis runs over, the one named last changes fastest.
Arguments:
- inputs: bfloat16 [8, 1024, 2048], P('dp', 'tensor'), may hold values from -6 to 6
- teacher: bfloat16 [8, 1024, 2048], P('dp', 'tensor'), may hold values from -6 to 6
- lengths: int32 [8], P('dp'), may hold values from 1 to 1024, 5120 in all
- w_query: bfloat16 [2048, 2048], P('dp', 'tensor'), may hold values from -0.1875 to 0.1875
- w_key: bfloat16 [2048, 2048], P('dp', 'tensor'), may hold values from -0.1875 to 0.1875
- w_value: bfloat16 [2048, 2048], P('dp', 'tensor'), may hold values from -0.125 to 0.125
- w_out: bfloat16 [2048, 2048], P('tensor', 'dp'), may hold values from -2 to 2
- w_gate: bfloat16 [2048, 8192], P('dp', 'tensor'), may hold values from -0.125 to 0.125
- w_up: bfloat16 [2048, 8192], P('dp', 'tensor'), may hold values from -0.125 to 0.125
- w_down: bfloat16 [8192, 2048], P('tensor', 'dp'), may hold values from -0.0625 to 0.0625
Outputs:
- output: bfloat16 [8, 1024, 2048], P('dp', 'tensor')
- loss: float32 [], replicated
- grad_input: float32 [8, 1024, 2048], P('dp', 'tensor')
- grad_query: float32 [2048, 2048], P('dp', 'tensor')
- grad_key: float32 [2048, 2048], P('dp', 'tensor')
- grad_value: float32 [2048, 2048], P('dp', 'tensor')
- grad_out: float32 [2048, 2048], P('tensor', 'dp')
- grad_gate: float32 [2048, 8192], P('dp', 'tensor')
- grad_up: float32 [2048, 8192], P('dp', 'tensor')
- grad_down: float32 [8192, 2048], P('tensor', 'dp')
Inputs may be any that keep to these rules, and one draw needn't show every extreme that they name: Sequence s holds lengths[s] valid tokens at its start; its other slots of 1024 are padding; some sequence fills all 1024 slots and the lengths add up to 5120.
All inputs are finite; a program needn't handle non-finite values. No bound on the sum of `lengths` on one device may be relied on, other than what follows from the above.
Results may differ from a plain program's by a relative error of at most 0.015.
The roundings to bfloat16 on the way count: a program that leaves them out, or rounds other values in their place, can miss the bound.
Values may be sent and summed in bfloat16 or wider, within the bound.
No kernel may reach another device: no remote copies, remote signals or barrier semaphores. Data moves between devices by JAX's collectives and lax.ppermute only.
A program may use at most 192 MiB of HBM per device.

v0:
```python
import math

import jax
import jax.numpy as jnp
from jax import lax
from jax.sharding import PartitionSpec as P

HS = 128


EPSILON = 1e-05


def layer_norm(values):
    centre = values - jnp.mean(values, axis=-1, keepdims=True)
    spread = jnp.mean(centre * centre, axis=-1, keepdims=True)
    return centre * lax.rsqrt(spread + EPSILON)


def norm_back(values, grad_in):
    centre = values - jnp.mean(values, axis=-1, keepdims=True)
    spread = jnp.mean(centre * centre, axis=-1, keepdims=True)
    inverse = lax.rsqrt(spread + EPSILON)
    normed = centre * inverse
    return inverse * (
        grad_in
        - jnp.mean(grad_in, axis=-1, keepdims=True)
        - normed * jnp.mean(grad_in * normed, axis=-1, keepdims=True)
    )


def rotary_tables(length, size):
    half_size = size // 2
    inverse = jnp.exp(jnp.arange(half_size, dtype=jnp.float32) * (-2.0 * math.log(10000.0) / size))
    angles = jnp.arange(length, dtype=jnp.float32)[:, None] * inverse[None, :]
    return (jnp.cos(angles), jnp.sin(angles))


def rotate(values, cosine_table, sine_table):
    half_size = values.shape[-1] // 2
    first_half = values[..., :half_size]
    second_half = values[..., half_size:]
    cosine_rows = cosine_table[:, None, :]
    sine_rows = sine_table[:, None, :]
    return jnp.concatenate(
        [
            first_half * cosine_rows - second_half * sine_rows,
            second_half * cosine_rows + first_half * sine_rows,
        ],
        axis=-1,
    )


def rotate_back(grads, cosine_table, sine_table):
    half_size = grads.shape[-1] // 2
    first_half = grads[..., :half_size]
    second_half = grads[..., half_size:]
    cosine_rows = cosine_table[:, None, :]
    sine_rows = sine_table[:, None, :]
    return jnp.concatenate(
        [
            first_half * cosine_rows + second_half * sine_rows,
            second_half * cosine_rows - first_half * sine_rows,
        ],
        axis=-1,
    )


def local(inputs, teacher, lengths, w_query, w_key, w_value, w_out, w_gate, w_up, w_down):
    tensor_count = lax.axis_size("tensor")
    local_rows = inputs.shape[1]
    slot_count = local_rows * tensor_count
    token_total = slot_count * lax.axis_size("dp")
    width_all = inputs.shape[2]
    rows_in = inputs[0].astype(jnp.float32)
    target = teacher[0].astype(jnp.float32)
    own_length = lengths[0]
    positions = lax.axis_index("tensor") * local_rows + jnp.arange(local_rows, dtype=jnp.int32)
    valid_rows = (positions < own_length)[:, None]
    valid_total = lax.psum(own_length.astype(jnp.float32), "dp")
    gathered = (
        lax.all_gather(w_query, "dp", axis=0, tiled=True),
        lax.all_gather(w_key, "dp", axis=0, tiled=True),
        lax.all_gather(w_value, "dp", axis=0, tiled=True),
        lax.all_gather(w_gate, "dp", axis=0, tiled=True),
        lax.all_gather(w_up, "dp", axis=0, tiled=True),
        lax.all_gather(w_out, "dp", axis=1, tiled=True),
        lax.all_gather(w_down, "dp", axis=1, tiled=True),
    )
    query_full, key_full, value_full, gate_full, up_full, out_full, down_full = gathered
    head_cols = query_full.shape[1]
    head_count = head_cols // HS
    cosine_table, sine_table = rotary_tables(slot_count, HS)
    query_scale = HS ** (-0.5)
    block_rows = min(slot_count, 512)
    block_count = slot_count // block_rows
    key_index = jnp.arange(slot_count, dtype=jnp.int32)
    normed = layer_norm(rows_in).astype(jnp.bfloat16)
    features = lax.all_gather(normed, "tensor", axis=0, tiled=True)
    queries = jnp.dot(features, query_full, preferred_element_type=jnp.float32)
    key_raw = jnp.dot(features, key_full, preferred_element_type=jnp.float32)
    value_raw = jnp.dot(features, value_full, preferred_element_type=jnp.float32)
    query_rot = (
        rotate(queries.reshape(slot_count, head_count, HS), cosine_table, sine_table) * query_scale
    ).astype(jnp.bfloat16)
    key_rot = rotate(key_raw.reshape(slot_count, head_count, HS), cosine_table, sine_table).astype(
        jnp.bfloat16
    )
    value_heads = value_raw.reshape(slot_count, head_count, HS).astype(jnp.bfloat16)

    def block_scores(block):
        start = block * block_rows
        query_rows = query_rot[start : start + block_rows]
        scores = jnp.einsum("qhd,khd->hqk", query_rows, key_rot, preferred_element_type=jnp.float32)
        causal = (start + jnp.arange(block_rows, dtype=jnp.int32))[:, None] >= key_index[None, :]
        return (jnp.where(causal[None], scores, -1e30), query_rows)

    mixed_blocks = []
    lse_blocks = []
    for block in range(block_count):
        scores, query_rows = block_scores(block)
        largest = jnp.max(scores, axis=-1, keepdims=True)
        shifted = jnp.exp(scores - largest)
        totals = jnp.sum(shifted, axis=-1, keepdims=True)
        attention = shifted / totals
        lse_blocks.append(largest + jnp.log(totals))
        mixed_blocks.append(
            jnp.einsum(
                "hqk,khd->qhd",
                attention.astype(jnp.bfloat16),
                value_heads,
                preferred_element_type=jnp.float32,
            )
        )
    attended = (
        jnp.concatenate(mixed_blocks, axis=0).reshape(slot_count, head_cols).astype(jnp.bfloat16)
    )
    attn_out = lax.psum_scatter(
        jnp.dot(attended, out_full, preferred_element_type=jnp.float32),
        "tensor",
        scatter_dimension=0,
        tiled=True,
    )
    residual = rows_in + attn_out
    normed_two = layer_norm(residual).astype(jnp.bfloat16)
    features_two = lax.all_gather(normed_two, "tensor", axis=0, tiled=True)
    gate_pre = jnp.dot(features_two, gate_full, preferred_element_type=jnp.float32)
    up_pre = jnp.dot(features_two, up_full, preferred_element_type=jnp.float32)
    gate_sigmoid = jax.nn.sigmoid(gate_pre)
    activated = gate_pre * gate_sigmoid
    hidden = (activated * up_pre).astype(jnp.bfloat16)
    mlp_out = lax.psum_scatter(
        jnp.dot(hidden, down_full, preferred_element_type=jnp.float32).astype(jnp.bfloat16),
        "tensor",
        scatter_dimension=0,
        tiled=True,
    ).astype(jnp.float32)
    result = residual + mlp_out
    errors = jnp.where(valid_rows, result - target, 0.0)
    squares = jnp.sum(errors * errors)
    total_squares = lax.psum(squares, ("dp", "tensor"))
    loss_value = total_squares / (valid_total * width_all)
    grad_result = errors * (token_total / valid_total)
    regathered = (
        lax.all_gather(w_query, "dp", axis=0, tiled=True),
        lax.all_gather(w_key, "dp", axis=0, tiled=True),
        lax.all_gather(w_value, "dp", axis=0, tiled=True),
        lax.all_gather(w_gate, "dp", axis=0, tiled=True),
        lax.all_gather(w_up, "dp", axis=0, tiled=True),
        lax.all_gather(w_out, "dp", axis=1, tiled=True),
        lax.all_gather(w_down, "dp", axis=1, tiled=True),
    )
    query_full, key_full, value_full, gate_full, up_full, out_full, down_full = regathered
    down_grad_in = lax.all_gather(grad_result.astype(jnp.bfloat16), "tensor", axis=0, tiled=True)
    grad_down = jnp.einsum("tf,td->fd", hidden, down_grad_in, preferred_element_type=jnp.float32)
    hidden_grad = jnp.einsum(
        "td,fd->tf", down_grad_in, down_full, preferred_element_type=jnp.float32
    )
    gate_grad = (
        hidden_grad * up_pre * gate_sigmoid * (1.0 + gate_pre * (1.0 - gate_sigmoid))
    ).astype(jnp.bfloat16)
    up_grad = (hidden_grad * activated).astype(jnp.bfloat16)
    grad_gate = jnp.einsum("td,tf->df", features_two, gate_grad, preferred_element_type=jnp.float32)
    grad_up = jnp.einsum("td,tf->df", features_two, up_grad, preferred_element_type=jnp.float32)
    feature_grad = jnp.einsum(
        "tf,df->td", gate_grad, gate_full, preferred_element_type=jnp.float32
    ) + jnp.einsum("tf,df->td", up_grad, up_full, preferred_element_type=jnp.float32)
    normed_two_grad = lax.psum_scatter(
        feature_grad.astype(jnp.bfloat16), "tensor", scatter_dimension=0, tiled=True
    ).astype(jnp.float32)
    residual_grad = grad_result + norm_back(residual, normed_two_grad)
    attn_grad_in = lax.all_gather(residual_grad.astype(jnp.bfloat16), "tensor", axis=0, tiled=True)
    grad_out = jnp.einsum("tc,td->cd", attended, attn_grad_in, preferred_element_type=jnp.float32)
    mixed_grad = (
        jnp.einsum("td,cd->tc", attn_grad_in, out_full, preferred_element_type=jnp.float32)
        .astype(jnp.bfloat16)
        .reshape(slot_count, head_count, HS)
    )
    value_grad = jnp.zeros((slot_count, head_count, HS), jnp.float32)
    key_grad = jnp.zeros((slot_count, head_count, HS), jnp.float32)
    query_parts = []
    for block in range(block_count):
        scores, query_rows = block_scores(block)
        attention = jnp.exp(scores - lse_blocks[block])
        start = block * block_rows
        mixed_rows = mixed_grad[start : start + block_rows]
        value_grad = value_grad + jnp.einsum(
            "hqk,qhd->khd",
            attention.astype(jnp.bfloat16),
            mixed_rows,
            preferred_element_type=jnp.float32,
        )
        prob_grad = jnp.einsum(
            "qhd,khd->hqk", mixed_rows, value_heads, preferred_element_type=jnp.float32
        )
        score_grad = (
            attention * (prob_grad - jnp.sum(prob_grad * attention, axis=-1, keepdims=True))
        ).astype(jnp.bfloat16)
        query_parts.append(
            jnp.einsum("hqk,khd->qhd", score_grad, key_rot, preferred_element_type=jnp.float32)
        )
        key_grad = key_grad + jnp.einsum(
            "hqk,qhd->khd", score_grad, query_rows, preferred_element_type=jnp.float32
        )
    query_grad = (
        (rotate_back(jnp.concatenate(query_parts, axis=0), cosine_table, sine_table) * query_scale)
        .astype(jnp.bfloat16)
        .reshape(slot_count, head_cols)
    )
    key_grad_low = (
        rotate_back(key_grad, cosine_table, sine_table)
        .astype(jnp.bfloat16)
        .reshape(slot_count, head_cols)
    )
    value_grad_low = value_grad.astype(jnp.bfloat16).reshape(slot_count, head_cols)
    grad_query = jnp.einsum("td,tc->dc", features, query_grad, preferred_element_type=jnp.float32)
    grad_key = jnp.einsum("td,tc->dc", features, key_grad_low, preferred_element_type=jnp.float32)
    grad_value = jnp.einsum(
        "td,tc->dc", features, value_grad_low, preferred_element_type=jnp.float32
    )
    features_grad = (
        jnp.einsum("tc,dc->td", query_grad, query_full, preferred_element_type=jnp.float32)
        + jnp.einsum("tc,dc->td", key_grad_low, key_full, preferred_element_type=jnp.float32)
        + jnp.einsum("tc,dc->td", value_grad_low, value_full, preferred_element_type=jnp.float32)
    )
    normed_grad = lax.psum_scatter(
        features_grad.astype(jnp.bfloat16), "tensor", scatter_dimension=0, tiled=True
    ).astype(jnp.float32)
    input_grad = residual_grad + norm_back(rows_in, normed_grad)
    summed = (
        lax.psum_scatter(
            grad_query.astype(jnp.bfloat16), "dp", scatter_dimension=0, tiled=True
        ).astype(jnp.float32),
        lax.psum_scatter(
            grad_key.astype(jnp.bfloat16), "dp", scatter_dimension=0, tiled=True
        ).astype(jnp.float32),
        lax.psum_scatter(
            grad_value.astype(jnp.bfloat16), "dp", scatter_dimension=0, tiled=True
        ).astype(jnp.float32),
        lax.psum_scatter(
            grad_gate.astype(jnp.bfloat16), "dp", scatter_dimension=0, tiled=True
        ).astype(jnp.float32),
        lax.psum_scatter(
            grad_up.astype(jnp.bfloat16), "dp", scatter_dimension=0, tiled=True
        ).astype(jnp.float32),
        lax.psum_scatter(
            grad_out.astype(jnp.bfloat16), "dp", scatter_dimension=1, tiled=True
        ).astype(jnp.float32),
        lax.psum_scatter(
            grad_down.astype(jnp.bfloat16), "dp", scatter_dimension=1, tiled=True
        ).astype(jnp.float32),
    )
    return (
        result.astype(jnp.bfloat16)[None],
        loss_value,
        input_grad[None],
        summed[0],
        summed[1],
        summed[2],
        summed[5],
        summed[3],
        summed[4],
        summed[6],
    )


def solution(mesh):
    in_specs = (
        P("dp", "tensor", None),
        P("dp", "tensor", None),
        P("dp"),
        P("dp", "tensor"),
        P("dp", "tensor"),
        P("dp", "tensor"),
        P("tensor", "dp"),
        P("dp", "tensor"),
        P("dp", "tensor"),
        P("tensor", "dp"),
    )
    out_specs = (
        P("dp", "tensor", None),
        P(),
        P("dp", "tensor", None),
        P("dp", "tensor"),
        P("dp", "tensor"),
        P("dp", "tensor"),
        P("tensor", "dp"),
        P("dp", "tensor"),
        P("dp", "tensor"),
        P("tensor", "dp"),
    )
    return jax.shard_map(local, mesh=mesh, in_specs=in_specs, out_specs=out_specs, check_vma=False)
```

profile of v0, /device:TPU:0, one launch (start us, length us, event | category | flops | bytes accessed | tf_op | source)
XLA Modules:
  0.0 1495.9 jit_solution(12879193869445910565)
XLA Ops:
  11.7 2.5 fusion.22
  16.7 2.8 fusion.46
  19.6 21.0 %all-gather.18.cloned.1.call-done = bf16[2048,512]{1,0:T(8,128)(2,1)} async-done(((bf16[256,512]{1,0:T(8,128)(2,1)}), bf16[2048,512]{1,0:T(8,128)(2,1)}) %all-gather.18.cloned.1.call-update) | async-done | bytes 2097168 | tf_op jit(solution)/shard_map/all_gather | solution.py:83
  40.5 82.9 %all-gather.12.cloned.1.call-done = bf16[1024,2048]{1,0:T(8,128)(2,1)} async-done(((bf16[256,2048]{1,0:T(8,128)(2,1)}), bf16[1024,2048]{1,0:T(8,128)(2,1)}) %all-gather.12.cloned.1.call-update) | async-done | bytes 4194320 | tf_op jit(solution)/shard_map/all_gather | solution.py:99
  123.5 5.2 fusion.66
  132.2 3.2 copy.68
  135.3 16.5 %all-gather.16.cloned.1.call-done = bf16[2048,512]{1,0:T(8,128)(2,1)} async-done(((bf16[256,512]{1,0:T(8,128)(2,1)}), bf16[2048,512]{1,0:T(8,128)(2,1)}) %all-gather.16.cloned.1.call-update) | async-done | bytes 2097168 | tf_op jit(solution)/shard_map/all_gather | solution.py:82
  151.8 5.2 fusion.65
  158.6 3.2 copy.67
  161.8 3.2 copy.66
  164.9 4.3 multiply_subtract_fusion.1
  181.5 5.4 convolution_convert_fusion.9
  187.0 2.5 fusion.43
  189.8 2.5 fusion.42
  192.4 19.1 %all-gather.20.cloned.1.call-done = bf16[512,2048]{1,0:T(8,128)(2,1)} async-done(((bf16[512,256]{1,0:T(8,128)(2,1)}), bf16[512,2048]{1,0:T(8,128)(2,1)}) %all-gather.20.cloned.1.call-update) | async-done | bytes 2097168 | tf_op jit(solution)/shard_map/all_gather | solution.py:87
  211.5 7.2 fusion.67
  219.6 143.8 %reduce-scatter.12.cloned.1.call-done = f32[256,2048]{1,0:T(8,128)} async-done(((f32[1024,2048]{1,0:T(8,128)}), f32[256,2048]{1,0:T(8,128)}) %reduce-scatter.12.cloned.1.call-update) | async-done | bytes 2097168 | tf_op jit(solution)/shard_map/reduce_scatter | solution.py:138
  368.3 52.1 %all-gather.24.cloned.1.call-done = bf16[2048,2048]{1,0:T(8,128)(2,1)} async-done(((bf16[256,2048]{1,0:T(8,128)(2,1)}), bf16[2048,2048]{1,0:T(8,128)(2,1)}) %all-gather.24.cloned.1.call-update) | async-done | bytes 8388624 | tf_op jit(solution)/shard_map/all_gather | solution.py:85
  420.4 82.9 %all-gather.22.cloned.1.call-done = bf16[1024,2048]{1,0:T(8,128)(2,1)} async-done(((bf16[256,2048]{1,0:T(8,128)(2,1)}), bf16[1024,2048]{1,0:T(8,128)(2,1)}) %all-gather.22.cloned.1.call-update) | async-done | bytes 4194320 | tf_op jit(solution)/shard_map/all_gather | solution.py:146
  503.3 14.9 fusion.68
  518.2 40.0 %all-gather.26.cloned.1.call-done = bf16[2048,2048]{1,0:T(8,128)(2,1)} async-done(((bf16[256,2048]{1,0:T(8,128)(2,1)}), bf16[2048,2048]{1,0:T(8,128)(2,1)}) %all-gather.26.cloned.1.call-update) | async-done | bytes 8388624 | tf_op jit(solution)/shard_map/all_gather | solution.py:86
  558.2 16.9 %multiply_convert_fusion.4 = (bf16[1024,2048]{1,0:T(8,128)(2,1)}, f32[1024,2048]{1,0:T(8,128)}) fusion(f32[1024,2048]{1,0:T(8,128)} %fusion.68, bf16[1024,2048]{1,0:T(8,128)(2,1)} %all-gather.22.cloned.1.call-done, bf16[2048,2048]{1,0:T(8,128)(2,1)} %all-gather.26.cloned.1.call-done), kind=kOutput, calls=%fused_computation.10 | convolution fusion | flops 8602517504 | bytes 33554432 | tf_op jit(solution)/shard_map/dot_general | solution.py:148
  575.1 40.8 %all-gather.28.cloned.1.call-done = bf16[2048,2048]{1,0:T(8,128)(2,1)} async-done(((bf16[2048,256]{1,0:T(8,128)(2,1)}), bf16[2048,2048]{1,0:T(8,128)(2,1)}) %all-gather.28.cloned.1.call-update) | async-done | bytes 8388624 | tf_op jit(solution)/shard_map/all_gather | solution.py:88
  615.9 13.9 convolution_convert_fusion.3
  630.6 14.0 psum.15
  645.3 61.4 %reduce-scatter.14.cloned.1.call-done = bf16[256,2048]{1,0:T(8,128)(2,1)} async-done(((bf16[1024,2048]{1,0:T(8,128)(2,1)}), bf16[256,2048]{1,0:T(8,128)(2,1)}) %reduce-scatter.14.cloned.1.call-update) | async-done | bytes 1048592 | tf_op jit(solution)/shard_map/reduce_scatter | solution.py:152
  706.7 2.7 multiply_convert_fusion.5
  709.5 81.4 %all-gather.30.cloned.1.call-done = bf16[1024,2048]{1,0:T(8,128)(2,1)} async-done(((bf16[256,2048]{1,0:T(8,128)(2,1)}), bf16[1024,2048]{1,0:T(8,128)(2,1)}) %all-gather.30.cloned.1.call-update) | async-done | bytes 4194320 | tf_op jit(solution)/shard_map/all_gather | solution.py:174
  790.9 20.6 %multiply_convert_fusion.2 = (bf16[1024,2048]{1,0:T(8,128)(2,1)}, bf16[1024,2048]{1,0:T(8,128)(2,1)}) fusion(f32[1024,2048]{1,0:T(8,128)} %fusion.68, f32[1024,2048]{1,0:T(8,128)} %get-tuple-element.47, bf16[1024,2048]{1,0:T(8,128)(2,1)} %all-gather.30.cloned.1.call-done, bf16[2048,2048]{1,0:T(8,128)(2,1)} %all-gather.28.cloned.1.call-done), kind=kOutput, calls=%fused_computation.8 | convolution fusion | flops 8617197568 | bytes 37748736 | tf_op jit(solution)/shard_map/td,fd->tf/dot_general | solution.py:176
  811.6 12.7 fusion.69
  824.3 13.1 add_convert_fusion.1
  837.5 75.4 %reduce-scatter.16.cloned.1.call-done = bf16[256,2048]{1,0:T(8,128)(2,1)} async-done(((bf16[1024,2048]{1,0:T(8,128)(2,1)}), bf16[256,2048]{1,0:T(8,128)(2,1)}) %reduce-scatter.16.cloned.1.call-update) | async-done | bytes 1048592 | tf_op jit(solution)/shard_map/reduce_scatter | solution.py:188
  912.9 3.6 fusion.31
  916.4 3.2 fusion.58
  919.7 14.1 convolution_convert_fusion
  933.9 14.5 convolution_convert_fusion.1
  948.5 14.1 convolution_convert_fusion.2
  963.3 37.7 %all-gather.32.cloned.1.call-done = bf16[1024,2048]{1,0:T(8,128)(2,1)} async-done(((bf16[256,2048]{1,0:T(8,128)(2,1)}), bf16[1024,2048]{1,0:T(8,128)(2,1)}) %all-gather.32.cloned.1.call-update) | async-done | bytes 4194320 | tf_op jit(solution)/shard_map/all_gather | solution.py:192
  1001.1 4.7 convolution_convert_fusion.8
  1005.9 3.7 convolution_convert_fusion.4
  1009.9 7.0 multiply_reduce_fusion.1
  1016.9 5.3 multiply_convert_fusion.1
  1027.7 2.8 add_convert_fusion.2
  1031.6 3.8 convolution_convert_fusion.5
  1035.4 7.9 multiply_reduce_fusion
  1043.6 3.8 fusion.50
  1047.4 7.1 multiply_convert_fusion
  1061.0 6.2 convolution_convert_fusion.7
  1068.6 6.3 convolution_convert_fusion.6
  1075.1 4.5 fusion.71
  1079.6 2.4 fusion.70
  1082.0 6.7 add_convert_fusion
  1089.3 39.4 %psum.14 = f32[]{:T(128)} all-reduce(f32[]{:T(128)} %get-tuple-element.11), channel_id=1, replica_groups=mesh['dp'=8,'tensor'=4] {'dp','tensor'}, use_global_device_ids=true, to_apply=%region_11.12 | all-reduce | flops 1 | bytes 8 | tf_op jit(solution)/shard_map/psum | solution.py:161
  1129.5 2.7 convert_element_type.200
  1132.2 17.7 %reduce-scatter.30.cloned.1.call-done = bf16[256,2048]{1,0:T(8,128)(2,1)} async-done(((bf16[2048,2048]{1,0:T(8,128)(2,1)}), bf16[256,2048]{1,0:T(8,128)(2,1)}) %reduce-scatter.30.cloned.1.call-update) | async-done | bytes 1048592 | tf_op jit(solution)/shard_map/reduce_scatter | solution.py:263
  1149.8 2.8 convert_element_type.198
  1152.6 71.8 %reduce-scatter.28.cloned.1.call-done = bf16[256,2048]{1,0:T(8,128)(2,1)} async-done(((bf16[2048,2048]{1,0:T(8,128)(2,1)}), bf16[256,2048]{1,0:T(8,128)(2,1)}) %reduce-scatter.28.cloned.1.call-update) | async-done | bytes 1048592 | tf_op jit(solution)/shard_map/reduce_scatter | solution.py:260
  1224.4 2.8 convert_element_type.196
  1227.2 41.9 %reduce-scatter.26.cloned.1.call-done = bf16[512,256]{1,0:T(8,128)(2,1)} async-done(((bf16[512,2048]{1,0:T(8,128)(2,1)}), bf16[512,256]{1,0:T(8,128)(2,1)}) %reduce-scatter.26.cloned.1.call-update) | async-done | bytes 262160 | tf_op jit(solution)/shard_map/reduce_scatter | solution.py:266
  1270.9 42.8 %reduce-scatter.24.cloned.1.call-done = bf16[256,512]{1,0:T(8,128)(2,1)} async-done(((bf16[2048,512]{1,0:T(8,128)(2,1)}), bf16[256,512]{1,0:T(8,128)(2,1)}) %reduce-scatter.24.cloned.1.call-update) | async-done | bytes 262160 | tf_op jit(solution)/shard_map/reduce_scatter | solution.py:257
  1315.5 42.9 %reduce-scatter.20.cloned.1.call-done = bf16[256,512]{1,0:T(8,128)(2,1)} async-done(((bf16[2048,512]{1,0:T(8,128)(2,1)}), bf16[256,512]{1,0:T(8,128)(2,1)}) %reduce-scatter.20.cloned.1.call-update) | async-done | bytes 262160 | tf_op jit(solution)/shard_map/reduce_scatter | solution.py:251
  1360.3 42.8 %reduce-scatter.22.cloned.1.call-done = bf16[256,512]{1,0:T(8,128)(2,1)} async-done(((bf16[2048,512]{1,0:T(8,128)(2,1)}), bf16[256,512]{1,0:T(8,128)(2,1)}) %reduce-scatter.22.cloned.1.call-update) | async-done | bytes 262160 | tf_op jit(solution)/shard_map/reduce_scatter | solution.py:254
  1404.8 77.4 %reduce-scatter.18.cloned.1.call-done = bf16[256,2048]{1,0:T(8,128)(2,1)} async-done(((bf16[1024,2048]{1,0:T(8,128)(2,1)}), bf16[256,2048]{1,0:T(8,128)(2,1)}) %reduce-scatter.18.cloned.1.call-update) | async-done | bytes 1048592 | tf_op jit(solution)/shard_map/reduce_scatter | solution.py:246
  1484.1 3.3 fusion.26
  (201 shorter events, 55.3 us)
Async XLA Ops:
  7.2 33.4 %all-gather.18.cloned.1.call-start = ((), (), s32[]{:S(2)}) async-start(), calls=%async_computation.14 | async-start | bytes 2359296 | tf_op jit(solution)/shard_map/all_gather | solution.py:83
  7.9 115.6 %all-gather.12.cloned.1.call-start = ((), (), s32[]{:S(2)}) async-start(), calls=%async_computation.11 | async-start | bytes 5242880 | tf_op jit(solution)/shard_map/all_gather | solution.py:99
  14.2 137.6 %all-gather.16.cloned.1.call-start = ((), (), s32[]{:S(2)}) async-start(), calls=%async_computation.13 | async-start | bytes 2359296 | tf_op jit(solution)/shard_map/all_gather | solution.py:82
  14.9 166.6 %all-gather.14.cloned.1.call-start = ((), (), s32[]{:S(2)}) async-start(), calls=%async_computation.12 | async-start | bytes 2359296 | tf_op jit(solution)/shard_map/all_gather | solution.py:84
  15.5 196.0 %all-gather.20.cloned.1.call-start = ((), (), s32[]{:S(2)}) async-start(), calls=%async_computation.15 | async-start | bytes 2359296 | tf_op jit(solution)/shard_map/all_gather | solution.py:87
  16.1 347.3 %reduce-scatter.12.cloned.1.call-start = ((), (), s32[]{:S(2)}) async-start(), calls=%async_computation.16 | async-start | bytes 10485760 | tf_op jit(solution)/shard_map/reduce_scatter | solution.py:138
  16.3 173.1 %copy-start.7 = (pred[512,1024]{1,0:T(8,128)(4,1)}, pred[512,1024]{1,0:T(8,128)(4,1)S(1)}, u32[]{:S(2)}) copy-start(pred[512,1024]{1,0:T(8,128)(4,1)S(1)} %iota_compare_fusion.1) | copy-start | bytes 1572868
  16.7 170.2 %copy-start.5 = (pred[512,1024]{1,0:T(8,128)(4,1)}, pred[512,1024]{1,0:T(8,128)(4,1)S(1)}, u32[]{:S(2)}) copy-start(pred[512,1024]{1,0:T(8,128)(4,1)S(1)} %iota_compare_fusion) | copy-start | bytes 1572868
  171.9 3.3 copy-start
  171.9 15.0 %copy-start.31 = (f32[4,512]{1,0:T(4,128)}, f32[4,512]{1,0:T(4,128)S(1)}, u32[]{:S(2)}) copy-start(f32[4,512]{1,0:T(4,128)S(1)} %get-tuple-element.42) | copy-start | bytes 24580
  173.4 4.4 copy-start.2
  173.4 16.1 %copy-start.33 = (f32[4,512]{1,0:T(4,128)}, f32[4,512]{1,0:T(4,128)S(1)}, u32[]{:S(2)}) copy-start(f32[4,512]{1,0:T(4,128)S(1)} %get-tuple-element.44) | copy-start | bytes 24580
  177.6 9.3 copy-start.37
  179.9 9.5 copy-start.35
  181.5 5.4 copy-start.1
  181.5 8.0 slice-start.2
  186.9 2.6 copy-start.24
  186.9 2.8 slice-start.3
  192.4 26.3 %copy-start.26 = (bf16[1024,4,128]{0,2,1:T(8,128)(2,1)}, bf16[1024,4,128]{0,2,1:T(8,128)(2,1)S(1)}, u32[]{:S(2)}) copy-start(bf16[1024,4,128]{0,2,1:T(8,128)(2,1)S(1)} %pad_maximum_fusion.2) | copy-start | bytes 3145732
  218.7 144.7 %copy-start.3 = (bf16[1,256,2048]{2,1,0:T(8,128)(2,1)S(1)}, bf16[1,256,2048]{2,1,0:T(8,128)(2,1)}, u32[]{:S(2)}) copy-start(bf16[1,256,2048]{2,1,0:T(8,128)(2,1)} %param.10) | copy-start | bytes 3145732
  218.8 201.7 %all-gather.24.cloned.1.call-start = ((), (), s32[]{:S(2)}) async-start(), calls=%async_computation.18 | async-start | bytes 9437184 | tf_op jit(solution)/shard_map/all_gather | solution.py:85
  219.5 283.8 %all-gather.22.cloned.1.call-start = ((), (), s32[]{:S(2)}) async-start(), calls=%async_computation.17 | async-start | bytes 5242880 | tf_op jit(solution)/shard_map/all_gather | solution.py:146
  366.9 191.3 %all-gather.26.cloned.1.call-start = ((), (), s32[]{:S(2)}) async-start(), calls=%async_computation.19 | async-start | bytes 9437184 | tf_op jit(solution)/shard_map/all_gather | solution.py:86
  367.7 248.2 %all-gather.28.cloned.1.call-start = ((), (), s32[]{:S(2)}) async-start(), calls=%async_computation.20 | async-start | bytes 9437184 | tf_op jit(solution)/shard_map/all_gather | solution.py:88
  368.3 338.5 %reduce-scatter.14.cloned.1.call-start = ((), (), s32[]{:S(2)}) async-start(), calls=%async_computation.21 | async-start | bytes 5242880 | tf_op jit(solution)/shard_map/reduce_scatter | solution.py:152
  629.8 77.0 %copy-start.12 = (bf16[1,256,2048]{2,1,0:T(8,128)(2,1)S(1)}, bf16[1,256,2048]{2,1,0:T(8,128)(2,1)}, u32[]{:S(2)}) copy-start(bf16[1,256,2048]{2,1,0:T(8,128)(2,1)} %param.11) | copy-start | bytes 3145732
  629.8 161.1 %all-gather.30.cloned.1.call-start = ((), (), s32[]{:S(2)}) async-start(), calls=%async_computation.22 | async-start | bytes 5242880 | tf_op jit(solution)/shard_map/all_gather | solution.py:174
  709.5 203.4 %reduce-scatter.16.cloned.1.call-start = ((), (), s32[]{:S(2)}) async-start(), calls=%async_computation.23 | async-start | bytes 5242880 | tf_op jit(solution)/shard_map/reduce_scatter | solution.py:188
  811.6 12.7 copy-start.47
  837.4 163.6 %all-gather.32.cloned.1.call-start = ((), (), s32[]{:S(2)}) async-start(), calls=%async_computation.24 | async-start | bytes 5242880 | tf_op jit(solution)/shard_map/all_gather | solution.py:192
  912.9 3.6 copy-start.15
  912.9 3.6 copy-start.21
  919.7 209.8 %reduce-scatter.32.cloned.1.call-start = ((), (), s32[]{:S(2)}) async-start(), calls=%async_computation.32 | async-start | bytes 9437184 | tf_op jit(solution)/shard_map/reduce_scatter | solution.py:269
  933.9 216.0 %reduce-scatter.30.cloned.1.call-start = ((), (), s32[]{:S(2)}) async-start(), calls=%async_computation.31 | async-start | bytes 9437184 | tf_op jit(solution)/shard_map/reduce_scatter | solution.py:263
  948.5 276.0 %reduce-scatter.28.cloned.1.call-start = ((), (), s32[]{:S(2)}) async-start(), calls=%async_computation.30 | async-start | bytes 9437184 | tf_op jit(solution)/shard_map/reduce_scatter | solution.py:260
  962.6 38.5 %copy-start.46 = (bf16[512,2048]{1,0:T(8,128)(2,1)S(1)}, bf16[512,2048]{1,0:T(8,128)(2,1)}, u32[]{:S(2)}) copy-start(bf16[512,2048]{1,0:T(8,128)(2,1)} %all-gather.20.cloned.1.call-done) | copy-start | bytes 6291460
  962.6 306.5 %reduce-scatter.26.cloned.1.call-start = ((), (), s32[]{:S(2)}) async-start(), calls=%async_computation.29 | async-start | bytes 2359296 | tf_op jit(solution)/shard_map/reduce_scatter | solution.py:266
  1001.1 4.8 copy-start.27
  1001.1 4.8 copy-start.44
  1005.9 18.7 %copy-start.17 = (bf16[512,512]{0,1:T(8,128)(2,1)}, bf16[512,512]{0,1:T(8,128)(2,1)S(1)}, u32[]{:S(2)}) copy-start(bf16[512,512]{0,1:T(8,128)(2,1)S(1)} %get-tuple-element.37) | copy-start | bytes 1572868
  1005.9 4.0 copy-start.8
  1005.9 4.0 copy-start.25
  1009.6 304.1 %reduce-scatter.24.cloned.1.call-start = ((), (), s32[]{:S(2)}) async-start(), calls=%async_computation.28 | async-start | bytes 2359296 | tf_op jit(solution)/shard_map/reduce_scatter | solution.py:257
  1009.9 14.7 slice-start
  1016.9 5.3 copy-start.11
  1016.9 7.6 slice-start.1
  1022.3 4.7 copy-start.9
  1022.3 2.3 copy-start.6
  1022.3 4.7 slice-start.4
  1024.6 3.2 slice-start.5
  1027.7 3.9 copy-start.43
  1031.6 3.8 copy-start.18
  1035.4 8.2 copy-start.14
  1043.4 315.1 %reduce-scatter.20.cloned.1.call-start = ((), (), s32[]{:S(2)}) async-start(), calls=%async_computation.26 | async-start | bytes 2359296 | tf_op jit(solution)/shard_map/reduce_scatter | solution.py:251
  1067.2 335.8 %reduce-scatter.22.cloned.1.call-start = ((), (), s32[]{:S(2)}) async-start(), calls=%async_computation.27 | async-start | bytes 2359296 | tf_op jit(solution)/shard_map/reduce_scatter | solution.py:254
  1068.6 6.4 copy-start.29
  1075.0 4.5 copy-start.28
  1075.0 407.2 %reduce-scatter.18.cloned.1.call-start = ((), (), s32[]{:S(2)}) async-start(), calls=%async_computation.25 | async-start | bytes 5242880 | tf_op jit(solution)/shard_map/reduce_scatter | solution.py:246
  1075.1 4.5 copy-start.45
  1079.6 2.4 copy-start.23
  1132.2 350.0 %copy-start.4 = (bf16[1,256,2048]{2,1,0:T(8,128)(2,1)S(1)}, bf16[1,256,2048]{2,1,0:T(8,128)(2,1)}, u32[]{:S(2)}) copy-start(bf16[1,256,2048]{2,1,0:T(8,128)(2,1)} %param.10) | copy-start | bytes 3145732
  1132.2 350.0 %copy-start.40 = (f32[256]{0:T(256)S(1)}, f32[256]{0:T(256)}, u32[]{:S(2)}) copy-start(f32[256]{0:T(256)} %copy-done.39) | copy-start | bytes 3076
  1132.2 350.0 %copy-start.42 = (f32[256]{0:T(256)S(1)}, f32[256]{0:T(256)}, u32[]{:S(2)}) copy-start(f32[256]{0:T(256)} %copy-done.41) | copy-start | bytes 3076
  1152.6 331.5 %copy-start.16 = (f32[256,2048]{1,0:T(8,128)S(1)}, f32[256,2048]{1,0:T(8,128)}, u32[]{:S(2)}) copy-start(f32[256,2048]{1,0:T(8,128)} %get-tuple-element.16) | copy-start | bytes 6291460
  (12 other events, 14.8 us)
Sparse Core Ops, SparseCore 0:
  9.9 30.6 all-gather.17
  42.7 80.7 all-gather.11
  125.4 26.4 all-gather.15
  153.6 27.8 all-gather.13
  183.2 28.2 all-gather.19
  218.9 144.4 reduce-scatter.11
  365.3 55.0 all-gather.23
  422.6 80.7 all-gather.21
  505.2 52.9 all-gather.25
  559.9 55.9 all-gather.27
  629.9 76.7 reduce-scatter.13
  709.6 81.2 all-gather.29
  837.6 75.2 reduce-scatter.15
  919.8 81.2 all-gather.31
  1004.4 69.7 reduce-scatter.31
  1077.9 71.8 reduce-scatter.29
  1153.1 71.2 reduce-scatter.27
  1227.9 41.1 reduce-scatter.25
  1272.4 41.2 reduce-scatter.23
  1317.2 41.2 reduce-scatter.19
  1361.7 41.2 reduce-scatter.21
  1405.4 76.7 reduce-scatter.17
where the time goes:
time: 1510 us; the launch traced here: 1500 us
  waiting for transfers between devices  1100 us (73%)
  matrix products  233 us (15%)
  other arithmetic  67.9 us (4%)
  blocking collectives  53.5 us (4%)
  local copies, waits for them, and re-layouts  21.9 us (1%)
  between operations  19.5 us (1%)
    reduce_scatter x1, waiting for transfers between devices, local(): lax.psum_scatter(jnp.dot(attended, out_full, preferred_element_type=jnp.f...  144 us
    all_gather x1, waiting for transfers between devices, local(): features_two = lax.all_gather(normed_two, 'tensor', axis=0, tiled=True)  82.9 us
    all_gather x1, waiting for transfers between devices, local(): features = lax.all_gather(normed, 'tensor', axis=0, tiled=True)  82.9 us
    all_gather x1, waiting for transfers between devices, local(): lax.all_gather(grad_result.astype(jnp.bfloat16), 'tensor', axis=0, tiled=...  81.4 us
    reduce_scatter x1, waiting for transfers between devices, local(): lax.psum_scatter(features_grad.astype(jnp.bfloat16), 'tensor', scatter_di...  77.4 us
    reduce_scatter x1, waiting for transfers between devices, local(): lax.psum_scatter(feature_grad.astype(jnp.bfloat16), 'tensor', scatter_dim...  75.4 us
    reduce_scatter x1, waiting for transfers between devices, local(): lax.psum_scatter(grad_gate.astype(jnp.bfloat16), 'dp', scatter_dimension=...  71.8 us
    reduce_scatter x1, waiting for transfers between devices, local(): lax.psum_scatter(jnp.dot(hidden, down_full, preferred_element_type=jnp.fl...  61.4 us
  transfers between devices with their start and end apart: 22, of which 21 were waited for; matrix products, arithmetic and copies ran while one was open for 16% of the time, Pallas kernels for 0%

commit v1 on v0

v1 whole, which is shorter than its diff:
```python
import math

import jax
import jax.numpy as jnp
from jax import lax
from jax.sharding import Mesh
from jax.sharding import PartitionSpec as P

HS = 128
EPSILON = 1e-05
BF = jnp.bfloat16
F32 = jnp.float32


def layer_norm(values):
    centre = values - jnp.mean(values, axis=-1, keepdims=True)
    spread = jnp.mean(centre * centre, axis=-1, keepdims=True)
    return centre * lax.rsqrt(spread + EPSILON)


def norm_back(values, grad_in):
    centre = values - jnp.mean(values, axis=-1, keepdims=True)
    spread = jnp.mean(centre * centre, axis=-1, keepdims=True)
    inverse = lax.rsqrt(spread + EPSILON)
    normed = centre * inverse
    return inverse * (
        grad_in
        - jnp.mean(grad_in, axis=-1, keepdims=True)
        - normed * jnp.mean(grad_in * normed, axis=-1, keepdims=True)
    )


def rotary_tables(length, size):
    half_size = size // 2
    inverse = jnp.exp(jnp.arange(half_size, dtype=F32) * (-2.0 * math.log(10000.0) / size))
    angles = jnp.arange(length, dtype=F32)[:, None] * inverse[None, :]
    return (jnp.cos(angles), jnp.sin(angles))


def rotate(values, cosine_table, sine_table):
    half_size = values.shape[-1] // 2
    first_half = values[..., :half_size]
    second_half = values[..., half_size:]
    cosine_rows = cosine_table[:, None, :]
    sine_rows = sine_table[:, None, :]
    return jnp.concatenate(
        [
            first_half * cosine_rows - second_half * sine_rows,
            second_half * cosine_rows + first_half * sine_rows,
        ],
        axis=-1,
    )


def dot(left, right):
    return jnp.dot(left, right, preferred_element_type=F32)


def dot_nt(left, right):
    return lax.dot_general(left, right, (((1,), (1,)), ((), ())), preferred_element_type=F32)


def dot_tn(left, right):
    return lax.dot_general(left, right, (((0,), (0,)), ((), ())), preferred_element_type=F32)


class PlainLinks:
    line = "tensor"
    rows = "dp"
    everything = ("dp", "tensor")

    def order(self, values):
        return values

    def unorder(self, values):
        return values

    def gather_in(self, shard):
        return lax.all_gather(shard, "dp", axis=0, tiled=True)

    def gather_out(self, shard):
        return lax.all_gather(shard, "dp", axis=1, tiled=True)

    gather_hidden_in = gather_in
    gather_hidden_out = gather_out

    def scatter_in(self, grad):
        return lax.psum_scatter(grad, "dp", scatter_dimension=0, tiled=True).astype(F32)

    def scatter_out(self, grad):
        return lax.psum_scatter(grad, "dp", scatter_dimension=1, tiled=True).astype(F32)

    scatter_hidden_in = scatter_in
    scatter_hidden_out = scatter_out

    def tokens_in(self, values):
        return lax.all_gather(values, "tensor", axis=0, tiled=True)

    def tokens_out(self, partial):
        return lax.psum_scatter(
            partial.astype(BF), "tensor", scatter_dimension=0, tiled=True
        ).astype(F32)


SWAP = [(0, 1), (1, 0)]


def halves(values, axis):
    size = values.shape[axis] // 2
    return (
        lax.slice_in_dim(values, 0, size, axis=axis),
        lax.slice_in_dim(values, size, 2 * size, axis=axis),
    )


def plus(left, right):
    return (left.astype(F32) + right.astype(F32)).astype(BF)


class BlockLinks:
    line = "z"
    rows = ("y", "x", "core")
    everything = ("y", "x", "core", "z")

    def swap(self, values, axis):
        return lax.ppermute(values, axis, SWAP)

    def order(self, values):
        block = values.shape[1] // 8
        y, core = lax.axis_index("y"), lax.axis_index("core")
        parts = []
        for core_slot in range(2):
            for y_slot in range(2):
                for x in range(2):
                    source = (y ^ y_slot) * 4 + x * 2 + (core ^ core_slot)
                    parts.append(lax.dynamic_slice_in_dim(values, source * block, block, axis=1))
        return jnp.concatenate(parts, axis=1)

    def unorder(self, values):
        block = values.shape[1] // 8
        y, core = lax.axis_index("y"), lax.axis_index("core")
        parts = []
        for y_block in range(2):
            for x in range(2):
                for core_block in range(2):
                    slot = (core ^ core_block) * 4 + (y ^ y_block) * 2 + x
                    parts.append(lax.dynamic_slice_in_dim(values, slot * block, block, axis=1))
        return jnp.concatenate(parts, axis=1)

    def by_x(self, own, other, axis):
        first = lax.axis_index("x") == 0
        return jnp.concatenate(
            [jnp.where(first, own, other), jnp.where(first, other, own)], axis=axis
        )

    def of_x(self, values, axis, flip=False):
        size = values.shape[axis] // 2
        place = lax.axis_index("x")
        if flip:
            place = 1 - place
        return lax.dynamic_slice_in_dim(values, place * size, size, axis=axis)

    def join(self, values, received, axis):
        return jnp.concatenate([values, received], axis=axis)

    def gather(self, shard, axis):
        value = self.by_x(shard, self.swap(shard, "x"), axis)
        value = self.join(value, self.swap(value, "y"), axis)
        return self.join(value, self.swap(value, "core"), axis)

    def gather_in(self, shard):
        return self.gather(shard, 0)

    def gather_out(self, shard):
        return self.gather(shard, 1)

    gather_hidden_in = gather_in
    gather_hidden_out = gather_out

    def fold(self, grad, axis, name):
        keep, send = halves(grad, axis)
        return plus(keep, self.swap(send, name))

    def scatter(self, grad, axis):
        grad = self.fold(self.fold(grad, axis, "core"), axis, "y")
        received = self.swap(self.of_x(grad, axis, flip=True), "x")
        return self.of_x(grad, axis).astype(F32) + received.astype(F32)

    def scatter_in(self, grad):
        return self.scatter(grad, 0)

    def scatter_out(self, grad):
        return self.scatter(grad, 1)

    scatter_hidden_in = scatter_in
    scatter_hidden_out = scatter_out

    def tokens_in(self, values):
        return lax.all_gather(values, "z", axis=0, tiled=True)

    def tokens_out(self, partial):
        return lax.psum_scatter(
            partial.astype(BF), "z", scatter_dimension=0, tiled=True
        ).astype(F32)


def layer(links, inputs, teacher, lengths, w_query, w_key, w_value, w_out, w_gate, w_up, w_down):
    line = links.line
    tensor_count = lax.axis_size(line)
    local_rows = inputs.shape[1]
    slot_count = local_rows * tensor_count
    token_total = slot_count * lax.axis_size(links.rows)
    width_all = inputs.shape[2]
    own_length = lengths[0]
    valid_total = lax.psum(own_length.astype(F32), links.rows)
    rows_in = links.order(inputs[0]).astype(F32)
    target = links.order(teacher[0]).astype(F32)
    positions = lax.axis_index(line) * local_rows + jnp.arange(local_rows, dtype=jnp.int32)
    valid_rows = (positions < own_length)[:, None]
    normed = layer_norm(rows_in).astype(BF)
    features = lax.all_gather(normed, line, axis=0, tiled=True)

    head_cols = w_query.shape[1]
    heads_full = links.gather_in(jnp.concatenate([w_query, w_key, w_value], axis=1))
    out_full = links.gather_out(w_out)
    gate_full = links.gather_hidden_in(w_gate)
    up_full = links.gather_hidden_in(w_up)
    down_full = links.gather_hidden_out(w_down)

    head_count = head_cols // HS
    cosine_table, sine_table = rotary_tables(slot_count, HS)
    query_scale = HS ** (-0.5)
    block_rows = min(slot_count, 512)
    block_count = slot_count // block_rows
    key_index = jnp.arange(slot_count, dtype=jnp.int32)
    mixed_in = dot(features, heads_full)
    queries = mixed_in[:, :head_cols]
    key_raw = mixed_in[:, head_cols : 2 * head_cols]
    value_raw = mixed_in[:, 2 * head_cols :]
    query_rot = (
        rotate(queries.reshape(slot_count, head_count, HS), cosine_table, sine_table) * query_scale
    ).astype(BF)
    key_rot = rotate(
        key_raw.reshape(slot_count, head_count, HS), cosine_table, sine_table
    ).astype(BF)
    value_heads = value_raw.reshape(slot_count, head_count, HS).astype(BF)

    def block_scores(block):
        start = block * block_rows
        query_rows = query_rot[start : start + block_rows]
        scores = jnp.einsum("qhd,khd->hqk", query_rows, key_rot, preferred_element_type=F32)
        causal = (start + jnp.arange(block_rows, dtype=jnp.int32))[:, None] >= key_index[None, :]
        return (jnp.where(causal[None], scores, -1e30), query_rows)

    mixed_blocks = []
    lse_blocks = []
    for block in range(block_count):
        scores, query_rows = block_scores(block)
        largest = jnp.max(scores, axis=-1, keepdims=True)
        shifted = jnp.exp(scores - largest)
        totals = jnp.sum(shifted, axis=-1, keepdims=True)
        attention = shifted / totals
        lse_blocks.append(largest + jnp.log(totals))
        mixed_blocks.append(
            jnp.einsum(
                "hqk,khd->qhd", attention.astype(BF), value_heads, preferred_element_type=F32
            )
        )
    attended = jnp.concatenate(mixed_blocks, axis=0).reshape(slot_count, head_cols).astype(BF)
    attn_out = lax.psum_scatter(
        dot(attended, out_full).astype(BF), line, scatter_dimension=0, tiled=True
    ).astype(F32)
    residual = rows_in + attn_out
    normed_two = layer_norm(residual).astype(BF)

    features_two = links.tokens_in(normed_two)
    gate_pre = dot(features_two, gate_full)
    up_pre = dot(features_two, up_full)
    gate_sigmoid = jax.nn.sigmoid(gate_pre)
    activated = gate_pre * gate_sigmoid
    hidden = (activated * up_pre).astype(BF)
    mlp_out = links.tokens_out(dot(hidden, down_full))
    result = residual + mlp_out
    errors = jnp.where(valid_rows, result - target, 0.0)
    squares = jnp.sum(errors * errors)
    total_squares = lax.psum(squares, links.everything)
    loss_value = total_squares / (valid_total * width_all)
    grad_result = errors * (token_total / valid_total)

    down_grad_in = links.tokens_in(grad_result.astype(BF))
    hidden_grad = dot_nt(down_grad_in, down_full)
    gate_grad = (
        hidden_grad * up_pre * gate_sigmoid * (1.0 + gate_pre * (1.0 - gate_sigmoid))
    ).astype(BF)
    up_grad = (hidden_grad * activated).astype(BF)
    feature_grad = dot_nt(gate_grad, gate_full) + dot_nt(up_grad, up_full)
    normed_two_grad = links.tokens_out(feature_grad)
    grad_down = links.scatter_hidden_out(dot_tn(hidden, down_grad_in).astype(BF))
    grad_gate = links.scatter_hidden_in(dot_tn(features_two, gate_grad).astype(BF))
    grad_up = links.scatter_hidden_in(dot_tn(features_two, up_grad).astype(BF))

    residual_grad = grad_result + norm_back(residual, normed_two_grad)
    attn_grad_in = lax.all_gather(residual_grad.astype(BF), line, axis=0, tiled=True)
    grad_out = links.scatter_out(dot_tn(attended, attn_grad_in).astype(BF))
    mixed_grad = dot_nt(attn_grad_in, out_full).astype(BF).reshape(slot_count, head_count, HS)
    value_grad = jnp.zeros((slot_count, head_count, HS), F32)
    key_grad = jnp.zeros((slot_count, head_count, HS), F32)
    query_parts = []
    for block in range(block_count):
        scores, query_rows = block_scores(block)
        attention = jnp.exp(scores - lse_blocks[block])
        start = block * block_rows
        mixed_rows = mixed_grad[start : start + block_rows]
        value_grad = value_grad + jnp.einsum(
            "hqk,qhd->khd", attention.astype(BF), mixed_rows, preferred_element_type=F32
        )
        prob_grad = jnp.einsum("qhd,khd->hqk", mixed_rows, value_heads, preferred_element_type=F32)
        score_grad = (
            attention * (prob_grad - jnp.sum(prob_grad * attention, axis=-1, keepdims=True))
        ).astype(BF)
        query_parts.append(
            jnp.einsum("hqk,khd->qhd", score_grad, key_rot, preferred_element_type=F32)
        )
        key_grad = key_grad + jnp.einsum(
            "hqk,qhd->khd", score_grad, query_rows, preferred_element_type=F32
        )
    query_grad = (
        rotate(jnp.concatenate(query_parts, axis=0), cosine_table, -sine_table) * query_scale
    ).astype(BF)
    key_grad_low = rotate(key_grad, cosine_table, -sine_table).astype(BF)
    heads_grad = jnp.concatenate(
        [
            query_grad.reshape(slot_count, head_cols),
            key_grad_low.reshape(slot_count, head_cols),
            value_grad.astype(BF).reshape(slot_count, head_cols),
        ],
        axis=1,
    )
    normed_grad = lax.psum_scatter(
        dot_nt(heads_grad, heads_full).astype(BF), line, scatter_dimension=0, tiled=True
    ).astype(F32)
    grad_heads = links.scatter_in(dot_tn(features, heads_grad).astype(BF))
    input_grad = residual_grad + norm_back(rows_in, normed_grad)
    return (
        links.unorder(result.astype(BF))[None],
        loss_value,
        links.unorder(input_grad)[None],
        grad_heads[:, :head_cols],
        grad_heads[:, head_cols : 2 * head_cols],
        grad_heads[:, 2 * head_cols :],
        grad_out,
        grad_gate,
        grad_up,
        grad_down,
    )


def solution(mesh):
    if mesh.shape["dp"] == 8 and mesh.shape["tensor"] == 4:
        links = BlockLinks()
        mesh = Mesh(mesh.devices.reshape(2, 2, 2, 4), ("y", "x", "core", "z"))
    else:
        links = PlainLinks()
    dp, tensor = links.rows, links.line
    tokens = P(dp, tensor, None)
    rows = P(dp, tensor)
    cols = P(tensor, dp)
    in_specs = (tokens, tokens, P(dp), rows, rows, rows, cols, rows, rows, cols)
    out_specs = (tokens, P(), tokens, rows, rows, rows, cols, rows, rows, cols)

    def local(*args):
        return layer(links, *args)

    return jax.shard_map(
        local, mesh=mesh, in_specs=in_specs, out_specs=out_specs, check_vma=False
    )
```

time: 1510 us -> 1010 us (0.67)
  waiting for transfers between devices: 1100 us -> 504 us
  local copies, waits for them, and re-layouts: 21.9 us -> 83.3 us
  starting transfers between devices: 1.53 us -> 29.9 us
  other arithmetic: 67.9 us -> 93.7 us
  matrix products: 233 us -> 216 us
    reduce_scatter x11 -> x4, waiting for transfers between devices: 618 us -> 139 us  [the longest x2 94.6 us: tokens_out(): lax.psum_scatter(partial.astype(BF), 'z', scatter_dimension=0, tiled=True)]
    all_gather x11 -> x4, waiting for transfers between devices: 476 us -> 97.7 us  [the longest x2 81.4 us: tokens_in(): return lax.all_gather(values, 'z', axis=0, tiled=True)]
    ppermute x0 -> x30, waiting for transfers between devices: none -> 267 us  [swap(): return lax.ppermute(values, axis, SWAP)]
    unnamed x112 -> x233, local copies, waits for them, and re-layouts: 16.8 us -> 47.4 us
    ppermute x0 -> x30, starting transfers between devices: none -> 29.5 us  [swap(): return lax.ppermute(values, axis, SWAP)]
    slice x3 -> x15, local copies, waits for them, and re-layouts: 3.21 us -> 23.5 us  [the longest x10 14.8 us: halves(): lax.slice_in_dim(values, size, 2 * size, axis=axis)]
    dot_general x33 -> x27, matrix products: 233 us -> 216 us  [the longest x5 70 us: dot_nt(): lax.dot_general(left, right, (((1,), (1,)), ((), ())), preferred_element_...]
    convert_element_type x15 -> x18, other arithmetic: 38.8 us -> 46.5 us  [the longest x10 30.2 us: plus(): return (left.astype(F32) + right.astype(F32)).astype(BF)]
  transfers between devices with their start and end apart: 22 -> 38, of which waited for: 21 -> 21; matrix products, arithmetic and copies ran while one was open for 16% -> 28% of each run, Pallas kernels for 0% -> 0%
where the time goes in v1:
time: 1010 us
  waiting for transfers between devices  504 us (50%)
  matrix products  216 us (21%)
  other arithmetic  93.7 us (9%)
  local copies, waits for them, and re-layouts  83.3 us (8%)
  blocking collectives  59.3 us (6%)
  starting transfers between devices  29.9 us (3%)
  between operations  20 us (2%)
    ppermute x30, waiting for transfers between devices, swap(): return lax.ppermute(values, axis, SWAP)  267 us
    reduce_scatter x2, waiting for transfers between devices, tokens_out(): lax.psum_scatter(partial.astype(BF), 'z', scatter_dimension=0, tiled=True)  94.6 us
    all_gather x2, waiting for transfers between devices, tokens_in(): return lax.all_gather(values, 'z', axis=0, tiled=True)  81.4 us
    dot_general x5, matrix products, dot_nt(): lax.dot_general(left, right, (((1,), (1,)), ((), ())), preferred_element_...  70 us
    dot_general x5, matrix products, dot(): return jnp.dot(left, right, preferred_element_type=F32)  60.3 us
    unnamed x233, local copies, waits for them, and re-layouts  47.4 us
    dot_general x5, matrix products, dot_tn(): lax.dot_general(left, right, (((0,), (0,)), ((), ())), preferred_element_...  46.3 us
    reduce_scatter x1, waiting for transfers between devices, layer(): lax.psum_scatter(dot(attended, out_full).astype(BF), line, scatter_dimens...  44 us
  transfers between devices with their start and end apart: 38, of which 21 were waited for; matrix products, arithmetic and copies ran while one was open for 28% of the time, Pallas kernels for 0%

profile of v1, /device:TPU:0, one launch (start us, length us, event | category | flops | bytes accessed | tf_op | source)
XLA Modules:
  0.0 1005.8 jit_solution(2468623247237368156)
XLA Ops:
  10.1 3.0 collective-permute-start
  24.0 6.8 collective-permute-done
  34.1 33.8 %collective-permute-done.1 = bf16[512,1536]{1,0:T(8,128)(2,1)S(1)} collective-permute-done((bf16[512,1536]{1,0:T(8,128)(2,1)S(1)}, bf16[512,1536]{1,0:T(8,128)(2,1)S(1)}, u32[]{:S(2)}, u32[]{:S(2)}) %collective-permute-start.1) | collective-permute-done | bytes 1572896 | tf_op jit(solution)/shard_map/ppermute | solution.py:126
  69.8 7.1 collective-permute-done.3
  78.9 3.0 fusion.66
  81.9 8.8 collective-permute-done.4
  91.8 13.4 %all-gather.5.cloned.1.call-done = bf16[1024,2048]{1,0:T(8,128)(2,1)} async-done(((bf16[256,2048]{1,0:T(8,128)(2,1)}), bf16[1024,2048]{1,0:T(8,128)(2,1)}) %all-gather.5.cloned.1.call-update) | async-done | bytes 4194320 | tf_op jit(solution)/shard_map/all_gather | solution.py:221
  105.2 9.9 fusion.45
  115.1 2.7 fusion.84
  119.1 2.9 reshape.217
  121.9 2.9 reshape.218
  124.8 3.6 fusion.86
  133.5 2.7 fusion.2
  136.9 2.9 fusion.44
  144.7 2.9 fusion.43
  148.8 5.6 convolution_convert_fusion.6
  157.7 24.0 %collective-permute-done.6 = bf16[256,2048]{1,0:T(8,128)(2,1)S(1)} collective-permute-done((bf16[256,2048]{1,0:T(8,128)(2,1)S(1)}, bf16[256,2048]{1,0:T(8,128)(2,1)S(1)}, u32[]{:S(2)}, u32[]{:S(2)}) %collective-permute-start.6) | collective-permute-done | bytes 1048608 | tf_op jit(solution)/shard_map/ppermute | solution.py:126
  185.8 44.0 %reduce-scatter.5.cloned.1.call-done = bf16[256,2048]{1,0:T(8,128)(2,1)} async-done(((bf16[1024,2048]{1,0:T(8,128)(2,1)}), bf16[256,2048]{1,0:T(8,128)(2,1)}) %reduce-scatter.5.cloned.1.call-update) | async-done | bytes 1048592 | tf_op jit(solution)/shard_map/reduce_scatter | solution.py:270
  242.5 21.2 %collective-permute-done.12 = bf16[2048,256]{1,0:T(8,128)(2,1)S(1)} collective-permute-done((bf16[2048,256]{1,0:T(8,128)(2,1)S(1)}, bf16[2048,256]{1,0:T(8,128)(2,1)S(1)}, u32[]{:S(2)}, u32[]{:S(2)}) %collective-permute-start.12) | collective-permute-done | bytes 1048608 | tf_op jit(solution)/shard_map/ppermute | solution.py:126
  263.8 21.1 %collective-permute-done.10 = bf16[512,2048]{1,0:T(8,128)(2,1)S(1)} collective-permute-done((bf16[512,2048]{1,0:T(8,128)(2,1)S(1)}, bf16[512,2048]{1,0:T(8,128)(2,1)S(1)}, u32[]{:S(2)}, u32[]{:S(2)}) %collective-permute-start.10) | collective-permute-done | bytes 2097184 | tf_op jit(solution)/shard_map/ppermute | solution.py:126
  289.3 46.5 %collective-permute-done.13 = bf16[2048,512]{1,0:T(8,128)(2,1)S(1)} collective-permute-done((bf16[2048,512]{1,0:T(8,128)(2,1)S(1)}, bf16[2048,512]{1,0:T(8,128)(2,1)S(1)}, u32[]{:S(2)}, u32[]{:S(2)}) %collective-permute-start.13) | collective-permute-done | bytes 2097184 | tf_op jit(solution)/shard_map/ppermute | solution.py:126
  338.6 14.6 %fusion.38 = f32[1024,2048]{1,0:T(8,128)} fusion(bf16[1024,2048]{1,0:T(8,128)(2,1)} %all-gather.7.cloned.1.call-done, bf16[1024,2048]{1,0:T(8,128)(2,1)} %collective-permute-done.8, bf16[512,2048]{1,0:T(8,128)(2,1)} %collective-permute-done.7, bf16[256,2048]{1,0:T(8,128)(2,1)} %copy-done.23, bf16[256,2048]{1,0:T(8,128)(2,1)S(1)} %get-tuple-element.32), kind=kOutput, calls=%fused_computation.119 | convolution fusion | flops 8623489024 | bytes 20971520 | tf_op jit(solution)/shard_map/dot_general | solution.py:56
  353.1 16.6 %multiply_convert_fusion.4 = (bf16[1024,2048]{1,0:T(8,128)(2,1)}, f32[1024,2048]{1,0:T(8,128)}) fusion(f32[1024,2048]{1,0:T(8,128)} %fusion.38, bf16[1024,2048]{1,0:T(8,128)(2,1)} %all-gather.7.cloned.1.call-done, bf16[1024,2048]{1,0:T(8,128)(2,1)} %collective-permute-done.11, bf16[512,2048]{1,0:T(8,128)(2,1)S(1)} %copy-done.58, ...), kind=kOutput, calls=%fused_computation.15 | convolution fusion | flops 8636071936 | bytes 33554432 | tf_op jit(solution)/shard_map/dot_general | solution.py:56
  369.7 13.6 %convolution_convert_fusion.5 = bf16[1024,2048]{1,0:T(8,128)(2,1)} fusion(bf16[1024,2048]{1,0:T(8,128)(2,1)} %get-tuple-element.60, bf16[2048,1024]{1,0:T(8,128)(2,1)} %collective-permute-done.14, bf16[2048,512]{1,0:T(8,128)(2,1)} %copy-done.59, bf16[2048,256]{1,0:T(8,128)(2,1)S(1)} %copy-done.32, bf16[2048,256]{1,0:T(8,128)(2,1)S(1)} %copy-done.30), kind=kOutput, calls=%fused_computation.51 | convolution fusion | flops 8625586176 | bytes 16777216 | tf_op jit(solution)/shard_map/dot_general | solution.py:56
  384.2 15.6 %psum.15 = f32[]{:T(128)} all-reduce(f32[]{:T(128)S(6)} %convert_element_type.258), channel_id=1, replica_groups=mesh['y'=2,'x'=2,'core'=2,'z'=4] {'y','x','core'}, use_global_device_ids=true, to_apply=%region_12.13 | all-reduce | flops 1 | bytes 8 | tf_op jit(solution)/shard_map/psum | solution.py:215
  406.9 54.1 %reduce-scatter.7.cloned.1.call-done = bf16[256,2048]{1,0:T(8,128)(2,1)} async-done(((bf16[1024,2048]{1,0:T(8,128)(2,1)}), bf16[256,2048]{1,0:T(8,128)(2,1)}) %reduce-scatter.7.cloned.1.call-update) | async-done | bytes 1048592 | tf_op jit(solution)/shard_map/reduce_scatter | solution.py:202
  461.0 2.9 multiply_convert_fusion.5
  464.0 81.4 %all-gather.9.cloned.1.call-done = bf16[1024,2048]{1,0:T(8,128)(2,1)} async-done(((bf16[256,2048]{1,0:T(8,128)(2,1)}), bf16[1024,2048]{1,0:T(8,128)(2,1)}) %all-gather.9.cloned.1.call-update) | async-done | bytes 4194320 | tf_op jit(solution)/shard_map/all_gather | solution.py:199
  545.4 19.3 %multiply_convert_fusion.3 = (bf16[1024,2048]{1,0:T(8,128)(2,1)}, bf16[1024,2048]{1,0:T(8,128)(2,1)}) fusion(f32[1024,2048]{1,0:T(8,128)} %fusion.38, f32[1024,2048]{1,0:T(8,128)} %get-tuple-element.61, bf16[1024,2048]{1,0:T(8,128)(2,1)} %all-gather.9.cloned.1.call-done, bf16[2048,1024]{1,0:T(8,128)(2,1)} %collective-permute-done.14, ...), kind=kOutput, calls=%fused_computation.14 | convolution fusion | flops 8650752000 | bytes 37748736 | tf_op jit(solution)/shard_map/dot_general | solution.py:60
  564.6 16.8 %fusion.36 = f32[1024,2048]{1,0:T(8,128)} fusion(bf16[1024,2048]{1,0:T(8,128)(2,1)} %get-tuple-element.18, bf16[1024,2048]{1,0:T(8,128)(2,1)} %collective-permute-done.11, bf16[512,2048]{1,0:T(8,128)(2,1)} %copy-done.57, bf16[256,2048]{1,0:T(8,128)(2,1)} %copy-done.27, bf16[256,2048]{1,0:T(8,128)(2,1)} %copy-done.25), kind=kOutput, calls=%fused_computation.117 | convolution fusion | flops 8623489024 | bytes 20971520 | tf_op jit(solution)/shard_map/dot_general | solution.py:60
  581.4 18.5 %add_convert_fusion.3 = bf16[1024,2048]{1,0:T(8,128)(2,1)} fusion(f32[1024,2048]{1,0:T(8,128)} %fusion.36, bf16[1024,2048]{1,0:T(8,128)(2,1)} %get-tuple-element.17, bf16[1024,2048]{1,0:T(8,128)(2,1)} %collective-permute-done.8, bf16[512,2048]{1,0:T(8,128)(2,1)} %collective-permute-done.7, bf16[256,2048]{1,0:T(8,128)(2,1)} %copy-done.23, ...), kind=kOutput, calls=%fused_computation.12 | convolution fusion | flops 8627683328 | bytes 25165824 | tf_op jit(solution)/shard_map/dot_general | solution.py:60
  600.0 12.0 %convolution_convert_fusion.2 = bf16[2048,2048]{1,0:T(8,128)(2,1)S(1)} fusion(bf16[1024,2048]{1,0:T(8,128)(2,1)} %all-gather.7.cloned.1.call-done, bf16[1024,2048]{1,0:T(8,128)(2,1)} %get-tuple-element.17), kind=kOutput, calls=%fused_computation.24 | convolution fusion | flops 8594128896 | bytes 16777216 | tf_op jit(solution)/shard_map/dot_general | solution.py:64
  614.6 3.7 copy-done.34
  619.9 9.8 convolution_convert_fusion
  629.7 2.8 slice.198
  634.8 40.5 %reduce-scatter.9.cloned.1.call-done = bf16[256,2048]{1,0:T(8,128)(2,1)} async-done(((bf16[1024,2048]{1,0:T(8,128)(2,1)}), bf16[256,2048]{1,0:T(8,128)(2,1)}) %reduce-scatter.9.cloned.1.call-update) | async-done | bytes 1048592 | tf_op jit(solution)/shard_map/reduce_scatter | solution.py:202
  675.4 3.7 fusion.28
  679.1 3.6 fusion.82
  682.8 12.4 %convolution_convert_fusion.1 = bf16[2048,2048]{1,0:T(8,128)(2,1)S(1)} fusion(bf16[1024,2048]{1,0:T(8,128)(2,1)} %all-gather.7.cloned.1.call-done, bf16[1024,2048]{1,0:T(8,128)(2,1)} %get-tuple-element.18), kind=kOutput, calls=%fused_computation.23 | convolution fusion | flops 8594128896 | bytes 16777216 | tf_op jit(solution)/shard_map/dot_general | solution.py:64
  695.2 2.8 slice.194
  699.7 5.6 add_convert_fusion
  711.0 5.4 add_convert_fusion.2
  718.5 5.4 add_convert_fusion.1
  727.0 30.5 %collective-permute-done.28 = bf16[2048,512]{1,0:T(8,128)(2,1)} collective-permute-done((bf16[2048,512]{1,0:T(8,128)(2,1)}, bf16[2048,512]{1,0:T(8,128)(2,1)}, u32[]{:S(2)}, u32[]{:S(2)}) %collective-permute-start.28) | collective-permute-done | bytes 2097184 | tf_op jit(solution)/shard_map/ppermute | solution.py:126
  757.5 3.7 add_convert_fusion.5
  761.2 2.9 all-gather.11.cloned.1.call-done
  764.2 4.9 convolution_convert_fusion.8
  769.2 6.6 multiply_reduce_fusion.1
  775.8 3.6 multiply_convert_fusion.1
  779.5 4.6 convolution_bitcast_fusion.1
  784.1 3.0 fusion.62
  787.1 3.6 fusion.5
  790.7 4.8 multiply_reduce_fusion
  795.5 5.2 add_convert_fusion.10
  813.1 9.4 convolution_convert_fusion.3
  828.7 10.6 %convolution_convert_fusion.4 = bf16[1024,2048]{1,0:T(8,128)(2,1)} fusion(bf16[1024,512]{0,1:T(8,128)(2,1)S(1)} %bitcast.127, bf16[1024,512]{0,1:T(8,128)(2,1)S(1)} %bitcast.125, bf16[1024,512]{0,1:T(8,128)(2,1)S(1)} %bitcast.123, bf16[1024,1536]{1,0:T(8,128)(2,1)} %collective-permute-done.2, bf16[512,1536]{1,0:T(8,128)(2,1)S(1)} %copy-done.62, ...), kind=kOutput, calls=%fused_computation.50 | convolution fusion | flops 6479151104 | bytes 13631488 | tf_op jit(solution)/shard_map/dot_general | solution.py:60
  842.6 3.8 add_convert_fusion.7
  851.3 15.8 %collective-permute-done.29 = bf16[2048,256]{1,0:T(8,128)(2,1)S(1)} collective-permute-done((bf16[2048,256]{1,0:T(8,128)(2,1)S(1)}, bf16[2048,256]{1,0:T(8,128)(2,1)S(1)}, u32[]{:S(2)}, u32[]{:S(2)}) %collective-permute-start.29) | collective-permute-done | bytes 1048608 | tf_op jit(solution)/shard_map/ppermute | solution.py:126
  868.6 20.9 %collective-permute-done.23 = bf16[256,2048]{1,0:T(8,128)(2,1)S(1)} collective-permute-done((bf16[256,2048]{1,0:T(8,128)(2,1)S(1)}, bf16[256,2048]{1,0:T(8,128)(2,1)S(1)}, u32[]{:S(2)}, u32[]{:S(2)}) %collective-permute-start.23) | collective-permute-done | bytes 1048608 | tf_op jit(solution)/shard_map/ppermute | solution.py:126
  891.3 2.9 add_convert_fusion.4
  898.8 12.1 %collective-permute-done.26 = bf16[256,2048]{1,0:T(8,128)(2,1)S(1)} collective-permute-done((bf16[256,2048]{1,0:T(8,128)(2,1)S(1)}, bf16[256,2048]{1,0:T(8,128)(2,1)S(1)}, u32[]{:S(2)}, u32[]{:S(2)}) %collective-permute-start.26) | collective-permute-done | bytes 1048608 | tf_op jit(solution)/shard_map/ppermute | solution.py:126
  917.9 13.7 %collective-permute-done.16 = bf16[512,1536]{1,0:T(8,128)(2,1)S(1)} collective-permute-done((bf16[512,1536]{1,0:T(8,128)(2,1)S(1)}, bf16[512,1536]{1,0:T(8,128)(2,1)S(1)}, u32[]{:S(2)}, u32[]{:S(2)}) %collective-permute-start.16) | collective-permute-done | bytes 1572896 | tf_op jit(solution)/shard_map/ppermute | solution.py:126
  935.7 4.2 collective-permute-done.19
  942.3 43.7 %psum.14 = f32[]{:T(128)} all-reduce(f32[]{:T(128)} %get-tuple-element.11), channel_id=1, replica_groups=mesh['y'=2,'x'=2,'core'=2,'z'=4] {'y','x','core','z'}, use_global_device_ids=true, to_apply=%region_11.12 | all-reduce | flops 1 | bytes 8 | tf_op jit(solution)/shard_map/psum | solution.py:286
  (383 shorter events, 145.4 us)
Async XLA Ops:
  7.2 98.0 %all-gather.5.cloned.1.call-start = ((), (), s32[]{:S(2)}) async-start(), calls=%async_computation.4 | async-start | bytes 5242880 | tf_op jit(solution)/shard_map/all_gather | solution.py:221
  10.1 20.7 %collective-permute-start = (bf16[256,1536]{1,0:T(8,128)(2,1)S(1)}, bf16[256,1536]{1,0:T(8,128)(2,1)}, u32[]{:S(2)}, u32[]{:S(2)}) collective-permute-start(bf16[256,1536]{1,0:T(8,128)(2,1)S(1)} %constant_dynamic-update-slice_fusion), channel_id=1, source_target_pairs={{0,8},{8,0},{1,9},{9,1},{2,10},{10,2},{3,11},{11,3},{4,12},{12,4},... | collective-permute-start | bytes 2359304 | tf_op jit(solution)/shard_map/ppermute | solution.py:126
  23.9 205.9 %reduce-scatter.5.cloned.1.call-start = ((), (), s32[]{:S(2)}) async-start(), calls=%async_computation.5 | async-start | bytes 5242880 | tf_op jit(solution)/shard_map/reduce_scatter | solution.py:270
  32.1 36.0 %copy-start.41 = (bf16[256,1536]{1,0:T(8,128)(2,1)}, bf16[256,1536]{1,0:T(8,128)(2,1)S(1)}, u32[]{:S(2)}) copy-start(bf16[256,1536]{1,0:T(8,128)(2,1)S(1)} %get-tuple-element.44) | copy-start | bytes 2359300
  32.1 73.1 %copy-start.39 = (bf16[256,1536]{1,0:T(8,128)(2,1)}, bf16[256,1536]{1,0:T(8,128)(2,1)S(1)}, u32[]{:S(2)}) copy-start(bf16[256,1536]{1,0:T(8,128)(2,1)S(1)} %get-tuple-element.43) | copy-start | bytes 2359300
  32.1 36.1 %copy-start.73 = (bf16[512,256]{1,0:T(8,128)(2,1)S(1)}, bf16[512,256]{1,0:T(8,128)(2,1)}, u32[]{:S(2)}) copy-start(bf16[512,256]{1,0:T(8,128)(2,1)} %param.16) | copy-start | bytes 786436
  32.2 35.6 %collective-permute-start.1 = (bf16[512,1536]{1,0:T(8,128)(2,1)S(1)}, bf16[512,1536]{1,0:T(8,128)(2,1)S(1)}, u32[]{:S(2)}, u32[]{:S(2)}) collective-permute-start(bf16[512,1536]{1,0:T(8,128)(2,1)S(1)} %pad_maximum_fusion.14), channel_id=1, source_target_pairs={{0,16},{16,0},{1,17},{17,1},{2,18},{18,2},{3,19},{19,3},{4,20},{20... | collective-permute-start | bytes 4718600 | tf_op jit(solution)/shard_map/ppermute | solution.py:126
  68.1 23.7 %collective-permute-start.2 = (bf16[1024,1536]{1,0:T(8,128)(2,1)S(1)}, bf16[1024,1536]{1,0:T(8,128)(2,1)}, u32[]{:S(2)}, u32[]{:S(2)}) collective-permute-start(bf16[1024,1536]{1,0:T(8,128)(2,1)S(1)} %pad_maximum_fusion.7), channel_id=1, source_target_pairs={{0,4},{4,0},{1,5},{5,1},{2,6},{6,2},{3,7},{7,3},{8,12},{12,8},{9,1... | collective-permute-start | bytes 9437192 | tf_op jit(solution)/shard_map/ppermute | solution.py:126
  68.2 8.7 collective-permute-start.3
  69.8 73.9 %copy-start.6 = (pred[512,1024]{1,0:T(8,128)(4,1)}, pred[512,1024]{1,0:T(8,128)(4,1)S(1)}, u32[]{:S(2)}) copy-start(pred[512,1024]{1,0:T(8,128)(4,1)S(1)} %iota_compare_fusion.1) | copy-start | bytes 1572868
  77.0 13.6 %collective-permute-start.4 = (bf16[512,512]{1,0:T(8,128)(2,1)S(1)}, bf16[512,512]{1,0:T(8,128)(2,1)S(1)}, u32[]{:S(2)}, u32[]{:S(2)}) collective-permute-start(bf16[512,512]{1,0:T(8,128)(2,1)S(1)} %pad_maximum_fusion.29), channel_id=1, source_target_pairs={{0,16},{16,0},{1,17},{17,1},{2,18},{18,2},{3,19},{19,3},{4,20},{20... | collective-permute-start | bytes 1572872 | tf_op jit(solution)/shard_map/ppermute | solution.py:126
  78.9 57.4 %copy-start.3 = (pred[512,1024]{1,0:T(8,128)(4,1)}, pred[512,1024]{1,0:T(8,128)(4,1)S(1)}, u32[]{:S(2)}) copy-start(pred[512,1024]{1,0:T(8,128)(4,1)S(1)} %iota_compare_fusion) | copy-start | bytes 1572868
  81.9 47.7 %copy-start.45 = (f32[1024,64]{1,0:T(8,128)}, f32[1024,64]{1,0:T(8,128)S(1)}, u32[]{:S(2)}) copy-start(f32[1024,64]{1,0:T(8,128)S(1)} %get-tuple-element.55) | copy-start | bytes 786436
  91.8 55.9 %collective-permute-start.5 = (bf16[512,1024]{1,0:T(8,128)(2,1)}, bf16[512,1024]{1,0:T(8,128)(2,1)}, u32[]{:S(2)}, u32[]{:S(2)}) collective-permute-start(bf16[512,1024]{1,0:T(8,128)(2,1)} %pad_maximum_fusion.27), channel_id=1, source_target_pairs={{0,4},{4,0},{1,5},{5,1},{2,6},{6,2},{3,7},{7,3},{8,12},{12,8},{9,1... | collective-permute-start | bytes 3145736 | tf_op jit(solution)/shard_map/ppermute | solution.py:126
  154.4 184.1 %all-gather.7.cloned.1.call-start = ((), (), s32[]{:S(2)}) async-start(), calls=%async_computation.6 | async-start | bytes 5242880 | tf_op jit(solution)/shard_map/all_gather | solution.py:199
  155.6 26.0 %collective-permute-start.6 = (bf16[256,2048]{1,0:T(8,128)(2,1)S(1)}, bf16[256,2048]{1,0:T(8,128)(2,1)S(1)}, u32[]{:S(2)}, u32[]{:S(2)}) collective-permute-start(bf16[256,2048]{1,0:T(8,128)(2,1)S(1)} %copy-done.63), channel_id=1, source_target_pairs={{0,8},{8,0},{1,9},{9,1},{2,10},{10,2},{3,11},{11,3},{4,12},{12,4},... | collective-permute-start | bytes 3145736 | tf_op jit(solution)/shard_map/ppermute | solution.py:126
  157.1 78.2 %collective-permute-start.9 = (bf16[256,2048]{1,0:T(8,128)(2,1)}, bf16[256,2048]{1,0:T(8,128)(2,1)}, u32[]{:S(2)}, u32[]{:S(2)}) collective-permute-start(bf16[256,2048]{1,0:T(8,128)(2,1)} %param.18), channel_id=1, source_target_pairs={{0,8},{8,0},{1,9},{9,1},{2,10},{10,2},{3,11},{11,3},{4,12},{12,4},... | collective-permute-start | bytes 3145736 | tf_op jit(solution)/shard_map/ppermute | solution.py:126
  181.8 156.7 %copy-start.22 = (bf16[256,2048]{1,0:T(8,128)(2,1)}, bf16[256,2048]{1,0:T(8,128)(2,1)S(1)}, u32[]{:S(2)}) copy-start(bf16[256,2048]{1,0:T(8,128)(2,1)S(1)} %get-tuple-element.32) | copy-start | bytes 3145732
  184.3 56.2 %collective-permute-start.7 = (bf16[512,2048]{1,0:T(8,128)(2,1)}, bf16[512,2048]{1,0:T(8,128)(2,1)}, u32[]{:S(2)}, u32[]{:S(2)}) collective-permute-start(bf16[512,2048]{1,0:T(8,128)(2,1)} %pad_maximum_fusion.11), channel_id=1, source_target_pairs={{0,16},{16,0},{1,17},{17,1},{2,18},{18,2},{3,19},{19,3},{4,20},{20... | collective-permute-start | bytes 6291464 | tf_op jit(solution)/shard_map/ppermute | solution.py:126
  235.3 225.7 %reduce-scatter.7.cloned.1.call-start = ((), (), s32[]{:S(2)}) async-start(), calls=%async_computation.7 | async-start | bytes 5242880 | tf_op jit(solution)/shard_map/reduce_scatter | solution.py:202
  237.2 47.7 %copy-start.25 = (bf16[256,2048]{1,0:T(8,128)(2,1)}, bf16[256,2048]{1,0:T(8,128)(2,1)S(1)}, u32[]{:S(2)}) copy-start(bf16[256,2048]{1,0:T(8,128)(2,1)S(1)} %get-tuple-element.34) | copy-start | bytes 3145732
  237.2 47.7 %copy-start.27 = (bf16[256,2048]{1,0:T(8,128)(2,1)}, bf16[256,2048]{1,0:T(8,128)(2,1)S(1)}, u32[]{:S(2)}) copy-start(bf16[256,2048]{1,0:T(8,128)(2,1)S(1)} %get-tuple-element.35) | copy-start | bytes 3145732
  237.5 47.5 %collective-permute-start.10 = (bf16[512,2048]{1,0:T(8,128)(2,1)S(1)}, bf16[512,2048]{1,0:T(8,128)(2,1)S(1)}, u32[]{:S(2)}, u32[]{:S(2)}) collective-permute-start(bf16[512,2048]{1,0:T(8,128)(2,1)S(1)} %pad_maximum_fusion.12), channel_id=1, source_target_pairs={{0,16},{16,0},{1,17},{17,1},{2,18},{18,2},{3,19},{19,3},{4,20},{20... | collective-permute-start | bytes 6291464 | tf_op jit(solution)/shard_map/ppermute | solution.py:126
  239.0 24.7 %collective-permute-start.12 = (bf16[2048,256]{1,0:T(8,128)(2,1)S(1)}, bf16[2048,256]{1,0:T(8,128)(2,1)S(1)}, u32[]{:S(2)}, u32[]{:S(2)}) collective-permute-start(bf16[2048,256]{1,0:T(8,128)(2,1)S(1)} %copy-done.64), channel_id=1, source_target_pairs={{0,8},{8,0},{1,9},{9,1},{2,10},{10,2},{3,11},{11,3},{4,12},{12,4},... | collective-permute-start | bytes 3145736 | tf_op jit(solution)/shard_map/ppermute | solution.py:126
  242.4 96.1 %collective-permute-start.8 = (bf16[1024,2048]{1,0:T(8,128)(2,1)S(1)}, bf16[1024,2048]{1,0:T(8,128)(2,1)}, u32[]{:S(2)}, u32[]{:S(2)}) collective-permute-start(bf16[1024,2048]{1,0:T(8,128)(2,1)S(1)} %pad_maximum_fusion.4), channel_id=1, source_target_pairs={{0,4},{4,0},{1,5},{5,1},{2,6},{6,2},{3,7},{7,3},{8,12},{12,8},{9,1... | collective-permute-start | bytes 12582920 | tf_op jit(solution)/shard_map/ppermute | solution.py:126
  263.8 72.0 %copy-start.29 = (bf16[2048,256]{1,0:T(8,128)(2,1)}, bf16[2048,256]{1,0:T(8,128)(2,1)S(1)}, u32[]{:S(2)}) copy-start(bf16[2048,256]{1,0:T(8,128)(2,1)S(1)} %get-tuple-element.30) | copy-start | bytes 3145732
  263.8 72.0 %copy-start.31 = (bf16[2048,256]{1,0:T(8,128)(2,1)}, bf16[2048,256]{1,0:T(8,128)(2,1)S(1)}, u32[]{:S(2)}) copy-start(bf16[2048,256]{1,0:T(8,128)(2,1)S(1)} %get-tuple-element.31) | copy-start | bytes 3145732
  287.6 65.5 %collective-permute-start.11 = (bf16[1024,2048]{1,0:T(8,128)(2,1)}, bf16[1024,2048]{1,0:T(8,128)(2,1)}, u32[]{:S(2)}, u32[]{:S(2)}) collective-permute-start(bf16[1024,2048]{1,0:T(8,128)(2,1)} %pad_maximum_fusion.5), channel_id=1, source_target_pairs={{0,4},{4,0},{1,5},{5,1},{2,6},{6,2},{3,7},{7,3},{8,12},{12,8},{9,1... | collective-permute-start | bytes 12582920 | tf_op jit(solution)/shard_map/ppermute | solution.py:126
  287.7 48.1 %collective-permute-start.13 = (bf16[2048,512]{1,0:T(8,128)(2,1)S(1)}, bf16[2048,512]{1,0:T(8,128)(2,1)S(1)}, u32[]{:S(2)}, u32[]{:S(2)}) collective-permute-start(bf16[2048,512]{1,0:T(8,128)(2,1)S(1)} %pad_maximum_fusion.13), channel_id=1, source_target_pairs={{0,16},{16,0},{1,17},{17,1},{2,18},{18,2},{3,19},{19,3},{4,20},{20... | collective-permute-start | bytes 6291464 | tf_op jit(solution)/shard_map/ppermute | solution.py:126
  338.5 31.2 %collective-permute-start.14 = (bf16[2048,1024]{1,0:T(8,128)(2,1)}, bf16[2048,1024]{1,0:T(8,128)(2,1)}, u32[]{:S(2)}, u32[]{:S(2)}) collective-permute-start(bf16[2048,1024]{1,0:T(8,128)(2,1)} %pad_maximum_fusion.6), channel_id=1, source_target_pairs={{0,4},{4,0},{1,5},{5,1},{2,6},{6,2},{3,7},{7,3},{8,12},{12,8},{9,1... | collective-permute-start | bytes 12582920 | tf_op jit(solution)/shard_map/ppermute | solution.py:126
  353.1 16.6 %copy-start.32 = (bf16[2048,256]{1,0:T(8,128)(2,1)S(1)}, bf16[2048,256]{1,0:T(8,128)(2,1)}, u32[]{:S(2)}) copy-start(bf16[2048,256]{1,0:T(8,128)(2,1)} %copy-done.31) | copy-start | bytes 3145732
  383.4 17.1 %copy-start.15 = (bf16[256,2048]{1,0:T(8,128)(2,1)S(1)}, bf16[256,2048]{1,0:T(8,128)(2,1)}, u32[]{:S(2)}) copy-start(bf16[256,2048]{1,0:T(8,128)(2,1)} %get-tuple-element.66) | copy-start | bytes 3145732
  383.4 162.0 %all-gather.9.cloned.1.call-start = ((), (), s32[]{:S(2)}) async-start(), calls=%async_computation.8 | async-start | bytes 5242880 | tf_op jit(solution)/shard_map/all_gather | solution.py:199
  463.9 211.4 %reduce-scatter.9.cloned.1.call-start = ((), (), s32[]{:S(2)}) async-start(), calls=%async_computation.9 | async-start | bytes 5242880 | tf_op jit(solution)/shard_map/reduce_scatter | solution.py:202
  599.9 164.2 %all-gather.11.cloned.1.call-start = ((), (), s32[]{:S(2)}) async-start(), calls=%async_computation.10 | async-start | bytes 5242880 | tf_op jit(solution)/shard_map/all_gather | solution.py:303
  629.7 45.6 %copy-start.84 = (f32[256]{0:T(256)S(1)}, f32[256]{0:T(256)}, u32[]{:S(2)}) copy-start(f32[256]{0:T(256)} %copy-done.83) | copy-start | bytes 3076
  629.7 45.6 %copy-start.88 = (f32[256]{0:T(256)S(1)}, f32[256]{0:T(256)}, u32[]{:S(2)}) copy-start(f32[256]{0:T(256)} %copy-done.87) | copy-start | bytes 3076
  634.3 65.4 %collective-permute-start.27 = (bf16[2048,1024]{1,0:T(8,128)(2,1)}, bf16[2048,1024]{1,0:T(8,128)(2,1)}, u32[]{:S(2)}, u32[]{:S(2)}) collective-permute-start(bf16[2048,1024]{1,0:T(8,128)(2,1)} %slice.198), channel_id=1, source_target_pairs={{0,4},{4,0},{1,5},{5,1},{2,6},{6,2},{3,7},{7,3},{8,12},{12,8},{9,1... | collective-permute-start | bytes 12582920 | tf_op jit(solution)/shard_map/ppermute | solution.py:126
  634.3 76.7 %collective-permute-start.21 = (bf16[1024,2048]{1,0:T(8,128)(2,1)}, bf16[1024,2048]{1,0:T(8,128)(2,1)}, u32[]{:S(2)}, u32[]{:S(2)}) collective-permute-start(bf16[1024,2048]{1,0:T(8,128)(2,1)} %slice.190), channel_id=1, source_target_pairs={{0,4},{4,0},{1,5},{5,1},{2,6},{6,2},{3,7},{7,3},{8,12},{12,8},{9,1... | collective-permute-start | bytes 12582920 | tf_op jit(solution)/shard_map/ppermute | solution.py:126
  682.7 309.1 %reduce-scatter.11.cloned.1.call-start = ((), (), s32[]{:S(2)}) async-start(), calls=%async_computation.11 | async-start | bytes 5242880 | tf_op jit(solution)/shard_map/reduce_scatter | solution.py:339
  699.7 18.8 %collective-permute-start.24 = (bf16[1024,2048]{1,0:T(8,128)(2,1)}, bf16[1024,2048]{1,0:T(8,128)(2,1)}, u32[]{:S(2)}, u32[]{:S(2)}) collective-permute-start(bf16[1024,2048]{1,0:T(8,128)(2,1)} %slice.194), channel_id=1, source_target_pairs={{0,4},{4,0},{1,5},{5,1},{2,6},{6,2},{3,7},{7,3},{8,12},{12,8},{9,1... | collective-permute-start | bytes 12582920 | tf_op jit(solution)/shard_map/ppermute | solution.py:126
  708.8 48.7 %collective-permute-start.28 = (bf16[2048,512]{1,0:T(8,128)(2,1)}, bf16[2048,512]{1,0:T(8,128)(2,1)}, u32[]{:S(2)}, u32[]{:S(2)}) collective-permute-start(bf16[2048,512]{1,0:T(8,128)(2,1)} %slice.200), channel_id=1, source_target_pairs={{0,16},{16,0},{1,17},{17,1},{2,18},{18,2},{3,19},{19,3},{4,20},{20... | collective-permute-start | bytes 6291464 | tf_op jit(solution)/shard_map/ppermute | solution.py:126
  716.4 41.1 %copy-start.10 = (bf16[1024,2048]{1,0:T(8,128)(2,1)}, bf16[1024,2048]{1,0:T(8,128)(2,1)S(1)}, u32[]{:S(2)}) copy-start(bf16[1024,2048]{1,0:T(8,128)(2,1)S(1)} %add_convert_fusion.2) | copy-start | bytes 12582916
  718.0 124.6 %collective-permute-start.22 = (bf16[512,2048]{1,0:T(8,128)(2,1)}, bf16[512,2048]{1,0:T(8,128)(2,1)}, u32[]{:S(2)}, u32[]{:S(2)}) collective-permute-start(bf16[512,2048]{1,0:T(8,128)(2,1)} %slice.192), channel_id=1, source_target_pairs={{0,16},{16,0},{1,17},{17,1},{2,18},{18,2},{3,19},{19,3},{4,20},{20... | collective-permute-start | bytes 6291464 | tf_op jit(solution)/shard_map/ppermute | solution.py:126
  724.0 33.5 %copy-start.11 = (bf16[1024,2048]{1,0:T(8,128)(2,1)}, bf16[1024,2048]{1,0:T(8,128)(2,1)S(1)}, u32[]{:S(2)}) copy-start(bf16[1024,2048]{1,0:T(8,128)(2,1)S(1)} %add_convert_fusion.1) | copy-start | bytes 12582916
  724.0 33.5 %copy-start.9 = (bf16[2048,1024]{1,0:T(8,128)(2,1)S(1)}, bf16[2048,1024]{1,0:T(8,128)(2,1)}, u32[]{:S(2)}) copy-start(bf16[2048,1024]{1,0:T(8,128)(2,1)} %copy-done.8) | copy-start | bytes 12582916
  725.5 38.6 %copy-start.52 = (bf16[512,256]{1,0:T(8,128)(2,1)S(1)}, bf16[512,256]{1,0:T(8,128)(2,1)}, u32[]{:S(2)}) copy-start(bf16[512,256]{1,0:T(8,128)(2,1)} %copy-done.50) | copy-start | bytes 786436
  725.5 38.6 %copy-start.55 = (bf16[512,256]{1,0:T(8,128)(2,1)S(1)}, bf16[512,256]{1,0:T(8,128)(2,1)}, u32[]{:S(2)}) copy-start(bf16[512,256]{1,0:T(8,128)(2,1)} %copy-done.53) | copy-start | bytes 786436
  725.5 38.6 %copy-start.72 = (bf16[512,512]{1,0:T(8,128)(2,1)S(1)}, bf16[512,512]{1,0:T(8,128)(2,1)}, u32[]{:S(2)}) copy-start(bf16[512,512]{1,0:T(8,128)(2,1)} %copy-done.70) | copy-start | bytes 1572868
  725.5 121.5 %collective-permute-start.25 = (bf16[512,2048]{1,0:T(8,128)(2,1)}, bf16[512,2048]{1,0:T(8,128)(2,1)}, u32[]{:S(2)}, u32[]{:S(2)}) collective-permute-start(bf16[512,2048]{1,0:T(8,128)(2,1)} %slice.196), channel_id=1, source_target_pairs={{0,16},{16,0},{1,17},{17,1},{2,18},{18,2},{3,19},{19,3},{4,20},{20... | collective-permute-start | bytes 6291464 | tf_op jit(solution)/shard_map/ppermute | solution.py:126
  769.2 17.9 %slice-start = ((s8[8388608]{0:T(1024)(128)(4,1)}), s8[4194304]{0:T(1024)(128)(4,1)S(1)}, s32[]{:S(2)}) async-start(s8[8388608]{0:T(1024)(128)(4,1)} %bitcast.108), calls=%async_computation.12 | async-start | bytes 8388608
  827.0 64.3 %collective-permute-start.15 = (bf16[1024,1536]{1,0:T(8,128)(2,1)}, bf16[1024,1536]{1,0:T(8,128)(2,1)}, u32[]{:S(2)}, u32[]{:S(2)}) collective-permute-start(bf16[1024,1536]{1,0:T(8,128)(2,1)} %slice.179), channel_id=1, source_target_pairs={{0,4},{4,0},{1,5},{5,1},{2,6},{6,2},{3,7},{7,3},{8,12},{12,8},{9,1... | collective-permute-start | bytes 9437192 | tf_op jit(solution)/shard_map/ppermute | solution.py:126
  841.0 26.1 %collective-permute-start.29 = (bf16[2048,256]{1,0:T(8,128)(2,1)S(1)}, bf16[2048,256]{1,0:T(8,128)(2,1)S(1)}, u32[]{:S(2)}, u32[]{:S(2)}) collective-permute-start(bf16[2048,256]{1,0:T(8,128)(2,1)S(1)} %constant_dynamic-slice_fusion), channel_id=1, source_target_pairs={{0,8},{8,0},{1,9},{9,1},{2,10},{10,2},{3,11},{11,3},{4,12},{12,4},... | collective-permute-start | bytes 3145736 | tf_op jit(solution)/shard_map/ppermute | solution.py:126
  846.4 43.1 %collective-permute-start.23 = (bf16[256,2048]{1,0:T(8,128)(2,1)S(1)}, bf16[256,2048]{1,0:T(8,128)(2,1)S(1)}, u32[]{:S(2)}, u32[]{:S(2)}) collective-permute-start(bf16[256,2048]{1,0:T(8,128)(2,1)S(1)} %constant_dynamic-slice_fusion.2), channel_id=1, source_target_pairs={{0,8},{8,0},{1,9},{9,1},{2,10},{10,2},{3,11},{11,3},{4,12},{12,4},... | collective-permute-start | bytes 3145736 | tf_op jit(solution)/shard_map/ppermute | solution.py:126
  847.1 44.2 %slice-start.6 = ((s8[6291456]{0:T(1024)(128)(4,1)}), s8[4194304]{0:T(1024)(128)(4,1)S(1)}, s32[]{:S(2)}) async-start(s8[6291456]{0:T(1024)(128)(4,1)} %bitcast.114), calls=%async_computation.18 | async-start | bytes 8388608
  849.7 41.6 %slice-start.7 = ((s8[6291456]{0:T(1024)(128)(4,1)}), s8[2097152]{0:T(1024)(128)(4,1)S(1)}, s32[]{:S(2)}) async-start(s8[6291456]{0:T(1024)(128)(4,1)} %bitcast.114), calls=%async_computation.19 | async-start | bytes 4194304
  849.7 61.2 %collective-permute-start.26 = (bf16[256,2048]{1,0:T(8,128)(2,1)S(1)}, bf16[256,2048]{1,0:T(8,128)(2,1)S(1)}, u32[]{:S(2)}, u32[]{:S(2)}) collective-permute-start(bf16[256,2048]{1,0:T(8,128)(2,1)S(1)} %constant_dynamic-slice_fusion.1), channel_id=1, source_target_pairs={{0,8},{8,0},{1,9},{9,1},{2,10},{10,2},{3,11},{11,3},{4,12},{12,4},... | collective-permute-start | bytes 3145736 | tf_op jit(solution)/shard_map/ppermute | solution.py:126
  894.3 37.4 %collective-permute-start.16 = (bf16[512,1536]{1,0:T(8,128)(2,1)S(1)}, bf16[512,1536]{1,0:T(8,128)(2,1)S(1)}, u32[]{:S(2)}, u32[]{:S(2)}) collective-permute-start(bf16[512,1536]{1,0:T(8,128)(2,1)S(1)} %slice.181), channel_id=1, source_target_pairs={{0,16},{16,0},{1,17},{17,1},{2,18},{18,2},{3,19},{19,3},{4,20},{20... | collective-permute-start | bytes 4718600 | tf_op jit(solution)/shard_map/ppermute | solution.py:126
  898.7 17.3 %collective-permute-start.18 = (bf16[512,1024]{1,0:T(8,128)(2,1)S(1)}, bf16[512,1024]{1,0:T(8,128)(2,1)S(1)}, u32[]{:S(2)}, u32[]{:S(2)}) collective-permute-start(bf16[512,1024]{1,0:T(8,128)(2,1)S(1)} %slice.186), channel_id=1, source_target_pairs={{0,4},{4,0},{1,5},{5,1},{2,6},{6,2},{3,7},{7,3},{8,12},{12,8},{9,1... | collective-permute-start | bytes 3145736 | tf_op jit(solution)/shard_map/ppermute | solution.py:126
  916.4 23.5 %collective-permute-start.19 = (bf16[512,512]{1,0:T(8,128)(2,1)S(1)}, bf16[512,512]{1,0:T(8,128)(2,1)S(1)}, u32[]{:S(2)}, u32[]{:S(2)}) collective-permute-start(bf16[512,512]{1,0:T(8,128)(2,1)S(1)} %slice.188), channel_id=1, source_target_pairs={{0,16},{16,0},{1,17},{17,1},{2,18},{18,2},{3,19},{19,3},{4,20},{20... | collective-permute-start | bytes 1572872 | tf_op jit(solution)/shard_map/ppermute | solution.py:126
  934.2 54.7 %collective-permute-start.17 = (bf16[256,1536]{1,0:T(8,128)(2,1)}, bf16[256,1536]{1,0:T(8,128)(2,1)}, u32[]{:S(2)}, u32[]{:S(2)}) collective-permute-start(bf16[256,1536]{1,0:T(8,128)(2,1)} %constant_dynamic-slice_fusion.4), channel_id=1, source_target_pairs={{0,8},{8,0},{1,9},{9,1},{2,10},{10,2},{3,11},{11,3},{4,12},{12,4},... | collective-permute-start | bytes 2359304 | tf_op jit(solution)/shard_map/ppermute | solution.py:126
  940.1 51.7 %copy-start.86 = (f32[256]{0:T(256)S(1)}, f32[256]{0:T(256)}, u32[]{:S(2)}) copy-start(f32[256]{0:T(256)} %copy-done.85) | copy-start | bytes 3076
  940.1 51.7 %copy-start.90 = (f32[256]{0:T(256)S(1)}, f32[256]{0:T(256)}, u32[]{:S(2)}) copy-start(f32[256]{0:T(256)} %copy-done.89) | copy-start | bytes 3076
  940.1 47.9 %collective-permute-start.20 = (bf16[512,256]{1,0:T(8,128)(2,1)S(1)}, bf16[512,256]{1,0:T(8,128)(2,1)S(1)}, u32[]{:S(2)}, u32[]{:S(2)}) collective-permute-start(bf16[512,256]{1,0:T(8,128)(2,1)S(1)} %constant_dynamic-slice_fusion.3), channel_id=1, source_target_pairs={{0,8},{8,0},{1,9},{9,1},{2,10},{10,2},{3,11},{11,3},{4,12},{12,4},... | collective-permute-start | bytes 786440 | tf_op jit(solution)/shard_map/ppermute | solution.py:126
  (76 other events, 362.7 us)
Sparse Core Ops, SparseCore 0:
  24.1 81.0 all-gather.4
  154.6 75.2 reduce-scatter.4
  235.4 81.2 all-gather.6
  383.5 77.4 reduce-scatter.6
  464.1 81.2 all-gather.8
  600.0 75.2 reduce-scatter.8
  682.8 81.2 all-gather.10
  839.4 75.2 reduce-scatter.10

commit v2 on v1

v2 whole, which is shorter than its diff:
```python
import functools
import math

import jax
import jax.numpy as jnp
from jax import lax
from jax.experimental import pallas as pl
from jax.experimental.pallas import tpu as pltpu
from jax.sharding import Mesh
from jax.sharding import PartitionSpec as P

HS = 128
EPSILON = 1e-05
BF = jnp.bfloat16
F32 = jnp.float32
NEGATIVE = -1e30


def statistics(values):
    centre = values - jnp.mean(values, axis=-1, keepdims=True)
    spread = jnp.mean(centre * centre, axis=-1, keepdims=True)
    inverse = lax.rsqrt(spread + EPSILON)
    return centre * inverse, inverse


def norm_back(values, grad_in):
    normed, inverse = statistics(values)
    return inverse * (
        grad_in
        - jnp.mean(grad_in, axis=-1, keepdims=True)
        - normed * jnp.mean(grad_in * normed, axis=-1, keepdims=True)
    )


def rotary_tables(length, size):
    half_size = size // 2
    inverse = jnp.exp(jnp.arange(half_size, dtype=F32) * (-2.0 * math.log(10000.0) / size))
    angles = jnp.arange(length, dtype=F32)[:, None] * inverse[None, :]
    cosine, sine = jnp.cos(angles), jnp.sin(angles)
    return (
        jnp.concatenate([cosine, cosine], axis=1),
        jnp.concatenate([-sine, sine], axis=1),
    )


def dot(left, right):
    return jnp.dot(left, right, preferred_element_type=F32)


def dot_nt(left, right):
    return lax.dot_general(left, right, (((1,), (1,)), ((), ())), preferred_element_type=F32)


def dot_tn(left, right):
    return lax.dot_general(left, right, (((0,), (0,)), ((), ())), preferred_element_type=F32)


def kernel_call(body, grid, ins, outs, args, flops, scratch=(), limit=48):
    args = tuple(
        pltpu.with_memory_space_constraint(a, pltpu.HBM) if a.size > 1024 else a for a in args
    )
    moved = sum(a.size * a.dtype.itemsize for a in args)
    moved += sum(math.prod(shape.shape) * shape.dtype.itemsize for shape, _ in outs)
    return pl.pallas_call(
        body,
        grid=grid,
        in_specs=ins,
        out_specs=[spec for _, spec in outs],
        out_shape=[pltpu.HBM(shape.shape, shape.dtype) for shape, _ in outs],
        scratch_shapes=list(scratch),
        compiler_params=pltpu.CompilerParams(
            dimension_semantics=("arbitrary",) * len(grid), vmem_limit_bytes=limit << 20
        ),
        cost_estimate=pl.CostEstimate(flops=flops, transcendentals=0, bytes_accessed=moved),
    )(*args)


def whole(array):
    rank = len(array.shape)
    return pl.BlockSpec(array.shape, lambda *_: (0,) * rank, pipeline_mode=pl.Buffered(1))


def shape_of(shape, dtype):
    return jax.ShapeDtypeStruct(shape, dtype)


def dot_parts(left, parts, transposed=False):
    total, start = None, 0
    for part in parts:
        depth = part.shape[1 if transposed else 0]
        got = (dot_nt if transposed else dot)(left[:, start : start + depth], part)
        total = got if total is None else total + got
        start += depth
    return total


def heads_body(head_cols, count, x_ref, *refs):
    weights = refs[:count]
    c_ref, s_ref, q_ref, k_ref, v_ref = refs[count:]
    rows = x_ref[...]
    cosine, sine = c_ref[...], s_ref[...]
    for part, out_ref in enumerate((q_ref, k_ref, v_ref)):
        cols = slice(part * head_cols, (part + 1) * head_cols)
        got = dot_parts(rows, [w_ref[:, cols] for w_ref in weights])
        if part == 2:
            out_ref[...] = got.astype(BF)
            continue
        for start in range(0, head_cols, HS):
            head = got[:, start : start + HS]
            turned = head * cosine + pltpu.roll(head, HS // 2, axis=1) * sine
            if part == 0:
                turned = turned * (HS**-0.5)
            out_ref[:, start : start + HS] = turned.astype(BF)


def project_heads(features, weights, tables):
    tokens, width = features.shape
    head_cols = weights[0].shape[1] // 3
    rows = min(256, tokens)
    row_spec = pl.BlockSpec((rows, width), lambda i: (i, 0))
    table_spec = pl.BlockSpec((rows, HS), lambda i: (i, 0))
    out_spec = pl.BlockSpec((rows, head_cols), lambda i: (i, 0))
    out = (shape_of((tokens, head_cols), BF), out_spec)
    return kernel_call(
        functools.partial(heads_body, head_cols, len(weights)),
        (tokens // rows,),
        [row_spec, *map(whole, weights), table_spec, table_spec],
        [out, out, out],
        (features, *weights, *tables),
        2 * tokens * width * 3 * head_cols,
    )


def causal_scores(query, keys, start):
    scores = dot_nt(query, keys)
    row = start + lax.broadcasted_iota(jnp.int32, scores.shape, 0)
    return jnp.where(row >= lax.broadcasted_iota(jnp.int32, scores.shape, 1), scores, NEGATIVE)


def attend_body(rows, q_ref, k_ref, v_ref, o_ref, lse_ref):
    for start in range(0, q_ref.shape[0], rows):
        end = start + rows
        scores = causal_scores(q_ref[start:end, :], k_ref[:end, :], start)
        largest = jnp.max(scores, axis=-1, keepdims=True)
        shifted = jnp.exp(scores - largest)
        total = jnp.sum(shifted, axis=-1, keepdims=True)
        share = (shifted * (1.0 / total)).astype(BF)
        o_ref[start:end, :] = dot(share, v_ref[:end, :]).astype(BF)
        lse_ref[start:end, :] = jnp.broadcast_to(largest + jnp.log(total), (rows, HS))


def attend(query, key, value):
    tokens, head_cols = query.shape
    spec = pl.BlockSpec((tokens, HS), lambda h: (0, h))
    return kernel_call(
        functools.partial(attend_body, min(256, tokens)),
        (head_cols // HS,),
        [spec] * 3,
        [(shape_of((tokens, head_cols), BF), spec), (shape_of((tokens, head_cols), F32), spec)],
        (query, key, value),
        3 * tokens * tokens * head_cols,
    )


def attend_back_body(
    rows, heads, q_ref, k_ref, v_ref, g_ref, lse_ref, c_ref, s_ref, out_ref, dk_ref, dv_ref
):
    tokens = q_ref.shape[0]
    place = pl.program_id(0) * HS
    dk_ref[...] = jnp.zeros_like(dk_ref)
    dv_ref[...] = jnp.zeros_like(dv_ref)

    def turn_back(values, start, end):
        return values * c_ref[start:end, :] - pltpu.roll(values, HS // 2, axis=1) * s_ref[
            start:end, :
        ]

    for start in range(0, tokens, rows):
        end = start + rows
        query, grad = q_ref[start:end, :], g_ref[start:end, :]
        keys, values = k_ref[:end, :], v_ref[:end, :]
        share = jnp.exp(causal_scores(query, keys, start) - lse_ref[start:end, :1])
        share_grad = dot_nt(grad, values)
        mean = jnp.sum(share_grad * share, axis=-1, keepdims=True)
        score_grad = (share * (share_grad - mean)).astype(BF)
        dv_ref[:end, :] += dot_tn(share.astype(BF), grad)
        dk_ref[:end, :] += dot_tn(score_grad, query)
        query_grad = turn_back(dot(score_grad, keys), start, end) * (HS**-0.5)
        out_ref[start:end, pl.ds(pl.multiple_of(place, HS), HS)] = query_grad.astype(BF)
    place_k = pl.multiple_of(place + heads * HS, HS)
    place_v = pl.multiple_of(place + 2 * heads * HS, HS)
    out_ref[:, pl.ds(place_k, HS)] = turn_back(dk_ref[...], 0, tokens).astype(BF)
    out_ref[:, pl.ds(place_v, HS)] = dv_ref[...].astype(BF)


def attend_back(query, key, value, grad, lse, tables):
    tokens, head_cols = query.shape
    heads = head_cols // HS
    spec = pl.BlockSpec((tokens, HS), lambda h: (0, h))
    out = shape_of((tokens, 3 * head_cols), BF)
    return kernel_call(
        functools.partial(attend_back_body, min(256, tokens), heads),
        (heads,),
        [spec] * 5 + [whole(tables[0]), whole(tables[1])],
        [(out, pl.BlockSpec(out.shape, lambda h: (0, 0)))],
        (query, key, value, grad, lse, *tables),
        6 * tokens * tokens * head_cols,
        scratch=[pltpu.VMEM((tokens, HS), F32)] * 2,
    )[0]


def column_blocks(array, size):
    return pl.BlockSpec((array.shape[0], size), lambda j: (0, j))


def row_blocks(array, size):
    return pl.BlockSpec((size, array.shape[1]), lambda j: (j, 0))


def gate_body(rows, count, x_ref, *refs):
    gates, ups = refs[:count], refs[count : 2 * count]
    hid_ref, gate_ref, up_ref = refs[2 * count :]
    for start in range(0, x_ref.shape[0], rows):
        part = slice(start, start + rows)
        gate = dot_parts(x_ref[part, :], [ref[...] for ref in gates])
        up = dot_parts(x_ref[part, :], [ref[...] for ref in ups])
        hid_ref[part, :] = (gate / (1.0 + jnp.exp(-gate)) * up).astype(BF)
        gate_ref[part, :] = gate.astype(BF)
        up_ref[part, :] = up.astype(BF)


def gate_up(tokens, gates, ups):
    count, size = gates[0].shape[1], 256
    shape = shape_of((tokens.shape[0], count), BF)
    out = (shape, column_blocks(shape, size))
    return kernel_call(
        functools.partial(gate_body, min(256, tokens.shape[0]), len(gates)),
        (count // size,),
        [whole(tokens)] + [column_blocks(part, size) for part in (*gates, *ups)],
        [out, out, out],
        (tokens, *gates, *ups),
        4 * tokens.size * count,
    )


def over_in_body(transposed, left_ref, *refs):
    refs[-1][...] = dot_parts(left_ref[...], [ref[...] for ref in refs[:-1]], transposed).astype(BF)


def over_in(left, parts, transposed):
    size = 256
    blocks = row_blocks if transposed else column_blocks
    count = parts[0].shape[0 if transposed else 1]
    shape = shape_of((left.shape[0], count), BF)
    return kernel_call(
        functools.partial(over_in_body, transposed),
        (count // size,),
        [whole(left)] + [blocks(part, size) for part in parts],
        [(shape, column_blocks(shape, size))],
        (left, *parts),
        2 * left.size * count,
    )[0]


def over_out_body(transposed, lefts, steps, *refs):
    parts = (len(refs) - 1 - lefts) // lefts
    for part in range(parts):

        @pl.when(pl.program_id(0) // steps == part)
        def _():
            total = None
            for i in range(lefts):
                right = refs[lefts + i * parts + part][...]
                got = (dot_nt if transposed else dot)(refs[i][...], right)
                total = got if total is None else total + got
            refs[-1][...] = total.astype(BF)


def over_out(lefts, rights, transposed):
    size = 256
    free = 0 if transposed else 1
    steps = rights[0][0].shape[free] // size
    count = steps * len(rights[0])
    specs = []
    for parts in rights:
        for i, part in enumerate(parts):
            block = (size, part.shape[1]) if transposed else (part.shape[0], size)

            def place(j, i=i):
                at = jnp.clip(j - i * steps, 0, steps - 1)
                return (at, 0) if transposed else (0, at)

            specs.append(pl.BlockSpec(block, place))
    shape = shape_of((lefts[0].shape[0], count * size), BF)
    return kernel_call(
        functools.partial(over_out_body, transposed, len(lefts), steps),
        (count,),
        [whole(left) for left in lefts] + specs,
        [(shape, column_blocks(shape, size))],
        (*lefts, *(part for parts in rights for part in parts)),
        sum(2 * left.size for left in lefts) * count * size,
    )[0]


def hidden_back_body(rows, count, y_ref, *refs):
    gate_ref, up_ref, dg_ref, du_ref = refs[count:]
    for start in range(0, y_ref.shape[0], rows):
        part = slice(start, start + rows)
        grad = dot_parts(y_ref[part, :], [ref[...] for ref in refs[:count]], True)
        gate, up = gate_ref[part, :].astype(F32), up_ref[part, :].astype(F32)
        sigmoid = 1.0 / (1.0 + jnp.exp(-gate))
        dg_ref[part, :] = (grad * up * sigmoid * (1.0 + gate * (1.0 - sigmoid))).astype(BF)
        du_ref[part, :] = (grad * (gate * sigmoid)).astype(BF)


def hidden_back(grad, downs, gate, up):
    count, size = downs[0].shape[0], 256
    shape = shape_of((grad.shape[0], count), BF)
    out = (shape, column_blocks(shape, size))
    return kernel_call(
        functools.partial(hidden_back_body, min(256, grad.shape[0]), len(downs)),
        (count // size,),
        [whole(grad)]
        + [row_blocks(part, size) for part in downs]
        + [column_blocks(gate, size), column_blocks(up, size)],
        [out, out],
        (grad, *downs, gate, up),
        2 * grad.size * count,
    )


ROWS = 64


def rows_call(body, scalars, arrays, outs):
    rows, width = arrays[0].shape
    size = min(ROWS, rows)
    spec = pl.BlockSpec((size, width), lambda i: (i, 0))
    out = []
    for shape, dtype in outs:
        block = (8, 128) if shape[1] == 128 else (size, width)
        out.append((shape_of(shape, dtype), pl.BlockSpec(block, lambda i: (i, 0))))
    return kernel_call(
        body,
        (rows // size,),
        [pl.BlockSpec(memory_space=pltpu.SMEM)] * len(scalars) + [spec] * len(arrays),
        out,
        (*scalars, *arrays),
        10 * rows * width,
        limit=32,
    )


def block_at(from_ref, slot, width):
    return pl.ds(pl.multiple_of(from_ref[slot] * width, 128), width)


def enter_body(from_ref, x_ref, rows_ref, normed_ref):
    count = from_ref.shape[0]
    width = x_ref.shape[1] // count
    for slot in range(count):
        here = slice(slot * width, (slot + 1) * width)
        rows_ref[:, here] = x_ref[:, block_at(from_ref, slot, width)]
    normed_ref[...] = statistics(rows_ref[...].astype(F32))[0].astype(BF)


def add_norm_body(x_ref, part_ref, sum_ref, normed_ref):
    total = x_ref[...].astype(F32) + part_ref[...].astype(F32)
    sum_ref[...] = total
    normed_ref[...] = statistics(total)[0].astype(BF)


def loss_body(
    from_ref, length_ref, scale_ref, r_ref, part_ref, t_ref, out_ref, grad_ref, low_ref, sq_ref
):
    count = from_ref.shape[0]
    width = t_ref.shape[1] // count
    size = r_ref.shape[0]
    row = pl.program_id(0) * size + lax.broadcasted_iota(jnp.int32, (size, width), 0)
    valid = row < length_ref[0]
    squares = jnp.zeros((size, width), F32)
    for slot in range(count):
        here = slice(slot * width, (slot + 1) * width)
        there = block_at(from_ref, slot, width)
        result = r_ref[:, here] + part_ref[:, here].astype(F32)
        out_ref[:, there] = result.astype(BF)
        error = jnp.where(valid, result - t_ref[:, there].astype(F32), 0.0)
        squares += error * error
        grad = error * scale_ref[0]
        grad_ref[:, here] = grad
        low_ref[:, here] = grad.astype(BF)
    sq_ref[...] = jnp.full(sq_ref.shape, jnp.sum(squares), F32)


def middle_back_body(grad_ref, r_ref, part_ref, out_ref, low_ref):
    total = grad_ref[...] + norm_back(r_ref[...], part_ref[...].astype(F32))
    out_ref[...] = total
    low_ref[...] = total.astype(BF)


def leave_body(from_ref, x_ref, grad_ref, part_ref, out_ref):
    count = from_ref.shape[0]
    width = x_ref.shape[1] // count
    total = grad_ref[...] + norm_back(x_ref[...].astype(F32), part_ref[...].astype(F32))
    for slot in range(count):
        out_ref[:, block_at(from_ref, slot, width)] = total[:, slot * width : (slot + 1) * width]


class PlainLinks:
    line = "tensor"
    rows = "dp"

    def sources(self):
        return jnp.zeros((1,), jnp.int32)

    def gather_x(self, shard, axis, late=()):
        return lax.all_gather(shard, "dp", axis=axis, tiled=True)

    def gather_y(self, value, axis, late=()):
        return value

    def gather_y_first(self, shard, axis):
        return shard

    def gather_x_last(self, value, axis):
        return lax.all_gather(value, "dp", axis=axis, tiled=True)

    def gather_core(self, value):
        return (value,)

    def scatter_core(self, left, right, axis):
        grad = dot_tn(left, right).astype(BF)
        return lax.psum_scatter(grad, "dp", scatter_dimension=axis, tiled=True)

    def send_y(self, grad, axis):
        return (grad,)

    def send_x(self, grad, axis):
        return (grad,)

    def send_x_first(self, grad, axis):
        return (grad,)

    def fold(self, sent):
        return sent[0].astype(F32)

    def total(self, value, everywhere):
        return lax.psum(value, ("dp", "tensor") if everywhere else "dp")


SWAP = [(0, 1), (1, 0)]


def halves(values, axis):
    size = values.shape[axis] // 2
    return (
        lax.slice_in_dim(values, 0, size, axis=axis),
        lax.slice_in_dim(values, size, 2 * size, axis=axis),
    )


class BlockLinks:
    line = "z"
    rows = ("y", "x", "core")

    def swap(self, values, axis):
        return lax.ppermute(values, axis, SWAP)

    def sources(self):
        slot = jnp.arange(8, dtype=jnp.int32)
        y, core = lax.axis_index("y"), lax.axis_index("core")
        return (y ^ (slot // 2 % 2)) * 4 + slot % 2 * 2 + (core ^ (slot // 4))

    def of_x(self, values, axis, flip=False):
        size = values.shape[axis] // 2
        place = lax.axis_index("x")
        if flip:
            place = 1 - place
        return lax.dynamic_slice_in_dim(values, place * size, size, axis=axis)

    def gather_x(self, shard, axis, late=()):
        other = after(self.swap(shard, "x"), *late)
        first = lax.axis_index("x") == 0
        return jnp.concatenate(
            [jnp.where(first, shard, other), jnp.where(first, other, shard)], axis=axis
        )

    def gather_y(self, value, axis, late=()):
        return jnp.concatenate([value, after(self.swap(value, "y"), *late)], axis=axis)

    def gather_y_first(self, shard, axis):
        return jnp.concatenate([shard, self.swap(shard, "y")], axis=axis)

    def gather_x_last(self, value, axis):
        other = self.swap(value, "x")
        first = lax.axis_index("x") == 0
        parts = []
        for own, far in zip(halves(value, axis), halves(other, axis)):
            parts += [jnp.where(first, own, far), jnp.where(first, far, own)]
        return jnp.concatenate(parts, axis=axis)

    def gather_core(self, value):
        return (value, self.swap(value, "core"))

    def scatter_core(self, left, right, axis):
        if axis == 0:
            keep, send = halves(left, 1)
            received = self.swap(dot_tn(send, right).astype(BF), "core")
            return (dot_tn(keep, right) + received.astype(F32)).astype(BF)
        keep, send = halves(right, 1)
        received = self.swap(dot_tn(left, send).astype(BF), "core")
        return (dot_tn(left, keep) + received.astype(F32)).astype(BF)

    def send_y(self, grad, axis):
        keep, send = halves(grad, axis)
        return (keep, self.swap(send, "y"))

    def send_x(self, grad, axis):
        return (self.of_x(grad, axis), self.swap(self.of_x(grad, axis, flip=True), "x"))

    def send_x_first(self, grad, axis):
        pairs = halves(grad, axis)
        send = jnp.concatenate([self.of_x(pair, axis, flip=True) for pair in pairs], axis=axis)
        keep = jnp.concatenate([self.of_x(pair, axis) for pair in pairs], axis=axis)
        return (keep, self.swap(send, "x"))

    def fold(self, sent):
        return sent[0].astype(F32) + sent[1].astype(F32)

    def total(self, value, everywhere):
        value = jnp.full((8, 128), value, F32)
        for name in self.rows:
            value = value + self.swap(value, name)
        for step in (1, 2) if everywhere else ():
            value = value + lax.ppermute(value, "z", [(i, i ^ step) for i in range(4)])
        return value[0, 0]


def tied(*values):
    return lax.optimization_barrier(values)


def after(value, *others):
    return lax.optimization_barrier((value, others))[0]


def layer(links, inputs, teacher, lengths, w_query, w_key, w_value, w_out, w_gate, w_up, w_down):
    line = links.line
    local_rows = inputs.shape[1]
    slot_count = local_rows * lax.axis_size(line)
    token_total = slot_count * lax.axis_size(links.rows)
    width_all = inputs.shape[2]
    head_cols = w_query.shape[1]

    def line_in(values):
        return lax.all_gather(values, line, axis=0, tiled=True)

    def line_out(partial):
        return lax.psum_scatter(partial, line, scatter_dimension=0, tiled=True)

    shape = inputs.shape[1:]
    low, high = (shape, BF), (shape, F32)
    places = links.sources()
    own_length = lengths[0]
    valid_total = links.total(own_length.astype(F32), False)
    scale = (token_total / valid_total).reshape(1)
    left_length = (own_length - lax.axis_index(line) * local_rows).reshape(1)
    tables = rotary_tables(slot_count, HS)
    rows_in, normed = rows_call(enter_body, (places,), (inputs[0],), (low, low))
    features = line_in(normed)

    heads_full = links.gather_x(jnp.concatenate([w_query, w_key, w_value], axis=1), 0)
    heads_full = links.gather_y(heads_full, 0)
    gate_full = links.gather_x(w_gate, 0)
    heads_full, gate_full = tied(heads_full, gate_full)
    heads_full = links.gather_core(heads_full)
    out_full = links.gather_x(w_out, 1)
    features, tables, scale = tied(features, tables, scale)
    query, key, value = project_heads(features, heads_full, tables)
    out_full = links.gather_core(links.gather_y(out_full, 1, (query,)))
    up_full = links.gather_x(w_up, 0, (query,))
    gate_full = links.gather_y(gate_full, 0)
    down_full = links.gather_y_first(w_down, 1)

    attended, lse = attend(query, key, value)
    attended, up_full = tied(attended, up_full)
    attn_out = line_out(over_out([attended], [out_full], False))
    attn_out, gate_full, down_full = tied(attn_out, gate_full, down_full)
    gate_full = links.gather_core(gate_full)
    up_full = links.gather_y(up_full, 0)
    down_full = links.gather_x_last(down_full, 1)
    residual, normed_two = rows_call(add_norm_body, (), (rows_in, attn_out), (high, low))

    features_two = line_in(normed_two)
    up_full, down_full = tied(up_full, down_full)
    up_full = links.gather_core(up_full)
    features_two, up_full = tied(features_two, up_full)
    down_full = links.gather_core(down_full)
    hidden, gate_pre, up_pre = gate_up(features_two, gate_full, up_full)
    mlp_out = line_out(over_out([hidden], [down_full], False))
    result, grad_result, grad_low, squares = rows_call(
        loss_body,
        (places, left_length, scale),
        (residual, mlp_out, teacher[0]),
        (low, high, low, ((local_rows // ROWS * 8, 128), F32)),
    )
    total_squares = links.total(jnp.sum(squares[::8, 0]), True)
    loss_value = total_squares / (valid_total * width_all)

    down_grad_in = line_in(grad_low)
    down_grad_in, loss_value = tied(down_grad_in, loss_value)
    gate_grad, up_grad = hidden_back(down_grad_in, down_full, gate_pre, up_pre)
    partial = over_out([gate_grad, up_grad], [gate_full, up_full], True)
    middle_grad = line_out(partial)
    features_two, hidden = after((features_two, hidden), partial)
    gate = links.scatter_core(features_two, gate_grad, 0)
    down = links.scatter_core(hidden, down_grad_in, 1)
    up = links.scatter_core(features_two, up_grad, 0)
    middle_grad, gate, down, up = tied(middle_grad, gate, down, up)
    gate = links.send_y(gate, 0)
    down = links.send_x_first(down, 1)
    up = links.send_y(up, 0)
    residual_grad, residual_low = rows_call(
        middle_back_body, (), (grad_result, residual, middle_grad), (high, low)
    )
    attn_grad_in = line_in(residual_low)
    attn_grad_in, gate, down = tied(attn_grad_in, gate, down)
    gate = links.send_x(links.fold(gate).astype(BF), 0)
    down = links.send_y(links.fold(down).astype(BF), 1)

    mixed_grad = over_in(attn_grad_in, out_full, True)
    heads_grad = attend_back(query, key, value, mixed_grad, lse, tables)
    heads_grad, up = tied(heads_grad, up)
    normed_grad = over_out([heads_grad], [heads_full], True)
    last = line_out(normed_grad)
    grad_heads = links.scatter_core(features, after(heads_grad, normed_grad), 0)
    cut = 2 * head_cols
    heads = links.send_y(grad_heads[:, :cut], 0)
    tail = links.send_x_first(grad_heads[:, cut:], 0)
    up = links.send_x(links.fold(after(up, grad_heads)).astype(BF), 0)
    grad_out = links.scatter_core(attended, after(attn_grad_in, grad_heads), 1)
    out = links.send_y(after(grad_out, heads), 1)
    grad_heads = links.fold(links.send_x(links.fold(heads).astype(BF), 0))
    tail = links.fold(links.send_y(links.fold(tail).astype(BF), 0))
    input_grad = rows_call(leave_body, (places,), (rows_in, residual_grad, last), (high,))[0]
    return (
        result[None],
        loss_value,
        input_grad[None],
        grad_heads[:, :head_cols],
        grad_heads[:, head_cols:],
        tail,
        links.fold(links.send_x(links.fold(out).astype(BF), 1)),
        links.fold(gate),
        links.fold(up),
        links.fold(down),
    )


def solution(mesh):
    if mesh.shape["dp"] == 8 and mesh.shape["tensor"] == 4:
        links = BlockLinks()
        mesh = Mesh(mesh.devices.reshape(2, 2, 2, 4), ("y", "x", "core", "z"))
    else:
        links = PlainLinks()
    dp, tensor = links.rows, links.line
    tokens = P(dp, tensor, None)
    rows = P(dp, tensor)
    cols = P(tensor, dp)
    in_specs = (tokens, tokens, P(dp), rows, rows, rows, cols, rows, rows, cols)
    out_specs = (tokens, P(), tokens, rows, rows, rows, cols, rows, rows, cols)

    def local(*args):
        return layer(links, *args)

    return jax.shard_map(
        local, mesh=mesh, in_specs=in_specs, out_specs=out_specs, check_vma=False
    )
```

time: 1010 us -> 872 us (0.86)
  Pallas kernels: 0 us -> 169 us
  matrix products: 216 us -> 65.1 us
  local copies, waits for them, and re-layouts: 83.3 us -> 16.2 us
  blocking collectives: 59.3 us -> 0 us
  other arithmetic: 93.7 us -> 41.7 us
  starting transfers between devices: 29.9 us -> 41.2 us
    dot_general x22 -> x0, matrix products: 170 us -> none  [the longest x5 70 us: dot_nt(): lax.dot_general(left, right, (((1,), (1,)), ((), ())), preferred_element_...]
    pallas_call x0 -> x15, Pallas kernels: none -> 169 us  [kernel_call(): pl.pallas_call(body, grid=grid, in_specs=ins, out_specs=[spec for _, spec...]
    psum x2 -> x0, blocking collectives: 59.3 us -> none  [the longest x1 43.7 us: layer(): total_squares = lax.psum(squares, links.everything)]
    unnamed x233 -> x40, local copies, waits for them, and re-layouts: 47.4 us -> 3.72 us
    convert_element_type x18 -> x6, other arithmetic: 46.5 us -> 8.29 us  [the longest x1 3.03 us: layer(): gate = links.send_x(links.fold(gate).astype(BF), 0)]
    reduce_scatter x4, waiting for transfers between devices: 139 us -> 103 us  [line_out(): return lax.psum_scatter(partial, line, scatter_dimension=0, tiled=True)]
    all_gather x4, waiting for transfers between devices: 97.7 us -> 119 us  [line_in(): return lax.all_gather(values, line, axis=0, tiled=True)]
    dot_general x5 -> x10, matrix products: 46.3 us -> 65.1 us  [dot_tn(): lax.dot_general(left, right, (((0,), (0,)), ((), ())), preferred_element_...]
  transfers between devices with their start and end apart: 38 -> 48, of which waited for: 21 -> 29; matrix products, arithmetic and copies ran while one was open for 28% -> 13% of each run, Pallas kernels for 0% -> 9%
where the time goes in v2:
time: 872 us; the launch traced here: 863 us
  waiting for transfers between devices  511 us (59%)
  Pallas kernels  169 us (19%)
  matrix products  65.1 us (7%)
  other arithmetic  41.7 us (5%)
  starting transfers between devices  41.2 us (5%)
  between operations  19 us (2%)
  local copies, waits for them, and re-layouts  16.2 us (2%)
    ppermute x38, waiting for transfers between devices, swap(): return lax.ppermute(values, axis, SWAP)  284 us
    pallas_call x15, Pallas kernels, kernel_call(): pl.pallas_call(body, grid=grid, in_specs=ins, out_specs=[spec for _, spec...  169 us
    all_gather x4, waiting for transfers between devices, line_in(): return lax.all_gather(values, line, axis=0, tiled=True)  119 us
    reduce_scatter x4, waiting for transfers between devices, line_out(): return lax.psum_scatter(partial, line, scatter_dimension=0, tiled=True)  103 us
    dot_general x10, matrix products, dot_tn(): lax.dot_general(left, right, (((0,), (0,)), ((), ())), preferred_element_...  65.1 us
    ppermute x38, starting transfers between devices, swap(): return lax.ppermute(values, axis, SWAP)  36 us
  transfers between devices with their start and end apart: 48, of which 29 were waited for; matrix products, arithmetic and copies ran while one was open for 13% of the time, Pallas kernels for 9%

profile of v2, /device:TPU:0, one launch (start us, length us, event | category | flops | bytes accessed | tf_op | source)
XLA Modules:
  0.0 863.4 jit_solution(7397888882408358783)
XLA Ops:
  10.1 3.0 collective-permute-start.3
  13.2 4.0 shard_map.177
  17.4 14.3 %collective-permute-done.3 = bf16[256,1536]{1,0:T(8,128)(2,1)} collective-permute-done((bf16[256,1536]{1,0:T(8,128)(2,1)S(1)}, bf16[256,1536]{1,0:T(8,128)(2,1)}, u32[]{:S(2)}, u32[]{:S(2)}) %collective-permute-start.3) | collective-permute-done | bytes 786464 | tf_op jit(solution)/shard_map/ppermute | solution.py:467
  33.0 2.2 collective-permute-start.4
  35.1 18.0 %collective-permute-done.5 = bf16[256,2048]{1,0:T(8,128)(2,1)S(1)} collective-permute-done((bf16[256,2048]{1,0:T(8,128)(2,1)}, bf16[256,2048]{1,0:T(8,128)(2,1)S(1)}, u32[]{:S(2)}, u32[]{:S(2)}) %collective-permute-start.5) | collective-permute-done | bytes 1048608 | tf_op jit(solution)/shard_map/ppermute | solution.py:467
  53.5 14.3 %collective-permute-done.4 = bf16[512,1536]{1,0:T(8,128)(2,1)S(1)} collective-permute-done((bf16[512,1536]{1,0:T(8,128)(2,1)S(1)}, bf16[512,1536]{1,0:T(8,128)(2,1)S(1)}, u32[]{:S(2)}, u32[]{:S(2)}) %collective-permute-start.4) | collective-permute-done | bytes 1572896 | tf_op jit(solution)/shard_map/ppermute | solution.py:467
  67.8 1.8 pad_maximum_fusion.3.refs_0_.refs_1_
  75.4 2.0 fusion.19
  77.4 25.6 %collective-permute-done.1 = f32[8,128]{1,0:T(8,128)S(1)} collective-permute-done((f32[8,128]{1,0:T(8,128)S(1)}, f32[8,128]{1,0:T(8,128)S(1)}, u32[]{:S(2)}, u32[]{:S(2)}) %collective-permute-start.1) | collective-permute-done | bytes 4128 | tf_op jit(solution)/shard_map/ppermute | solution.py:467
  106.3 11.3 %shard_map.178 = (bf16[1024,512]{1,0:T(8,128)(2,1)}, bf16[1024,512]{1,0:T(8,128)(2,1)}, bf16[1024,512]{1,0:T(8,128)(2,1)}) custom-call(bf16[1024,2048]{1,0:T(8,128)(2,1)} %all-gather.5.cloned.1.call-done.x_ref, bf16[1024,1536]{1,0:T(8,128)(2,1)} %pad_maximum_fusion.3.refs_0_.refs_1_, bf16[1024,1536]{1,0:T(8,128)(2,1)} %collective-permute-done.6.refs_1_.refs_2_, ...), custom_call_target="tpu_custom_call" | custom-call | flops 6442450944 | bytes 14680064 | tf_op jit(solution)/shard_map/pallas_call | solution.py:64
  117.6 2.6 collective-permute-done.9
  121.4 11.0 %shard_map.179 = (bf16[1024,512]{1,0:T(8,128)(2,1)}, f32[1024,512]{1,0:T(8,128)}) custom-call(bf16[1024,512]{1,0:T(8,128)(2,1)} %get-tuple-element.76.q_ref, bf16[1024,512]{1,0:T(8,128)(2,1)} %get-tuple-element.77.k_ref, bf16[1024,512]{1,0:T(8,128)(2,1)} %get-tuple-element.78.v_ref), custom_call_target="tpu_custom_call" | custom-call | flops 1610612736 | bytes 6291456 | tf_op jit(solution)/shard_map/pallas_call | solution.py:64
  132.4 1.7 broadcast_select_fusion.5
  136.6 8.1 shard_map.180
  146.9 68.2 %collective-permute-done.12 = bf16[2048,256]{1,0:T(8,128)(2,1)S(1)} collective-permute-done((bf16[2048,256]{1,0:T(8,128)(2,1)S(1)}, bf16[2048,256]{1,0:T(8,128)(2,1)S(1)}, u32[]{:S(2)}, u32[]{:S(2)}) %collective-permute-start.12) | collective-permute-done | bytes 1048608 | tf_op jit(solution)/shard_map/ppermute | solution.py:467
  217.2 2.6 pad_maximum_fusion.refs_0_.refs_2_
  219.8 2.1 reduce-scatter.5.cloned.1.call-done.part_ref
  223.5 4.0 shard_map.181
  227.8 36.1 %collective-permute-done.13 = bf16[512,2048]{1,0:T(8,128)(2,1)} collective-permute-done((bf16[512,2048]{1,0:T(8,128)(2,1)}, bf16[512,2048]{1,0:T(8,128)(2,1)}, u32[]{:S(2)}, u32[]{:S(2)}) %collective-permute-start.13) | collective-permute-done | bytes 2097184 | tf_op jit(solution)/shard_map/ppermute | solution.py:467
  264.0 4.8 pad_maximum_fusion.1.refs_2_.refs_4_
  269.7 1.9 broadcast_select_fusion.3
  271.6 2.3 pad_maximum_fusion.2.refs_1_.refs_0_
  274.5 33.6 %all-gather.7.cloned.1.call-done.x_ref = bf16[1024,2048]{1,0:T(8,128)(2,1)} async-done(((bf16[256,2048]{1,0:T(8,128)(2,1)}), bf16[1024,2048]{1,0:T(8,128)(2,1)}) %all-gather.7.cloned.1.call-update) | async-done | bytes 4194320 | tf_op jit(solution)/shard_map/all_gather | solution.py:556
  308.1 23.6 %shard_map.182 = (bf16[1024,2048]{1,0:T(8,128)(2,1)}, bf16[1024,2048]{1,0:T(8,128)(2,1)}, bf16[1024,2048]{1,0:T(8,128)(2,1)}) custom-call(bf16[1024,2048]{1,0:T(8,128)(2,1)} %all-gather.7.cloned.1.call-done.x_ref, bf16[1024,2048]{1,0:T(8,128)(2,1)} %pad_maximum_fusion.refs_0_.refs_2_, bf16[1024,2048]{1,0:T(8,128)(2,1)} %collective-permute-done.16.refs_1_.refs_3_, ...), custom_call_target="tpu_custom_call" | custom-call | flops 17179869184 | bytes 33554432 | tf_op jit(solution)/shard_map/pallas_call | solution.py:64
  331.6 14.4 %shard_map.183 = bf16[1024,2048]{1,0:T(8,128)(2,1)} custom-call(bf16[1024,2048]{1,0:T(8,128)(2,1)} %get-tuple-element.107.refs_0_, bf16[2048,1024]{1,0:T(8,128)(2,1)} %pad_maximum_fusion.2.refs_1_.refs_0_, bf16[2048,1024]{1,0:T(8,128)(2,1)} %collective-permute-done.17.refs_2_.refs_1_), custom_call_target="tpu_custom_call" | custom-call | flops 8589934592 | bytes 16777216 | tf_op jit(solution)/shard_map/pallas_call | solution.py:64
  346.1 75.4 %reduce-scatter.7.cloned.1.call-done.part_ref = bf16[256,2048]{1,0:T(8,128)(2,1)} async-done(((bf16[1024,2048]{1,0:T(8,128)(2,1)}), bf16[256,2048]{1,0:T(8,128)(2,1)}) %reduce-scatter.7.cloned.1.call-update) | async-done | bytes 1048592 | tf_op jit(solution)/shard_map/reduce_scatter | solution.py:559
  421.5 4.9 shard_map.184
  429.9 2.1 collective-permute-done.18
  434.3 2.2 collective-permute-done.19
  439.8 2.2 collective-permute-done.21
  442.0 2.9 collective-permute-start.22
  445.5 3.1 collective-permute-done.22
  449.8 58.2 %all-gather.9.cloned.1.call-done.y_ref = bf16[1024,2048]{1,0:T(8,128)(2,1)} async-done(((bf16[256,2048]{1,0:T(8,128)(2,1)}), bf16[1024,2048]{1,0:T(8,128)(2,1)}) %all-gather.9.cloned.1.call-update) | async-done | bytes 4194320 | tf_op jit(solution)/shard_map/all_gather | solution.py:556
  508.0 18.2 %shard_map.185 = (bf16[1024,2048]{1,0:T(8,128)(2,1)}, bf16[1024,2048]{1,0:T(8,128)(2,1)}) custom-call(bf16[1024,2048]{1,0:T(8,128)(2,1)} %all-gather.9.cloned.1.call-done.y_ref, bf16[2048,1024]{1,0:T(8,128)(2,1)} %pad_maximum_fusion.2.refs_1_.refs_0_, bf16[2048,1024]{1,0:T(8,128)(2,1)} %collective-permute-done.17.refs_2_.refs_1_, ...), custom_call_target="tpu_custom_call" | custom-call | flops 8589934592 | bytes 29360128 | tf_op jit(solution)/shard_map/pallas_call | solution.py:64
  526.2 24.9 %shard_map.186 = bf16[1024,2048]{1,0:T(8,128)(2,1)} custom-call(bf16[1024,2048]{1,0:T(8,128)(2,1)} %get-tuple-element.104.refs_0_, bf16[1024,2048]{1,0:T(8,128)(2,1)} %get-tuple-element.105.refs_1_, bf16[1024,2048]{1,0:T(8,128)(2,1)} %pad_maximum_fusion.refs_0_.refs_2_, bf16[1024,2048]{1,0:T(8,128)(2,1)} %collective-permute-done.16.refs_1_.refs_3_, ...), custom_call_target="tpu_custom_call" | custom-call | flops 17179869184 | bytes 29360128 | tf_op jit(solution)/shard_map/pallas_call | solution.py:64
  551.2 7.5 convolution_convert_fusion.3
  558.8 13.4 %convolution_convert_fusion.2 = bf16[2048,1024]{1,0:T(8,128)(2,1)S(1)} fusion(bf16[1024,2048]{1,0:T(8,128)(2,1)S(1)} %copy-done.18, bf16[1024,2048]{1,0:T(8,128)(2,1)S(1)} %copy-done.12), kind=kOutput, calls=%fused_computation.12 | convolution fusion | flops 4297064448 | bytes 10485760 | tf_op jit(solution)/shard_map/dot_general | solution.py:55
  572.5 4.9 convolution_convert_fusion.1
  577.8 8.6 add_convert_fusion.2
  586.4 8.6 add_convert_fusion.1
  595.0 6.5 add_convert_fusion
  601.5 25.1 %reduce-scatter.9.cloned.1.call-done.part_ref = bf16[256,2048]{1,0:T(8,128)(2,1)} async-done(((bf16[1024,2048]{1,0:T(8,128)(2,1)}), bf16[256,2048]{1,0:T(8,128)(2,1)}) %reduce-scatter.9.cloned.1.call-update) | async-done | bytes 1048592 | tf_op jit(solution)/shard_map/reduce_scatter | solution.py:559
  626.6 5.3 shard_map.187
  632.2 4.2 fusion.29
  641.0 2.5 fusion.27
  644.0 41.1 %collective-permute-done.26 = bf16[512,2048]{1,0:T(8,128)(2,1)} collective-permute-done((bf16[512,2048]{1,0:T(8,128)(2,1)S(1)}, bf16[512,2048]{1,0:T(8,128)(2,1)}, u32[]{:S(2)}, u32[]{:S(2)}) %collective-permute-start.26) | collective-permute-done | bytes 2097184 | tf_op jit(solution)/shard_map/ppermute | solution.py:467
  686.0 27.3 %all-gather.11.cloned.1.call-done.left_ref = bf16[1024,2048]{1,0:T(8,128)(2,1)} async-done(((bf16[256,2048]{1,0:T(8,128)(2,1)}), bf16[1024,2048]{1,0:T(8,128)(2,1)}) %all-gather.11.cloned.1.call-update) | async-done | bytes 4194320 | tf_op jit(solution)/shard_map/all_gather | solution.py:556
  713.4 6.0 shard_map.188.g_ref
  719.3 15.9 %shard_map.189.refs_0_ = bf16[1024,1536]{1,0:T(8,128)(2,1)} custom-call(bf16[1024,512]{1,0:T(8,128)(2,1)} %get-tuple-element.76.q_ref, bf16[1024,512]{1,0:T(8,128)(2,1)} %get-tuple-element.77.k_ref, bf16[1024,512]{1,0:T(8,128)(2,1)} %get-tuple-element.78.v_ref, bf16[1024,512]{1,0:T(8,128)(2,1)} %shard_map.188.g_ref, f32[1024,512]{1,0:T(8,128)} %get-tuple-element.114.lse_ref, ...), custom_call_target="tpu_custom_call" | custom-call | flops 3221225472 | bytes 10485760 | tf_op jit(solution)/shard_map/pallas_call | solution.py:64
  735.2 12.4 %shard_map.190 = bf16[1024,2048]{1,0:T(8,128)(2,1)} custom-call(bf16[1024,1536]{1,0:T(8,128)(2,1)} %shard_map.189.refs_0_, bf16[1024,1536]{1,0:T(8,128)(2,1)} %pad_maximum_fusion.3.refs_0_.refs_1_, bf16[1024,1536]{1,0:T(8,128)(2,1)} %collective-permute-done.6.refs_1_.refs_2_), custom_call_target="tpu_custom_call" | custom-call | flops 6442450944 | bytes 13631488 | tf_op jit(solution)/shard_map/pallas_call | solution.py:64
  747.6 7.7 convolution_convert_fusion
  755.3 2.5 add_convert_fusion.4
  759.5 3.0 add_convert_fusion.6
  764.3 19.3 %collective-permute-done.39 = bf16[2048,256]{1,0:T(8,128)(2,1)S(1)} collective-permute-done((bf16[2048,256]{1,0:T(8,128)(2,1)S(1)}, bf16[2048,256]{1,0:T(8,128)(2,1)S(1)}, u32[]{:S(2)}, u32[]{:S(2)}) %collective-permute-start.39) | collective-permute-done | bytes 1048608 | tf_op jit(solution)/shard_map/ppermute | solution.py:467
  785.1 5.4 add_convert_fusion.3
  792.3 1.7 convert_add_fusion.2
  797.0 7.4 collective-permute-done.32
  806.2 2.2 add_convert_fusion.5
  810.0 14.4 %collective-permute-done.33 = bf16[256,512]{1,0:T(8,128)(2,1)S(1)} collective-permute-done((bf16[256,512]{1,0:T(8,128)(2,1)S(1)}, bf16[256,512]{1,0:T(8,128)(2,1)S(1)}, u32[]{:S(2)}, u32[]{:S(2)}) %collective-permute-start.33) | collective-permute-done | bytes 262176 | tf_op jit(solution)/shard_map/ppermute | solution.py:467
  829.1 5.4 collective-permute-done.38
  836.3 3.6 collective-permute-done.35
  841.7 4.1 collective-permute-done.31
  847.0 2.2 collective-permute-done.36
  850.1 4.9 shard_map.191
  (171 shorter events, 63.7 us)
Async XLA Ops:
  7.2 99.1 %all-gather.5.cloned.1.call-start = ((), (), s32[]{:S(2)}) async-start(), calls=%async_computation.4 | async-start | bytes 5242880 | tf_op jit(solution)/shard_map/all_gather | solution.py:556
  10.1 21.5 %collective-permute-start.3 = (bf16[256,1536]{1,0:T(8,128)(2,1)S(1)}, bf16[256,1536]{1,0:T(8,128)(2,1)}, u32[]{:S(2)}, u32[]{:S(2)}) collective-permute-start(bf16[256,1536]{1,0:T(8,128)(2,1)S(1)} %constant_dynamic-update-slice_fusion), channel_id=1, source_target_pairs={{0,8},{8,0},{1,9},{9,1},{2,10},{10,2},{3,11},{11,3},{4,12},{12,4},... | collective-permute-start | bytes 2359304 | tf_op jit(solution)/shard_map/ppermute | solution.py:467
  13.2 40.0 %copy-start.5 = (bf16[256,2048]{1,0:T(8,128)(2,1)S(1)}, bf16[256,2048]{1,0:T(8,128)(2,1)}, u32[]{:S(2)}) copy-start(bf16[256,2048]{1,0:T(8,128)(2,1)} %param.17) | copy-start | bytes 3145732
  17.2 204.8 %reduce-scatter.5.cloned.1.call-start = ((), (), s32[]{:S(2)}) async-start(), calls=%async_computation.5 | async-start | bytes 5242880 | tf_op jit(solution)/shard_map/reduce_scatter | solution.py:559
  17.2 35.9 %collective-permute-start.5 = (bf16[256,2048]{1,0:T(8,128)(2,1)}, bf16[256,2048]{1,0:T(8,128)(2,1)S(1)}, u32[]{:S(2)}, u32[]{:S(2)}) collective-permute-start(bf16[256,2048]{1,0:T(8,128)(2,1)} %param.17), channel_id=1, source_target_pairs={{0,8},{8,0},{1,9},{9,1},{2,10},{10,2},{3,11},{11,3},{4,12},{12,4},... | collective-permute-start | bytes 3145736 | tf_op jit(solution)/shard_map/ppermute | solution.py:467
  33.0 34.8 %collective-permute-start.4 = (bf16[512,1536]{1,0:T(8,128)(2,1)S(1)}, bf16[512,1536]{1,0:T(8,128)(2,1)S(1)}, u32[]{:S(2)}, u32[]{:S(2)}) collective-permute-start(bf16[512,1536]{1,0:T(8,128)(2,1)S(1)} %pad_maximum_fusion.9), channel_id=1, source_target_pairs={{0,16},{16,0},{1,17},{17,1},{2,18},{18,2},{3,19},{19,3},{4,20},{20... | collective-permute-start | bytes 4718600 | tf_op jit(solution)/shard_map/ppermute | solution.py:467
  53.5 19.9 %copy-start.8 = (bf16[512,256]{1,0:T(8,128)(2,1)S(1)}, bf16[512,256]{1,0:T(8,128)(2,1)}, u32[]{:S(2)}) copy-start(bf16[512,256]{1,0:T(8,128)(2,1)} %param.16) | copy-start | bytes 786436
  69.6 36.7 %collective-permute-start.6 = (bf16[1024,1536]{1,0:T(8,128)(2,1)}, bf16[1024,1536]{1,0:T(8,128)(2,1)}, u32[]{:S(2)}, u32[]{:S(2)}) collective-permute-start(bf16[1024,1536]{1,0:T(8,128)(2,1)} %pad_maximum_fusion.3.refs_0_.refs_1_), channel_id=1, source_target_pairs={{0,4},{4,0},{1,5},{5,1},{2,6},{6,2},{3,7},{7,3},{8,12},{12,8},{9,1... | collective-permute-start | bytes 9437192 | tf_op jit(solution)/shard_map/ppermute | solution.py:467
  70.3 3.7 collective-permute-start
  71.8 49.6 %collective-permute-start.7 = (bf16[256,2048]{1,0:T(8,128)(2,1)}, bf16[256,2048]{1,0:T(8,128)(2,1)}, u32[]{:S(2)}, u32[]{:S(2)}) collective-permute-start(bf16[256,2048]{1,0:T(8,128)(2,1)} %param.18), channel_id=1, source_target_pairs={{0,8},{8,0},{1,9},{9,1},{2,10},{10,2},{3,11},{11,3},{4,12},{12,4},... | collective-permute-start | bytes 3145736 | tf_op jit(solution)/shard_map/ppermute | solution.py:467
  73.3 32.2 %collective-permute-start.8 = (bf16[512,256]{1,0:T(8,128)(2,1)S(1)}, bf16[512,256]{1,0:T(8,128)(2,1)S(1)}, u32[]{:S(2)}, u32[]{:S(2)}) collective-permute-start(bf16[512,256]{1,0:T(8,128)(2,1)S(1)} %copy-done.8), channel_id=1, source_target_pairs={{0,8},{8,0},{1,9},{9,1},{2,10},{10,2},{3,11},{11,3},{4,12},{12,4},... | collective-permute-start | bytes 786440 | tf_op jit(solution)/shard_map/ppermute | solution.py:467
  74.0 29.0 %collective-permute-start.1 = (f32[8,128]{1,0:T(8,128)S(1)}, f32[8,128]{1,0:T(8,128)S(1)}, u32[]{:S(2)}, u32[]{:S(2)}) collective-permute-start(f32[8,128]{1,0:T(8,128)S(1)} %broadcast_add_fusion.1), channel_id=1, source_target_pairs={{0,8},{8,0},{1,9},{9,1},{2,10},{10,2},{3,11},{11,3},{4,12},{12,4},... | collective-permute-start | bytes 12296 | tf_op jit(solution)/shard_map/ppermute | solution.py:467
  103.0 1.3 collective-permute-start.2
  105.7 14.5 %collective-permute-start.9 = (bf16[512,512]{1,0:T(8,128)(2,1)S(1)}, bf16[512,512]{1,0:T(8,128)(2,1)}, u32[]{:S(2)}, u32[]{:S(2)}) collective-permute-start(bf16[512,512]{1,0:T(8,128)(2,1)S(1)} %pad_maximum_fusion.13), channel_id=1, source_target_pairs={{0,16},{16,0},{1,17},{17,1},{2,18},{18,2},{3,19},{19,3},{4,20},{20... | collective-permute-start | bytes 1572872 | tf_op jit(solution)/shard_map/ppermute | solution.py:467
  121.3 12.8 %copy-start.6 = (bf16[512,1024]{1,0:T(8,128)(2,1)}, bf16[512,1024]{1,0:T(8,128)(2,1)S(1)}, u32[]{:S(2)}) copy-start(bf16[512,1024]{1,0:T(8,128)(2,1)S(1)} %pad_maximum_fusion.10.refs_1_.refs_0_) | copy-start | bytes 3145732
  121.3 14.4 %collective-permute-start.10 = (bf16[512,1024]{1,0:T(8,128)(2,1)S(1)}, bf16[512,1024]{1,0:T(8,128)(2,1)S(1)}, u32[]{:S(2)}, u32[]{:S(2)}) collective-permute-start(bf16[512,1024]{1,0:T(8,128)(2,1)S(1)} %pad_maximum_fusion.10.refs_1_.refs_0_), channel_id=1, source_target_pairs={{0,4},{4,0},{1,5},{5,1},{2,6},{6,2},{3,7},{7,3},{8,12},{12,8},{9,1... | collective-permute-start | bytes 3145736 | tf_op jit(solution)/shard_map/ppermute | solution.py:467
  135.7 9.8 %copy-start.7 = (bf16[2048,256]{1,0:T(8,128)(2,1)S(1)}, bf16[2048,256]{1,0:T(8,128)(2,1)}, u32[]{:S(2)}) copy-start(bf16[2048,256]{1,0:T(8,128)(2,1)} %param.19) | copy-start | bytes 3145732
  144.8 163.3 %all-gather.7.cloned.1.call-start = ((), (), s32[]{:S(2)}) async-start(), calls=%async_computation.6 | async-start | bytes 5242880 | tf_op jit(solution)/shard_map/all_gather | solution.py:556
  144.8 71.8 %collective-permute-start.11 = (bf16[512,2048]{1,0:T(8,128)(2,1)S(1)}, bf16[512,2048]{1,0:T(8,128)(2,1)S(1)}, u32[]{:S(2)}, u32[]{:S(2)}) collective-permute-start(bf16[512,2048]{1,0:T(8,128)(2,1)S(1)} %pad_maximum_fusion.4), channel_id=1, source_target_pairs={{0,16},{16,0},{1,17},{17,1},{2,18},{18,2},{3,19},{19,3},{4,20},{20... | collective-permute-start | bytes 6291464 | tf_op jit(solution)/shard_map/ppermute | solution.py:467
  145.5 69.6 %collective-permute-start.12 = (bf16[2048,256]{1,0:T(8,128)(2,1)S(1)}, bf16[2048,256]{1,0:T(8,128)(2,1)S(1)}, u32[]{:S(2)}, u32[]{:S(2)}) collective-permute-start(bf16[2048,256]{1,0:T(8,128)(2,1)S(1)} %copy-done.7), channel_id=1, source_target_pairs={{0,16},{16,0},{1,17},{17,1},{2,18},{18,2},{3,19},{19,3},{4,20},{20... | collective-permute-start | bytes 3145736 | tf_op jit(solution)/shard_map/ppermute | solution.py:467
  216.6 47.4 %collective-permute-start.13 = (bf16[512,2048]{1,0:T(8,128)(2,1)}, bf16[512,2048]{1,0:T(8,128)(2,1)}, u32[]{:S(2)}, u32[]{:S(2)}) collective-permute-start(bf16[512,2048]{1,0:T(8,128)(2,1)} %pad_maximum_fusion.5), channel_id=1, source_target_pairs={{0,16},{16,0},{1,17},{17,1},{2,18},{18,2},{3,19},{19,3},{4,20},{20... | collective-permute-start | bytes 6291464 | tf_op jit(solution)/shard_map/ppermute | solution.py:467
  222.0 47.7 %collective-permute-start.14 = (bf16[2048,512]{1,0:T(8,128)(2,1)}, bf16[2048,512]{1,0:T(8,128)(2,1)}, u32[]{:S(2)}, u32[]{:S(2)}) collective-permute-start(bf16[2048,512]{1,0:T(8,128)(2,1)} %pad_maximum_fusion.6), channel_id=1, source_target_pairs={{0,8},{8,0},{1,9},{9,1},{2,10},{10,2},{3,11},{11,3},{4,12},{12,4},... | collective-permute-start | bytes 6291464 | tf_op jit(solution)/shard_map/ppermute | solution.py:467
  227.5 42.2 %copy-start.2 = (bf16[2048,512]{1,0:T(8,128)(2,1)S(1)}, bf16[2048,512]{1,0:T(8,128)(2,1)}, u32[]{:S(2)}) copy-start(bf16[2048,512]{1,0:T(8,128)(2,1)} %pad_maximum_fusion.6) | copy-start | bytes 6291460
  227.5 194.0 %reduce-scatter.7.cloned.1.call-start = ((), (), s32[]{:S(2)}) async-start(), calls=%async_computation.7 | async-start | bytes 5242880 | tf_op jit(solution)/shard_map/reduce_scatter | solution.py:559
  273.9 34.1 %collective-permute-start.15 = (bf16[1024,2048]{1,0:T(8,128)(2,1)}, bf16[1024,2048]{1,0:T(8,128)(2,1)}, u32[]{:S(2)}, u32[]{:S(2)}) collective-permute-start(bf16[1024,2048]{1,0:T(8,128)(2,1)} %pad_maximum_fusion.1.refs_2_.refs_4_), channel_id=1, source_target_pairs={{0,4},{4,0},{1,5},{5,1},{2,6},{6,2},{3,7},{7,3},{8,12},{12,8},{9,1... | collective-permute-start | bytes 12582920 | tf_op jit(solution)/shard_map/ppermute | solution.py:467
  274.0 34.1 %collective-permute-start.16 = (bf16[1024,2048]{1,0:T(8,128)(2,1)}, bf16[1024,2048]{1,0:T(8,128)(2,1)}, u32[]{:S(2)}, u32[]{:S(2)}) collective-permute-start(bf16[1024,2048]{1,0:T(8,128)(2,1)} %pad_maximum_fusion.refs_0_.refs_2_), channel_id=1, source_target_pairs={{0,4},{4,0},{1,5},{5,1},{2,6},{6,2},{3,7},{7,3},{8,12},{12,8},{9,1... | collective-permute-start | bytes 12582920 | tf_op jit(solution)/shard_map/ppermute | solution.py:467
  274.5 57.2 %collective-permute-start.17 = (bf16[2048,1024]{1,0:T(8,128)(2,1)}, bf16[2048,1024]{1,0:T(8,128)(2,1)}, u32[]{:S(2)}, u32[]{:S(2)}) collective-permute-start(bf16[2048,1024]{1,0:T(8,128)(2,1)} %pad_maximum_fusion.2.refs_1_.refs_0_), channel_id=1, source_target_pairs={{0,4},{4,0},{1,5},{5,1},{2,6},{6,2},{3,7},{7,3},{8,12},{12,8},{9,1... | collective-permute-start | bytes 12582920 | tf_op jit(solution)/shard_map/ppermute | solution.py:467
  346.0 161.9 %all-gather.9.cloned.1.call-start = ((), (), s32[]{:S(2)}) async-start(), calls=%async_computation.8 | async-start | bytes 5242880 | tf_op jit(solution)/shard_map/all_gather | solution.py:556
  426.4 200.2 %reduce-scatter.9.cloned.1.call-start = ((), (), s32[]{:S(2)}) async-start(), calls=%async_computation.9 | async-start | bytes 5242880 | tf_op jit(solution)/shard_map/reduce_scatter | solution.py:559
  428.4 3.7 collective-permute-start.18
  432.7 3.7 collective-permute-start.19
  437.1 1.2 collective-permute-start.20
  438.3 3.7 collective-permute-start.21
  442.0 6.6 collective-permute-start.22
  551.1 162.2 %all-gather.11.cloned.1.call-start = ((), (), s32[]{:S(2)}) async-start(), calls=%async_computation.10 | async-start | bytes 5242880 | tf_op jit(solution)/shard_map/all_gather | solution.py:556
  551.2 7.7 copy-start.12
  551.2 7.7 copy-start.18
  558.7 13.8 %copy-start.10 = (bf16[1024,2048]{1,0:T(8,128)(2,1)S(1)}, bf16[1024,2048]{1,0:T(8,128)(2,1)}, u32[]{:S(2)}) copy-start(bf16[1024,2048]{1,0:T(8,128)(2,1)} %all-gather.7.cloned.1.call-done.x_ref) | copy-start | bytes 12582916
  558.7 13.8 %copy-start.16 = (bf16[1024,2048]{1,0:T(8,128)(2,1)S(1)}, bf16[1024,2048]{1,0:T(8,128)(2,1)}, u32[]{:S(2)}) copy-start(bf16[1024,2048]{1,0:T(8,128)(2,1)} %get-tuple-element.105.refs_1_) | copy-start | bytes 12582916
  558.7 19.1 %collective-permute-start.23 = (bf16[1024,2048]{1,0:T(8,128)(2,1)S(1)}, bf16[1024,2048]{1,0:T(8,128)(2,1)S(1)}, u32[]{:S(2)}, u32[]{:S(2)}) collective-permute-start(bf16[1024,2048]{1,0:T(8,128)(2,1)S(1)} %convolution_convert_fusion.3), channel_id=1, source_target_pairs={{0,4},{4,0},{1,5},{5,1},{2,6},{6,2},{3,7},{7,3},{8,12},{12,8},{9,1... | collective-permute-start | bytes 12582920 | tf_op jit(solution)/shard_map/ppermute | solution.py:467
  572.2 14.2 %collective-permute-start.24 = (bf16[2048,1024]{1,0:T(8,128)(2,1)S(1)}, bf16[2048,1024]{1,0:T(8,128)(2,1)S(1)}, u32[]{:S(2)}, u32[]{:S(2)}) collective-permute-start(bf16[2048,1024]{1,0:T(8,128)(2,1)S(1)} %convolution_convert_fusion.2), channel_id=1, source_target_pairs={{0,4},{4,0},{1,5},{5,1},{2,6},{6,2},{3,7},{7,3},{8,12},{12,8},{9,1... | collective-permute-start | bytes 12582920 | tf_op jit(solution)/shard_map/ppermute | solution.py:467
  577.5 17.6 %collective-permute-start.25 = (bf16[1024,2048]{1,0:T(8,128)(2,1)S(1)}, bf16[1024,2048]{1,0:T(8,128)(2,1)S(1)}, u32[]{:S(2)}, u32[]{:S(2)}) collective-permute-start(bf16[1024,2048]{1,0:T(8,128)(2,1)S(1)} %convolution_convert_fusion.1), channel_id=1, source_target_pairs={{0,4},{4,0},{1,5},{5,1},{2,6},{6,2},{3,7},{7,3},{8,12},{12,8},{9,1... | collective-permute-start | bytes 12582920 | tf_op jit(solution)/shard_map/ppermute | solution.py:467
  586.4 8.6 copy-start.17
  631.9 218.1 %reduce-scatter.11.cloned.1.call-start = ((), (), s32[]{:S(2)}) async-start(), calls=%async_computation.11 | async-start | bytes 5242880 | tf_op jit(solution)/shard_map/reduce_scatter | solution.py:559
  632.2 5.7 copy-start.4
  636.4 48.6 %collective-permute-start.26 = (bf16[512,2048]{1,0:T(8,128)(2,1)S(1)}, bf16[512,2048]{1,0:T(8,128)(2,1)}, u32[]{:S(2)}, u32[]{:S(2)}) collective-permute-start(bf16[512,2048]{1,0:T(8,128)(2,1)S(1)} %get-tuple-element.132), channel_id=1, source_target_pairs={{0,16},{16,0},{1,17},{17,1},{2,18},{18,2},{3,19},{19,3},{4,20},{20... | collective-permute-start | bytes 6291464 | tf_op jit(solution)/shard_map/ppermute | solution.py:467
  638.7 47.3 %collective-permute-start.27 = (bf16[2048,512]{1,0:T(8,128)(2,1)S(1)}, bf16[2048,512]{1,0:T(8,128)(2,1)}, u32[]{:S(2)}, u32[]{:S(2)}) collective-permute-start(bf16[2048,512]{1,0:T(8,128)(2,1)S(1)} %pad_maximum_fusion.8), channel_id=1, source_target_pairs={{0,8},{8,0},{1,9},{9,1},{2,10},{10,2},{3,11},{11,3},{4,12},{12,4},... | collective-permute-start | bytes 6291464 | tf_op jit(solution)/shard_map/ppermute | solution.py:467
  643.5 91.7 %collective-permute-start.28 = (bf16[512,2048]{1,0:T(8,128)(2,1)}, bf16[512,2048]{1,0:T(8,128)(2,1)}, u32[]{:S(2)}, u32[]{:S(2)}) collective-permute-start(bf16[512,2048]{1,0:T(8,128)(2,1)} %get-tuple-element.128), channel_id=1, source_target_pairs={{0,16},{16,0},{1,17},{17,1},{2,18},{18,2},{3,19},{19,3},{4,20},{20... | collective-permute-start | bytes 6291464 | tf_op jit(solution)/shard_map/ppermute | solution.py:467
  755.3 29.7 %collective-permute-start.29 = (bf16[1024,1536]{1,0:T(8,128)(2,1)}, bf16[1024,1536]{1,0:T(8,128)(2,1)}, u32[]{:S(2)}, u32[]{:S(2)}) collective-permute-start(bf16[1024,1536]{1,0:T(8,128)(2,1)} %convolution_convert_fusion), channel_id=1, source_target_pairs={{0,4},{4,0},{1,5},{5,1},{2,6},{6,2},{3,7},{7,3},{8,12},{12,8},{9,1... | collective-permute-start | bytes 9437192 | tf_op jit(solution)/shard_map/ppermute | solution.py:467
  757.9 25.6 %collective-permute-start.39 = (bf16[2048,256]{1,0:T(8,128)(2,1)S(1)}, bf16[2048,256]{1,0:T(8,128)(2,1)S(1)}, u32[]{:S(2)}, u32[]{:S(2)}) collective-permute-start(bf16[2048,256]{1,0:T(8,128)(2,1)S(1)} %slice.151), channel_id=1, source_target_pairs={{0,16},{16,0},{1,17},{17,1},{2,18},{18,2},{3,19},{19,3},{4,20},{20... | collective-permute-start | bytes 3145736 | tf_op jit(solution)/shard_map/ppermute | solution.py:467
  759.5 25.6 %copy-start.15 = (bf16[1024,1536]{1,0:T(8,128)(2,1)S(1)}, bf16[1024,1536]{1,0:T(8,128)(2,1)}, u32[]{:S(2)}) copy-start(bf16[1024,1536]{1,0:T(8,128)(2,1)} %shard_map.189.refs_0_) | copy-start | bytes 9437188
  762.5 22.5 %copy-start.9 = (bf16[1024,2048]{1,0:T(8,128)(2,1)S(1)}, bf16[1024,2048]{1,0:T(8,128)(2,1)}, u32[]{:S(2)}) copy-start(bf16[1024,2048]{1,0:T(8,128)(2,1)} %all-gather.5.cloned.1.call-done.x_ref) | copy-start | bytes 12582916
  762.7 29.6 %collective-permute-start.37 = (bf16[256,2048]{1,0:T(8,128)(2,1)S(1)}, bf16[256,2048]{1,0:T(8,128)(2,1)S(1)}, u32[]{:S(2)}, u32[]{:S(2)}) collective-permute-start(bf16[256,2048]{1,0:T(8,128)(2,1)S(1)} %constant_dynamic-slice_fusion.1), channel_id=1, source_target_pairs={{0,8},{8,0},{1,9},{9,1},{2,10},{10,2},{3,11},{11,3},{4,12},{12,4},... | collective-permute-start | bytes 3145736 | tf_op jit(solution)/shard_map/ppermute | solution.py:467
  790.6 5.0 copy-start.11
  790.6 5.0 copy-start.14
  790.7 13.7 %collective-permute-start.32 = (bf16[512,512]{1,0:T(8,128)(2,1)S(1)}, bf16[512,512]{1,0:T(8,128)(2,1)S(1)}, u32[]{:S(2)}, u32[]{:S(2)}) collective-permute-start(bf16[512,512]{1,0:T(8,128)(2,1)S(1)} %pad_maximum_fusion.14), channel_id=1, source_target_pairs={{0,8},{8,0},{1,9},{9,1},{2,10},{10,2},{3,11},{11,3},{4,12},{12,4},... | collective-permute-start | bytes 1572872 | tf_op jit(solution)/shard_map/ppermute | solution.py:467
  794.1 12.1 %copy-start = (bf16[512,2048]{1,0:T(8,128)(2,1)S(1)}, bf16[512,2048]{1,0:T(8,128)(2,1)}, u32[]{:S(2)}) copy-start(bf16[512,2048]{1,0:T(8,128)(2,1)} %get-tuple-element.124) | copy-start | bytes 6291460
  794.1 31.2 %collective-permute-start.30 = (bf16[512,1024]{1,0:T(8,128)(2,1)S(1)}, bf16[512,1024]{1,0:T(8,128)(2,1)S(1)}, u32[]{:S(2)}, u32[]{:S(2)}) collective-permute-start(bf16[512,1024]{1,0:T(8,128)(2,1)S(1)} %slice.143), channel_id=1, source_target_pairs={{0,16},{16,0},{1,17},{17,1},{2,18},{18,2},{3,19},{19,3},{4,20},{20... | collective-permute-start | bytes 3145736 | tf_op jit(solution)/shard_map/ppermute | solution.py:467
  796.9 29.3 %collective-permute-start.34 = (bf16[512,1024]{1,0:T(8,128)(2,1)S(1)}, bf16[512,1024]{1,0:T(8,128)(2,1)S(1)}, u32[]{:S(2)}, u32[]{:S(2)}) collective-permute-start(bf16[512,1024]{1,0:T(8,128)(2,1)S(1)} %fusion.12), channel_id=1, source_target_pairs={{0,4},{4,0},{1,5},{5,1},{2,6},{6,2},{3,7},{7,3},{8,12},{12,8},{9,1... | collective-permute-start | bytes 3145736 | tf_op jit(solution)/shard_map/ppermute | solution.py:467
  804.6 19.8 %collective-permute-start.33 = (bf16[256,512]{1,0:T(8,128)(2,1)S(1)}, bf16[256,512]{1,0:T(8,128)(2,1)S(1)}, u32[]{:S(2)}, u32[]{:S(2)}) collective-permute-start(bf16[256,512]{1,0:T(8,128)(2,1)S(1)} %slice.149), channel_id=1, source_target_pairs={{0,16},{16,0},{1,17},{17,1},{2,18},{18,2},{3,19},{19,3},{4,20},{20... | collective-permute-start | bytes 786440 | tf_op jit(solution)/shard_map/ppermute | solution.py:467
  808.4 26.2 %collective-permute-start.38 = (bf16[256,2048]{1,0:T(8,128)(2,1)S(1)}, bf16[256,2048]{1,0:T(8,128)(2,1)S(1)}, u32[]{:S(2)}, u32[]{:S(2)}) collective-permute-start(bf16[256,2048]{1,0:T(8,128)(2,1)S(1)} %constant_dynamic-slice_fusion), channel_id=1, source_target_pairs={{0,8},{8,0},{1,9},{9,1},{2,10},{10,2},{3,11},{11,3},{4,12},{12,4},... | collective-permute-start | bytes 3145736 | tf_op jit(solution)/shard_map/ppermute | solution.py:467
  825.7 20.2 %collective-permute-start.31 = (bf16[256,1024]{1,0:T(8,128)(2,1)S(1)}, bf16[256,1024]{1,0:T(8,128)(2,1)S(1)}, u32[]{:S(2)}, u32[]{:S(2)}) collective-permute-start(bf16[256,1024]{1,0:T(8,128)(2,1)S(1)} %constant_dynamic-slice_fusion.7), channel_id=1, source_target_pairs={{0,8},{8,0},{1,9},{9,1},{2,10},{10,2},{3,11},{11,3},{4,12},{12,4},... | collective-permute-start | bytes 1572872 | tf_op jit(solution)/shard_map/ppermute | solution.py:467
  827.5 12.4 %collective-permute-start.35 = (bf16[512,512]{1,0:T(8,128)(2,1)S(1)}, bf16[512,512]{1,0:T(8,128)(2,1)S(1)}, u32[]{:S(2)}, u32[]{:S(2)}) collective-permute-start(bf16[512,512]{1,0:T(8,128)(2,1)S(1)} %slice.137), channel_id=1, source_target_pairs={{0,16},{16,0},{1,17},{17,1},{2,18},{18,2},{3,19},{19,3},{4,20},{20... | collective-permute-start | bytes 1572872 | tf_op jit(solution)/shard_map/ppermute | solution.py:467
  840.1 9.1 %collective-permute-start.36 = (bf16[512,256]{1,0:T(8,128)(2,1)S(1)}, bf16[512,256]{1,0:T(8,128)(2,1)S(1)}, u32[]{:S(2)}, u32[]{:S(2)}) collective-permute-start(bf16[512,256]{1,0:T(8,128)(2,1)S(1)} %constant_dynamic-slice_fusion.2), channel_id=1, source_target_pairs={{0,8},{8,0},{1,9},{9,1},{2,10},{10,2},{3,11},{11,3},{4,12},{12,4},... | collective-permute-start | bytes 786440 | tf_op jit(solution)/shard_map/ppermute | solution.py:467
  (3 other events, 7.7 us)
Sparse Core Ops, SparseCore 0:
  17.3 81.0 all-gather.4
  144.9 77.0 reduce-scatter.4
  227.6 80.3 all-gather.6
  346.2 75.2 reduce-scatter.6
  426.5 81.4 all-gather.8
  551.2 75.2 reduce-scatter.8
  632.1 81.2 all-gather.10
  755.5 75.4 reduce-scatter.10

commit v3 on v2

--- a/solution.py
+++ b/solution.py
@@ -94,10 +94,18 @@
     return total
 
 
-def heads_body(head_cols, count, x_ref, *refs):
+def in_order(from_ref, x_ref):
+    count = from_ref.shape[0]
+    width = x_ref.shape[1] // count
+    parts = [x_ref[:, block_at(from_ref, slot, width)] for slot in range(count)]
+    return jnp.concatenate(parts, axis=1).astype(F32)
+
+
+def heads_body(head_cols, count, from_ref, x_ref, *refs):
     weights = refs[:count]
-    c_ref, s_ref, q_ref, k_ref, v_ref = refs[count:]
-    rows = x_ref[...]
+    c_ref, s_ref, f_ref, q_ref, k_ref, v_ref = refs[count:]
+    rows = statistics(in_order(from_ref, x_ref))[0].astype(BF)
+    f_ref[...] = rows
     cosine, sine = c_ref[...], s_ref[...]
     for part, out_ref in enumerate((q_ref, k_ref, v_ref)):
         cols = slice(part * head_cols, (part + 1) * head_cols)
@@ -113,8 +121,8 @@
             out_ref[:, start : start + HS] = turned.astype(BF)
 
 
-def project_heads(features, weights, tables):
-    tokens, width = features.shape
+def project_heads(places, states, weights, tables):
+    tokens, width = states.shape
     head_cols = weights[0].shape[1] // 3
     rows = min(256, tokens)
     row_spec = pl.BlockSpec((rows, width), lambda i: (i, 0))
@@ -124,10 +132,43 @@
     return kernel_call(
         functools.partial(heads_body, head_cols, len(weights)),
         (tokens // rows,),
-        [row_spec, *map(whole, weights), table_spec, table_spec],
-        [out, out, out],
-        (features, *weights, *tables),
+        [pl.BlockSpec(memory_space=pltpu.SMEM), row_spec]
+        + [*map(whole, weights), table_spec, table_spec],
+        [(shape_of((tokens, width), BF), row_spec), out, out, out],
+        (places, states, *weights, *tables),
         2 * tokens * width * 3 * head_cols,
+    )
+
+
+def residual_body(count, from_ref, x_ref, o_ref, *refs):
+    weights = refs[:count]
+    r_ref, b_ref = refs[count:]
+    depth = o_ref.shape[2]
+    total = []
+    for w_ref in weights:
+        part = None
+        for z in range(o_ref.shape[0]):
+            got = dot(o_ref[z], w_ref[z * depth : (z + 1) * depth, :])
+            part = got if part is None else part + got
+        total.append(part)
+    total = in_order(from_ref, x_ref) + jnp.concatenate(total, axis=1)
+    r_ref[...] = total
+    b_ref[...] = statistics(total)[0].astype(BF)
+
+
+def residual_rows(places, states, attended, weights):
+    tokens, width = states.shape
+    rows = min(256, tokens)
+    row_spec = pl.BlockSpec((rows, width), lambda i: (i, 0))
+    line, _, cols = attended.shape
+    return kernel_call(
+        functools.partial(residual_body, len(weights)),
+        (tokens // rows,),
+        [pl.BlockSpec(memory_space=pltpu.SMEM), row_spec]
+        + [pl.BlockSpec((line, rows, cols), lambda i: (0, i, 0)), *map(whole, weights)],
+        [(shape_of((tokens, width), F32), row_spec), (shape_of((tokens, width), BF), row_spec)],
+        (places, states, attended, *weights),
+        2 * tokens * width * line * cols,
     )
 
 
@@ -353,21 +394,6 @@
 
 def block_at(from_ref, slot, width):
     return pl.ds(pl.multiple_of(from_ref[slot] * width, 128), width)
-
-
-def enter_body(from_ref, x_ref, rows_ref, normed_ref):
-    count = from_ref.shape[0]
-    width = x_ref.shape[1] // count
-    for slot in range(count):
-        here = slice(slot * width, (slot + 1) * width)
-        rows_ref[:, here] = x_ref[:, block_at(from_ref, slot, width)]
-    normed_ref[...] = statistics(rows_ref[...].astype(F32))[0].astype(BF)
-
-
-def add_norm_body(x_ref, part_ref, sum_ref, normed_ref):
-    total = x_ref[...].astype(F32) + part_ref[...].astype(F32)
-    sum_ref[...] = total
-    normed_ref[...] = statistics(total)[0].astype(BF)
 
 
 def loss_body(
@@ -401,7 +427,7 @@
 def leave_body(from_ref, x_ref, grad_ref, part_ref, out_ref):
     count = from_ref.shape[0]
     width = x_ref.shape[1] // count
-    total = grad_ref[...] + norm_back(x_ref[...].astype(F32), part_ref[...].astype(F32))
+    total = grad_ref[...] + norm_back(in_order(from_ref, x_ref), part_ref[...].astype(F32))
     for slot in range(count):
         out_ref[:, block_at(from_ref, slot, width)] = total[:, slot * width : (slot + 1) * width]
 
@@ -419,10 +445,16 @@
     def gather_y(self, value, axis, late=()):
         return value
 
+    def begin_y(self, value):
+        return (value,)
+
+    def end(self, pair, axis):
+        return pair[0]
+
     def gather_y_first(self, shard, axis):
         return shard
 
-    def gather_x_last(self, value, axis):
+    def gather_x_last(self, value, axis, late=()):
         return lax.all_gather(value, "dp", axis=axis, tiled=True)
 
     def gather_core(self, value):
@@ -488,11 +520,17 @@
     def gather_y(self, value, axis, late=()):
         return jnp.concatenate([value, after(self.swap(value, "y"), *late)], axis=axis)
 
+    def begin_y(self, value):
+        return (value, self.swap(value, "y"))
+
+    def end(self, pair, axis):
+        return jnp.concatenate(pair, axis=axis)
+
     def gather_y_first(self, shard, axis):
         return jnp.concatenate([shard, self.swap(shard, "y")], axis=axis)
 
-    def gather_x_last(self, value, axis):
-        other = self.swap(value, "x")
+    def gather_x_last(self, value, axis, late=()):
+        other = after(self.swap(value, "x"), *late)
         first = lax.axis_index("x") == 0
         parts = []
         for own, far in zip(halves(value, axis), halves(other, axis)):
@@ -566,36 +604,39 @@
     scale = (token_total / valid_total).reshape(1)
     left_length = (own_length - lax.axis_index(line) * local_rows).reshape(1)
     tables = rotary_tables(slot_count, HS)
-    rows_in, normed = rows_call(enter_body, (places,), (inputs[0],), (low, low))
-    features = line_in(normed)
+    states = line_in(inputs[0])
 
     heads_full = links.gather_x(jnp.concatenate([w_query, w_key, w_value], axis=1), 0)
     heads_full = links.gather_y(heads_full, 0)
     gate_full = links.gather_x(w_gate, 0)
     heads_full, gate_full = tied(heads_full, gate_full)
     heads_full = links.gather_core(heads_full)
-    out_full = links.gather_x(w_out, 1)
-    features, tables, scale = tied(features, tables, scale)
-    query, key, value = project_heads(features, heads_full, tables)
-    out_full = links.gather_core(links.gather_y(out_full, 1, (query,)))
-    up_full = links.gather_x(w_up, 0, (query,))
-    gate_full = links.gather_y(gate_full, 0)
-    down_full = links.gather_y_first(w_down, 1)
+    down_full = links.gather_x(after(w_down, gate_full), 1)
+    up_full = links.gather_y_first(w_up, 0)
+    states, tables, scale, down_full, up_full = tied(states, tables, scale, down_full, up_full)
+    out_full = lax.all_gather(after(w_out, states), line, axis=0, tiled=True)
+    features, query, key, value = project_heads(places, states, heads_full, tables)
+    gate_full = links.begin_y(gate_full)
+    up_full = links.gather_x_last(up_full, 0, (query,))
 
     attended, lse = attend(query, key, value)
-    attended, up_full = tied(attended, up_full)
-    attn_out = line_out(over_out([attended], [out_full], False))
-    attn_out, gate_full, down_full = tied(attn_out, gate_full, down_full)
+    attended, up_full, gate_full = tied(attended, up_full, gate_full)
+    out_full = links.gather_y_first(after(out_full, attended), 1)
+    out_full = links.gather_x_last(out_full, 1)
+    down_full = links.gather_y(down_full, 1)
+    gate_full = links.end(after(gate_full, attended), 0)
+    everyone = lax.all_gather(attended, line, axis=0)
+    everyone, out_full, down_full = tied(everyone, out_full, down_full)
+    out_full = links.gather_core(out_full)
     gate_full = links.gather_core(gate_full)
-    up_full = links.gather_y(up_full, 0)
-    down_full = links.gather_x_last(down_full, 1)
-    residual, normed_two = rows_call(add_norm_body, (), (rows_in, attn_out), (high, low))
-
-    features_two = line_in(normed_two)
-    up_full, down_full = tied(up_full, down_full)
     up_full = links.gather_core(up_full)
-    features_two, up_full = tied(features_two, up_full)
-    down_full = links.gather_core(down_full)
+    residual, features_two = residual_rows(places, states, everyone, out_full)
+    down_full = links.gather_core(after(down_full, features_two))
+    place = lax.axis_index(line)
+    residual = lax.dynamic_slice_in_dim(residual, place * local_rows, local_rows, axis=0)
+    out_rows = tuple(
+        lax.dynamic_slice_in_dim(part, place * head_cols, head_cols, axis=0) for part in out_full
+    )
     hidden, gate_pre, up_pre = gate_up(features_two, gate_full, up_full)
     mlp_out = line_out(over_out([hidden], [down_full], False))
     result, grad_result, grad_low, squares = rows_call(
@@ -628,7 +669,7 @@
     gate = links.send_x(links.fold(gate).astype(BF), 0)
     down = links.send_y(links.fold(down).astype(BF), 1)
 
-    mixed_grad = over_in(attn_grad_in, out_full, True)
+    mixed_grad = over_in(attn_grad_in, out_rows, True)
     heads_grad = attend_back(query, key, value, mixed_grad, lse, tables)
     heads_grad, up = tied(heads_grad, up)
     normed_grad = over_out([heads_grad], [heads_full], True)
@@ -642,7 +683,9 @@
     out = links.send_y(after(grad_out, heads), 1)
     grad_heads = links.fold(links.send_x(links.fold(heads).astype(BF), 0))
     tail = links.fold(links.send_y(links.fold(tail).astype(BF), 0))
-    input_grad = rows_call(leave_body, (places,), (rows_in, residual_grad, last), (high,))[0]
+    input_grad = rows_call(
+        leave_body, (places,), (inputs[0], residual_grad, last), (high,)
+    )[0]
     return (
         result[None],
         loss_value,

time: 872 us -> 825 us (0.946)
  waiting for transfers between devices: 511 us -> 453 us
  local copies, waits for them, and re-layouts: 16.2 us -> 27.2 us
    all_gather x4 -> x3, waiting for transfers between devices: 119 us -> 82.5 us  [line_in(): return lax.all_gather(values, line, axis=0, tiled=True)]
    ppermute x38, waiting for transfers between devices: 284 us -> 256 us  [swap(): return lax.ppermute(values, axis, SWAP)]
    pallas_call x15 -> x13, Pallas kernels: 169 us -> 172 us  [kernel_call(): pl.pallas_call(body, grid=grid, in_specs=ins, out_specs=[spec for _, spec...]
    reduce_scatter x4 -> x3, waiting for transfers between devices: 103 us -> 103 us  [line_out(): return lax.psum_scatter(partial, line, scatter_dimension=0, tiled=True)]
  transfers between devices with their start and end apart: 48 -> 48, of which waited for: 29 -> 28; matrix products, arithmetic and copies ran while one was open for 13% -> 15% of each run, Pallas kernels for 9% -> 11%
where the time goes in v3:
time: 825 us; the launch traced here: 817 us
  waiting for transfers between devices  453 us (55%)
  Pallas kernels  172 us (21%)
  matrix products  59.4 us (7%)
  other arithmetic  44.6 us (5%)
  starting transfers between devices  41.7 us (5%)
  local copies, waits for them, and re-layouts  27.2 us (3%)
  between operations  19 us (2%)
    ppermute x38, waiting for transfers between devices, swap(): return lax.ppermute(values, axis, SWAP)  256 us
    pallas_call x13, Pallas kernels, kernel_call(): pl.pallas_call(body, grid=grid, in_specs=ins, out_specs=[spec for _, spec...  172 us
    reduce_scatter x3, waiting for transfers between devices, line_out(): return lax.psum_scatter(partial, line, scatter_dimension=0, tiled=True)  103 us
    all_gather x3, waiting for transfers between devices, line_in(): return lax.all_gather(values, line, axis=0, tiled=True)  82.5 us
    dot_general x10, matrix products, dot_tn(): lax.dot_general(left, right, (((0,), (0,)), ((), ())), preferred_element_...  59.4 us
    ppermute x38, starting transfers between devices, swap(): return lax.ppermute(values, axis, SWAP)  36.3 us
  transfers between devices with their start and end apart: 48, of which 28 were waited for; matrix products, arithmetic and copies ran while one was open for 15% of the time, Pallas kernels for 11%

profile of v3, /device:TPU:0, one launch (start us, length us, event | category | flops | bytes accessed | tf_op | source)
XLA Modules:
  0.0 816.9 jit_solution(15105333029703565987)
XLA Ops:
  11.0 3.0 collective-permute-start.3
  14.0 18.4 %collective-permute-done.3 = bf16[256,1536]{1,0:T(8,128)(2,1)} collective-permute-done((bf16[256,1536]{1,0:T(8,128)(2,1)S(1)}, bf16[256,1536]{1,0:T(8,128)(2,1)}, u32[]{:S(2)}, u32[]{:S(2)}) %collective-permute-start.3) | collective-permute-done | bytes 786464 | tf_op jit(solution)/shard_map/ppermute | solution.py:499
  35.8 2.1 collective-permute-start.4
  38.7 2.0 collective-permute-start.7
  40.7 13.4 %collective-permute-done.5 = bf16[256,2048]{1,0:T(8,128)(2,1)} collective-permute-done((bf16[256,2048]{1,0:T(8,128)(2,1)}, bf16[256,2048]{1,0:T(8,128)(2,1)}, u32[]{:S(2)}, u32[]{:S(2)}) %collective-permute-start.5) | collective-permute-done | bytes 1048608 | tf_op jit(solution)/shard_map/ppermute | solution.py:499
  55.6 17.9 %collective-permute-done.4 = bf16[512,1536]{1,0:T(8,128)(2,1)} collective-permute-done((bf16[512,1536]{1,0:T(8,128)(2,1)}, bf16[512,1536]{1,0:T(8,128)(2,1)}, u32[]{:S(2)}, u32[]{:S(2)}) %collective-permute-start.4) | collective-permute-done | bytes 1572896 | tf_op jit(solution)/shard_map/ppermute | solution.py:499
  73.5 3.3 pad_maximum_fusion.3.refs_0_.refs_1_
  76.8 2.0 collective-permute-start.6
  80.9 15.9 %collective-permute-done.1 = f32[8,128]{1,0:T(8,128)S(1)} collective-permute-done((f32[8,128]{1,0:T(8,128)S(1)}, f32[8,128]{1,0:T(8,128)S(1)}, u32[]{:S(2)}, u32[]{:S(2)}) %collective-permute-start.1) | collective-permute-done | bytes 4128 | tf_op jit(solution)/shard_map/ppermute | solution.py:499
  104.9 13.9 %shard_map.177 = (bf16[1024,2048]{1,0:T(8,128)(2,1)}, bf16[1024,512]{1,0:T(8,128)(2,1)}, bf16[1024,512]{1,0:T(8,128)(2,1)}, bf16[1024,512]{1,0:T(8,128)(2,1)}) custom-call(s32[8]{0:T(128)S(1)} %fusion.22.from_ref, bf16[1024,2048]{1,0:T(8,128)(2,1)} %bitcast.25, bf16[1024,1536]{1,0:T(8,128)(2,1)} %pad_maximum_fusion.3.refs_0_.refs_1_, ...), custom_call_target="tpu_custom_call" | custom-call | flops 6442450944 | bytes 18874400 | tf_op jit(solution)/shard_map/pallas_call | solution.py:64
  118.8 11.0 %shard_map.178 = (bf16[1024,512]{1,0:T(8,128)(2,1)}, f32[1024,512]{1,0:T(8,128)}) custom-call(bf16[1024,512]{1,0:T(8,128)(2,1)} %get-tuple-element.79.q_ref, bf16[1024,512]{1,0:T(8,128)(2,1)} %get-tuple-element.80.k_ref, bf16[1024,512]{1,0:T(8,128)(2,1)} %get-tuple-element.81.v_ref), custom_call_target="tpu_custom_call" | custom-call | flops 1610612736 | bytes 6291456 | tf_op jit(solution)/shard_map/pallas_call | solution.py:64
  129.8 21.0 %collective-permute-done.9 = bf16[512,2048]{1,0:T(8,128)(2,1)} collective-permute-done((bf16[512,2048]{1,0:T(8,128)(2,1)}, bf16[512,2048]{1,0:T(8,128)(2,1)}, u32[]{:S(2)}, u32[]{:S(2)}) %collective-permute-start.9) | collective-permute-done | bytes 2097184 | tf_op jit(solution)/shard_map/ppermute | solution.py:499
  152.7 2.3 pad_maximum_fusion.refs_2_.refs_4_
  157.5 24.2 %collective-permute-done.11 = bf16[2048,256]{1,0:T(8,128)(2,1)S(1)} collective-permute-done((bf16[2048,256]{1,0:T(8,128)(2,1)}, bf16[2048,256]{1,0:T(8,128)(2,1)S(1)}, u32[]{:S(2)}, u32[]{:S(2)}) %collective-permute-start.11) | collective-permute-done | bytes 1048608 | tf_op jit(solution)/shard_map/ppermute | solution.py:499
  184.0 41.3 %collective-permute-done.13 = bf16[2048,512]{1,0:T(8,128)(2,1)S(1)} collective-permute-done((bf16[2048,512]{1,0:T(8,128)(2,1)}, bf16[2048,512]{1,0:T(8,128)(2,1)S(1)}, u32[]{:S(2)}, u32[]{:S(2)}) %collective-permute-start.13) | collective-permute-done | bytes 2097184 | tf_op jit(solution)/shard_map/ppermute | solution.py:499
  225.4 2.6 pad_maximum_fusion.2.refs_1_.refs_0_
  228.7 2.3 pad_maximum_fusion.1.refs_0_
  231.0 5.6 all-gather.16.cloned.1.call-done
  239.7 4.4 collective-permute-done.14.refs_1_
  244.1 16.8 %shard_map.179 = (f32[1024,2048]{1,0:T(8,128)}, bf16[1024,2048]{1,0:T(8,128)(2,1)}) custom-call(s32[8]{0:T(128)S(1)} %fusion.22.from_ref, bf16[1024,2048]{1,0:T(8,128)(2,1)} %bitcast.26, bf16[4,1024,512]{2,1,0:T(8,128)(2,1)} %bitcast.27, bf16[2048,1024]{1,0:T(8,128)(2,1)} %pad_maximum_fusion.1.refs_0_, bf16[2048,1024]{1,0:T(8,128)(2,1)} %collective-permute-done.14.refs_1_), custom_call_target="tpu_custom_call" | custom-call | flops 8589934592 | bytes 29360160 | tf_op jit(solution)/shard_map/pallas_call | solution.py:64
  261.2 23.5 %shard_map.180 = (bf16[1024,2048]{1,0:T(8,128)(2,1)}, bf16[1024,2048]{1,0:T(8,128)(2,1)}, bf16[1024,2048]{1,0:T(8,128)(2,1)}) custom-call(bf16[1024,2048]{1,0:T(8,128)(2,1)} %get-tuple-element.111.x_ref, bf16[1024,2048]{1,0:T(8,128)(2,1)} %copy-done.13, bf16[1024,2048]{1,0:T(8,128)(2,1)} %collective-permute-done.15.refs_1_.refs_3_, ...), custom_call_target="tpu_custom_call" | custom-call | flops 17179869184 | bytes 33554432 | tf_op jit(solution)/shard_map/pallas_call | solution.py:64
  284.7 14.4 %shard_map.181 = bf16[1024,2048]{1,0:T(8,128)(2,1)} custom-call(bf16[1024,2048]{1,0:T(8,128)(2,1)} %get-tuple-element.112.refs_0_, bf16[2048,1024]{1,0:T(8,128)(2,1)} %pad_maximum_fusion.2.refs_1_.refs_0_, bf16[2048,1024]{1,0:T(8,128)(2,1)} %collective-permute-done.17.refs_2_.refs_1_), custom_call_target="tpu_custom_call" | custom-call | flops 8589934592 | bytes 16777216 | tf_op jit(solution)/shard_map/pallas_call | solution.py:64
  299.2 3.1 constant_dynamic-slice_fusion.14.r_ref
  302.3 72.3 %reduce-scatter.4.cloned.1.call-done.part_ref = bf16[256,2048]{1,0:T(8,128)(2,1)} async-done(((bf16[1024,2048]{1,0:T(8,128)(2,1)}), bf16[256,2048]{1,0:T(8,128)(2,1)}) %reduce-scatter.4.cloned.1.call-update) | async-done | bytes 1048592 | tf_op jit(solution)/shard_map/reduce_scatter | solution.py:597
  374.6 4.9 shard_map.182
  383.5 2.1 collective-permute-done.18
  387.8 2.2 collective-permute-done.19
  393.3 2.2 collective-permute-done.21
  395.5 2.9 collective-permute-start.22
  399.1 2.7 collective-permute-done.22
  403.0 58.2 %all-gather.10.cloned.1.call-done.y_ref = bf16[1024,2048]{1,0:T(8,128)(2,1)} async-done(((bf16[256,2048]{1,0:T(8,128)(2,1)}), bf16[1024,2048]{1,0:T(8,128)(2,1)}) %all-gather.10.cloned.1.call-update) | async-done | bytes 4194320 | tf_op jit(solution)/shard_map/all_gather | solution.py:594
  461.1 18.2 %shard_map.183 = (bf16[1024,2048]{1,0:T(8,128)(2,1)}, bf16[1024,2048]{1,0:T(8,128)(2,1)}) custom-call(bf16[1024,2048]{1,0:T(8,128)(2,1)} %all-gather.10.cloned.1.call-done.y_ref, bf16[2048,1024]{1,0:T(8,128)(2,1)} %pad_maximum_fusion.2.refs_1_.refs_0_, bf16[2048,1024]{1,0:T(8,128)(2,1)} %collective-permute-done.17.refs_2_.refs_1_, ...), custom_call_target="tpu_custom_call" | custom-call | flops 8589934592 | bytes 29360128 | tf_op jit(solution)/shard_map/pallas_call | solution.py:64
  479.3 24.9 %shard_map.184 = bf16[1024,2048]{1,0:T(8,128)(2,1)} custom-call(bf16[1024,2048]{1,0:T(8,128)(2,1)} %get-tuple-element.109.refs_0_, bf16[1024,2048]{1,0:T(8,128)(2,1)} %get-tuple-element.110.refs_1_, bf16[1024,2048]{1,0:T(8,128)(2,1)} %copy-done.13, bf16[1024,2048]{1,0:T(8,128)(2,1)} %collective-permute-done.15.refs_1_.refs_3_, ...), custom_call_target="tpu_custom_call" | custom-call | flops 17179869184 | bytes 29360128 | tf_op jit(solution)/shard_map/pallas_call | solution.py:64
  504.3 7.5 convolution_convert_fusion.3
  512.0 5.1 convolution_convert_fusion.1
  517.6 7.0 convolution_convert_fusion.2
  524.8 9.6 %add_convert_fusion.2 = bf16[1024,2048]{1,0:T(8,128)(2,1)} fusion(bf16[1024,2048]{1,0:T(8,128)(2,1)S(1)} %collective-permute-done.23, bf16[1024,2048]{1,0:T(8,128)(2,1)} %get-tuple-element.109.refs_0_, bf16[1024,2048]{1,0:T(8,128)(2,1)} %get-tuple-element.111.x_ref), kind=kOutput, calls=%fused_computation.2 | convolution fusion | flops 4301258752 | bytes 14680064 | tf_op jit(solution)/shard_map/dot_general | solution.py:55
  534.4 8.0 add_convert_fusion
  542.4 6.5 add_convert_fusion.1
  548.9 30.8 %reduce-scatter.6.cloned.1.call-done.part_ref = bf16[256,2048]{1,0:T(8,128)(2,1)} async-done(((bf16[1024,2048]{1,0:T(8,128)(2,1)}), bf16[256,2048]{1,0:T(8,128)(2,1)}) %reduce-scatter.6.cloned.1.call-update) | async-done | bytes 1048592 | tf_op jit(solution)/shard_map/reduce_scatter | solution.py:597
  579.7 5.2 shard_map.185
  585.1 5.0 fusion.29
  596.0 2.6 fusion.27
  599.2 2.3 constant_dynamic-slice_fusion.9.refs_0_
  601.5 2.3 constant_dynamic-slice_fusion.8.refs_1_
  605.2 33.7 %collective-permute-done.26 = bf16[512,2048]{1,0:T(8,128)(2,1)} collective-permute-done((bf16[512,2048]{1,0:T(8,128)(2,1)}, bf16[512,2048]{1,0:T(8,128)(2,1)}, u32[]{:S(2)}, u32[]{:S(2)}) %collective-permute-start.26) | collective-permute-done | bytes 2097184 | tf_op jit(solution)/shard_map/ppermute | solution.py:499
  638.9 3.2 collective-permute-done.27
  642.0 24.4 %all-gather.12.cloned.1.call-done.left_ref = bf16[1024,2048]{1,0:T(8,128)(2,1)} async-done(((bf16[256,2048]{1,0:T(8,128)(2,1)}), bf16[1024,2048]{1,0:T(8,128)(2,1)}) %all-gather.12.cloned.1.call-update) | async-done | bytes 4194320 | tf_op jit(solution)/shard_map/all_gather | solution.py:594
  666.4 6.1 shard_map.186.g_ref
  672.5 15.9 %shard_map.187.refs_0_ = bf16[1024,1536]{1,0:T(8,128)(2,1)} custom-call(bf16[1024,512]{1,0:T(8,128)(2,1)} %get-tuple-element.79.q_ref, bf16[1024,512]{1,0:T(8,128)(2,1)} %get-tuple-element.80.k_ref, bf16[1024,512]{1,0:T(8,128)(2,1)} %get-tuple-element.81.v_ref, bf16[1024,512]{1,0:T(8,128)(2,1)} %shard_map.186.g_ref, f32[1024,512]{1,0:T(8,128)} %get-tuple-element.119.lse_ref, ...), custom_call_target="tpu_custom_call" | custom-call | flops 3221225472 | bytes 10485760 | tf_op jit(solution)/shard_map/pallas_call | solution.py:64
  688.4 12.5 %shard_map.188 = bf16[1024,2048]{1,0:T(8,128)(2,1)} custom-call(bf16[1024,1536]{1,0:T(8,128)(2,1)} %shard_map.187.refs_0_, bf16[1024,1536]{1,0:T(8,128)(2,1)} %pad_maximum_fusion.3.refs_0_.refs_1_, bf16[1024,1536]{1,0:T(8,128)(2,1)} %collective-permute-done.8.refs_1_.refs_2_), custom_call_target="tpu_custom_call" | custom-call | flops 6442450944 | bytes 13631488 | tf_op jit(solution)/shard_map/pallas_call | solution.py:64
  700.9 7.7 convolution_convert_fusion
  708.6 2.5 add_convert_fusion.4
  712.7 3.0 add_convert_fusion.6
  717.5 19.3 %collective-permute-done.39 = bf16[2048,256]{1,0:T(8,128)(2,1)S(1)} collective-permute-done((bf16[2048,256]{1,0:T(8,128)(2,1)S(1)}, bf16[2048,256]{1,0:T(8,128)(2,1)S(1)}, u32[]{:S(2)}, u32[]{:S(2)}) %collective-permute-start.39) | collective-permute-done | bytes 1048608 | tf_op jit(solution)/shard_map/ppermute | solution.py:499
  738.3 5.4 add_convert_fusion.3
  750.2 7.4 collective-permute-done.32
  759.4 2.4 add_convert_fusion.5
  763.5 14.1 %collective-permute-done.33 = bf16[256,512]{1,0:T(8,128)(2,1)S(1)} collective-permute-done((bf16[256,512]{1,0:T(8,128)(2,1)S(1)}, bf16[256,512]{1,0:T(8,128)(2,1)S(1)}, u32[]{:S(2)}, u32[]{:S(2)}) %collective-permute-start.33) | collective-permute-done | bytes 262176 | tf_op jit(solution)/shard_map/ppermute | solution.py:499
  782.4 5.7 collective-permute-done.38
  789.8 3.4 collective-permute-done.35
  795.0 4.4 collective-permute-done.31
  800.6 2.2 collective-permute-done.36
  803.6 4.9 shard_map.189
  (181 shorter events, 72.7 us)
Async XLA Ops:
  7.2 95.3 %all-gather.14.cloned.1.call-start = ((), (), s32[]{:S(2)}) async-start(), calls=%async_computation.9 | async-start | bytes 5242880 | tf_op jit(solution)/shard_map/all_gather | solution.py:594
  7.9 46.2 %copy-start.11 = (bf16[256,2048]{1,0:T(8,128)(2,1)S(1)}, bf16[256,2048]{1,0:T(8,128)(2,1)}, u32[]{:S(2)}) copy-start(bf16[256,2048]{1,0:T(8,128)(2,1)} %param.17) | copy-start | bytes 3145732
  7.9 147.4 %all-gather.8.cloned.1.call-start = ((), (), s32[]{:S(2)}) async-start(), calls=%async_computation.3 | async-start | bytes 1310720 | tf_op jit(solution)/shard_map/all_gather | solution.py:617
  11.0 21.5 %collective-permute-start.3 = (bf16[256,1536]{1,0:T(8,128)(2,1)S(1)}, bf16[256,1536]{1,0:T(8,128)(2,1)}, u32[]{:S(2)}, u32[]{:S(2)}) collective-permute-start(bf16[256,1536]{1,0:T(8,128)(2,1)S(1)} %constant_dynamic-update-slice_fusion), channel_id=1, source_target_pairs={{0,8},{8,0},{1,9},{9,1},{2,10},{10,2},{3,11},{11,3},{4,12},{12,4},... | collective-permute-start | bytes 2359304 | tf_op jit(solution)/shard_map/ppermute | solution.py:499
  14.0 40.1 %collective-permute-start.5 = (bf16[256,2048]{1,0:T(8,128)(2,1)}, bf16[256,2048]{1,0:T(8,128)(2,1)}, u32[]{:S(2)}, u32[]{:S(2)}) collective-permute-start(bf16[256,2048]{1,0:T(8,128)(2,1)} %param.17), channel_id=1, source_target_pairs={{0,8},{8,0},{1,9},{9,1},{2,10},{10,2},{3,11},{11,3},{4,12},{12,4},... | collective-permute-start | bytes 3145736 | tf_op jit(solution)/shard_map/ppermute | solution.py:499
  35.8 37.7 %collective-permute-start.4 = (bf16[512,1536]{1,0:T(8,128)(2,1)}, bf16[512,1536]{1,0:T(8,128)(2,1)}, u32[]{:S(2)}, u32[]{:S(2)}) collective-permute-start(bf16[512,1536]{1,0:T(8,128)(2,1)} %pad_maximum_fusion.10), channel_id=1, source_target_pairs={{0,16},{16,0},{1,17},{17,1},{2,18},{18,2},{3,19},{19,3},{4,20},{20... | collective-permute-start | bytes 4718600 | tf_op jit(solution)/shard_map/ppermute | solution.py:499
  38.6 40.2 %collective-permute-start = (f32[8,128]{1,0:T(8,128)S(1)}, f32[8,128]{1,0:T(8,128)S(1)}, u32[]{:S(2)}, u32[]{:S(2)}) collective-permute-start(f32[8,128]{1,0:T(8,128)S(1)} %broadcast_in_dim.14), channel_id=1, source_target_pairs={{0,16},{16,0},{1,17},{17,1},{2,18},{18,2},{3,19},{19,3},{4,20},{20... | collective-permute-start | bytes 12296 | tf_op jit(solution)/shard_map/ppermute | solution.py:499
  38.7 60.7 %collective-permute-start.7 = (bf16[256,2048]{1,0:T(8,128)(2,1)}, bf16[256,2048]{1,0:T(8,128)(2,1)S(1)}, u32[]{:S(2)}, u32[]{:S(2)}) collective-permute-start(bf16[256,2048]{1,0:T(8,128)(2,1)} %param.18), channel_id=1, source_target_pairs={{0,16},{16,0},{1,17},{17,1},{2,18},{18,2},{3,19},{19,3},{4,20},{20... | collective-permute-start | bytes 3145736 | tf_op jit(solution)/shard_map/ppermute | solution.py:499
  40.7 32.9 %copy-start.5 = (bf16[256,1536]{1,0:T(8,128)(2,1)S(1)}, bf16[256,1536]{1,0:T(8,128)(2,1)}, u32[]{:S(2)}) copy-start(bf16[256,1536]{1,0:T(8,128)(2,1)} %copy-done.4) | copy-start | bytes 2359300
  55.5 21.4 %copy-start.12 = (bf16[2048,256]{1,0:T(8,128)(2,1)S(1)}, bf16[2048,256]{1,0:T(8,128)(2,1)}, u32[]{:S(2)}) copy-start(bf16[2048,256]{1,0:T(8,128)(2,1)} %param.19) | copy-start | bytes 3145732
  55.6 43.7 %copy-start.15 = (bf16[256,2048]{1,0:T(8,128)(2,1)S(1)}, bf16[256,2048]{1,0:T(8,128)(2,1)}, u32[]{:S(2)}) copy-start(bf16[256,2048]{1,0:T(8,128)(2,1)} %param.18) | copy-start | bytes 3145732
  76.8 24.0 %collective-permute-start.6 = (bf16[2048,256]{1,0:T(8,128)(2,1)S(1)}, bf16[2048,256]{1,0:T(8,128)(2,1)S(1)}, u32[]{:S(2)}, u32[]{:S(2)}) collective-permute-start(bf16[2048,256]{1,0:T(8,128)(2,1)S(1)} %copy-done.12), channel_id=1, source_target_pairs={{0,8},{8,0},{1,9},{9,1},{2,10},{10,2},{3,11},{11,3},{4,12},{12,4},... | collective-permute-start | bytes 3145736 | tf_op jit(solution)/shard_map/ppermute | solution.py:499
  78.8 26.1 %collective-permute-start.8 = (bf16[1024,1536]{1,0:T(8,128)(2,1)}, bf16[1024,1536]{1,0:T(8,128)(2,1)}, u32[]{:S(2)}, u32[]{:S(2)}) collective-permute-start(bf16[1024,1536]{1,0:T(8,128)(2,1)} %pad_maximum_fusion.3.refs_0_.refs_1_), channel_id=1, source_target_pairs={{0,4},{4,0},{1,5},{5,1},{2,6},{6,2},{3,7},{7,3},{8,12},{12,8},{9,1... | collective-permute-start | bytes 9437192 | tf_op jit(solution)/shard_map/ppermute | solution.py:499
  78.8 18.0 %collective-permute-start.1 = (f32[8,128]{1,0:T(8,128)S(1)}, f32[8,128]{1,0:T(8,128)S(1)}, u32[]{:S(2)}, u32[]{:S(2)}) collective-permute-start(f32[8,128]{1,0:T(8,128)S(1)} %broadcast_add_fusion.1), channel_id=1, source_target_pairs={{0,8},{8,0},{1,9},{9,1},{2,10},{10,2},{3,11},{11,3},{4,12},{12,4},... | collective-permute-start | bytes 12296 | tf_op jit(solution)/shard_map/ppermute | solution.py:499
  96.8 1.3 collective-permute-start.2
  102.4 48.4 %collective-permute-start.9 = (bf16[512,2048]{1,0:T(8,128)(2,1)}, bf16[512,2048]{1,0:T(8,128)(2,1)}, u32[]{:S(2)}, u32[]{:S(2)}) collective-permute-start(bf16[512,2048]{1,0:T(8,128)(2,1)} %pad_maximum_fusion.6), channel_id=1, source_target_pairs={{0,8},{8,0},{1,9},{9,1},{2,10},{10,2},{3,11},{11,3},{4,12},{12,4},... | collective-permute-start | bytes 6291464 | tf_op jit(solution)/shard_map/ppermute | solution.py:499
  103.3 51.8 %collective-permute-start.10 = (bf16[512,2048]{1,0:T(8,128)(2,1)S(1)}, bf16[512,2048]{1,0:T(8,128)(2,1)}, u32[]{:S(2)}, u32[]{:S(2)}) collective-permute-start(bf16[512,2048]{1,0:T(8,128)(2,1)S(1)} %pad_maximum_fusion.4), channel_id=1, source_target_pairs={{0,16},{16,0},{1,17},{17,1},{2,18},{18,2},{3,19},{19,3},{4,20},{20... | collective-permute-start | bytes 6291464 | tf_op jit(solution)/shard_map/ppermute | solution.py:499
  104.8 131.8 %all-gather.16.cloned.1.call-start = ((), (), s32[]{:S(2)}) async-start(), calls=%async_computation.10 | async-start | bytes 5242880 | tf_op jit(solution)/shard_map/all_gather | solution.py:628
  118.8 32.0 %copy-start.3 = (bf16[512,2048]{1,0:T(8,128)(2,1)S(1)}, bf16[512,2048]{1,0:T(8,128)(2,1)}, u32[]{:S(2)}) copy-start(bf16[512,2048]{1,0:T(8,128)(2,1)} %pad_maximum_fusion.6) | copy-start | bytes 6291460
  155.1 219.6 %reduce-scatter.4.cloned.1.call-start = ((), (), s32[]{:S(2)}) async-start(), calls=%async_computation.4 | async-start | bytes 5242880 | tf_op jit(solution)/shard_map/reduce_scatter | solution.py:597
  155.4 70.0 %copy-start.2 = (bf16[2048,512]{1,0:T(8,128)(2,1)S(1)}, bf16[2048,512]{1,0:T(8,128)(2,1)}, u32[]{:S(2)}) copy-start(bf16[2048,512]{1,0:T(8,128)(2,1)} %pad_maximum_fusion.5) | copy-start | bytes 6291460
  155.4 26.3 %collective-permute-start.11 = (bf16[2048,256]{1,0:T(8,128)(2,1)}, bf16[2048,256]{1,0:T(8,128)(2,1)S(1)}, u32[]{:S(2)}, u32[]{:S(2)}) collective-permute-start(bf16[2048,256]{1,0:T(8,128)(2,1)} %all-gather.8.cloned.1.call-done), channel_id=1, source_target_pairs={{0,16},{16,0},{1,17},{17,1},{2,18},{18,2},{3,19},{19,3},{4,20},{20... | collective-permute-start | bytes 3145736 | tf_op jit(solution)/shard_map/ppermute | solution.py:499
  156.3 69.1 %collective-permute-start.13 = (bf16[2048,512]{1,0:T(8,128)(2,1)}, bf16[2048,512]{1,0:T(8,128)(2,1)S(1)}, u32[]{:S(2)}, u32[]{:S(2)}) collective-permute-start(bf16[2048,512]{1,0:T(8,128)(2,1)} %pad_maximum_fusion.5), channel_id=1, source_target_pairs={{0,16},{16,0},{1,17},{17,1},{2,18},{18,2},{3,19},{19,3},{4,20},{20... | collective-permute-start | bytes 6291464 | tf_op jit(solution)/shard_map/ppermute | solution.py:499
  183.1 45.3 %copy-start.10 = (bf16[2048,256]{1,0:T(8,128)(2,1)S(1)}, bf16[2048,256]{1,0:T(8,128)(2,1)}, u32[]{:S(2)}) copy-start(bf16[2048,256]{1,0:T(8,128)(2,1)} %all-gather.8.cloned.1.call-done) | copy-start | bytes 3145732
  183.1 45.3 %collective-permute-start.12 = (bf16[2048,512]{1,0:T(8,128)(2,1)S(1)}, bf16[2048,512]{1,0:T(8,128)(2,1)S(1)}, u32[]{:S(2)}, u32[]{:S(2)}) collective-permute-start(bf16[2048,512]{1,0:T(8,128)(2,1)S(1)} %pad_maximum_fusion.7), channel_id=1, source_target_pairs={{0,8},{8,0},{1,9},{9,1},{2,10},{10,2},{3,11},{11,3},{4,12},{12,4},... | collective-permute-start | bytes 6291464 | tf_op jit(solution)/shard_map/ppermute | solution.py:499
  236.6 7.5 collective-permute-start.14
  238.7 22.2 %copy-start.13 = (bf16[1024,2048]{1,0:T(8,128)(2,1)}, bf16[1024,2048]{1,0:T(8,128)(2,1)S(1)}, u32[]{:S(2)}) copy-start(bf16[1024,2048]{1,0:T(8,128)(2,1)S(1)} %constant_dynamic-update-slice_fusion.3.refs_0_.refs_2_) | copy-start | bytes 12582916
  238.8 22.2 %copy-start.7 = (bf16[2048,1024]{1,0:T(8,128)(2,1)S(1)}, bf16[2048,1024]{1,0:T(8,128)(2,1)}, u32[]{:S(2)}) copy-start(bf16[2048,1024]{1,0:T(8,128)(2,1)} %pad_maximum_fusion.2.refs_1_.refs_0_) | copy-start | bytes 12582916
  238.8 22.4 %collective-permute-start.15 = (bf16[1024,2048]{1,0:T(8,128)(2,1)S(1)}, bf16[1024,2048]{1,0:T(8,128)(2,1)}, u32[]{:S(2)}, u32[]{:S(2)}) collective-permute-start(bf16[1024,2048]{1,0:T(8,128)(2,1)S(1)} %constant_dynamic-update-slice_fusion.3.refs_0_.refs_2_), channel_id=1, source_target_pairs={{0,4},{4,0},{1,5},{5,1},{2,6},{6,2},{3,7},{7,3},{8,12},{12,8},{9,1... | collective-permute-start | bytes 12582920 | tf_op jit(solution)/shard_map/ppermute | solution.py:499
  239.6 21.6 %collective-permute-start.16 = (bf16[1024,2048]{1,0:T(8,128)(2,1)S(1)}, bf16[1024,2048]{1,0:T(8,128)(2,1)}, u32[]{:S(2)}, u32[]{:S(2)}) collective-permute-start(bf16[1024,2048]{1,0:T(8,128)(2,1)S(1)} %copy-done.6), channel_id=1, source_target_pairs={{0,4},{4,0},{1,5},{5,1},{2,6},{6,2},{3,7},{7,3},{8,12},{12,8},{9,1... | collective-permute-start | bytes 12582920 | tf_op jit(solution)/shard_map/ppermute | solution.py:499
  261.0 23.8 %collective-permute-start.17 = (bf16[2048,1024]{1,0:T(8,128)(2,1)S(1)}, bf16[2048,1024]{1,0:T(8,128)(2,1)}, u32[]{:S(2)}, u32[]{:S(2)}) collective-permute-start(bf16[2048,1024]{1,0:T(8,128)(2,1)S(1)} %copy-done.7), channel_id=1, source_target_pairs={{0,4},{4,0},{1,5},{5,1},{2,6},{6,2},{3,7},{7,3},{8,12},{12,8},{9,1... | collective-permute-start | bytes 12582920 | tf_op jit(solution)/shard_map/ppermute | solution.py:499
  299.1 162.0 %all-gather.10.cloned.1.call-start = ((), (), s32[]{:S(2)}) async-start(), calls=%async_computation.5 | async-start | bytes 5242880 | tf_op jit(solution)/shard_map/all_gather | solution.py:594
  379.5 200.2 %reduce-scatter.6.cloned.1.call-start = ((), (), s32[]{:S(2)}) async-start(), calls=%async_computation.6 | async-start | bytes 5242880 | tf_op jit(solution)/shard_map/reduce_scatter | solution.py:597
  382.0 3.7 collective-permute-start.18
  386.3 3.7 collective-permute-start.19
  390.6 1.2 collective-permute-start.20
  391.9 3.7 collective-permute-start.21
  395.5 6.3 collective-permute-start.22
  504.3 162.1 %all-gather.12.cloned.1.call-start = ((), (), s32[]{:S(2)}) async-start(), calls=%async_computation.7 | async-start | bytes 5242880 | tf_op jit(solution)/shard_map/all_gather | solution.py:594
  504.3 7.7 copy-start.19
  504.3 7.7 copy-start.21
  511.9 12.9 %collective-permute-start.23 = (bf16[1024,2048]{1,0:T(8,128)(2,1)S(1)}, bf16[1024,2048]{1,0:T(8,128)(2,1)S(1)}, u32[]{:S(2)}, u32[]{:S(2)}) collective-permute-start(bf16[1024,2048]{1,0:T(8,128)(2,1)S(1)} %convolution_convert_fusion.3), channel_id=1, source_target_pairs={{0,4},{4,0},{1,5},{5,1},{2,6},{6,2},{3,7},{7,3},{8,12},{12,8},{9,1... | collective-permute-start | bytes 12582920 | tf_op jit(solution)/shard_map/ppermute | solution.py:499
  517.1 17.3 %collective-permute-start.25 = (bf16[1024,2048]{1,0:T(8,128)(2,1)S(1)}, bf16[1024,2048]{1,0:T(8,128)(2,1)S(1)}, u32[]{:S(2)}, u32[]{:S(2)}) collective-permute-start(bf16[1024,2048]{1,0:T(8,128)(2,1)S(1)} %convolution_convert_fusion.1), channel_id=1, source_target_pairs={{0,4},{4,0},{1,5},{5,1},{2,6},{6,2},{3,7},{7,3},{8,12},{12,8},{9,1... | collective-permute-start | bytes 12582920 | tf_op jit(solution)/shard_map/ppermute | solution.py:499
  524.7 17.7 %collective-permute-start.24 = (bf16[2048,1024]{1,0:T(8,128)(2,1)S(1)}, bf16[2048,1024]{1,0:T(8,128)(2,1)S(1)}, u32[]{:S(2)}, u32[]{:S(2)}) collective-permute-start(bf16[2048,1024]{1,0:T(8,128)(2,1)S(1)} %convolution_convert_fusion.2), channel_id=1, source_target_pairs={{0,4},{4,0},{1,5},{5,1},{2,6},{6,2},{3,7},{7,3},{8,12},{12,8},{9,1... | collective-permute-start | bytes 12582920 | tf_op jit(solution)/shard_map/ppermute | solution.py:499
  534.4 8.1 copy-start.22
  585.0 218.6 %reduce-scatter.8.cloned.1.call-start = ((), (), s32[]{:S(2)}) async-start(), calls=%async_computation.8 | async-start | bytes 5242880 | tf_op jit(solution)/shard_map/reduce_scatter | solution.py:597
  585.0 6.5 copy-start.9
  590.0 48.8 %collective-permute-start.26 = (bf16[512,2048]{1,0:T(8,128)(2,1)}, bf16[512,2048]{1,0:T(8,128)(2,1)}, u32[]{:S(2)}, u32[]{:S(2)}) collective-permute-start(bf16[512,2048]{1,0:T(8,128)(2,1)} %get-tuple-element.138), channel_id=1, source_target_pairs={{0,16},{16,0},{1,17},{17,1},{2,18},{18,2},{3,19},{19,3},{4,20},{20... | collective-permute-start | bytes 6291464 | tf_op jit(solution)/shard_map/ppermute | solution.py:499
  594.6 47.4 %collective-permute-start.27 = (bf16[2048,512]{1,0:T(8,128)(2,1)}, bf16[2048,512]{1,0:T(8,128)(2,1)}, u32[]{:S(2)}, u32[]{:S(2)}) collective-permute-start(bf16[2048,512]{1,0:T(8,128)(2,1)} %pad_maximum_fusion.9), channel_id=1, source_target_pairs={{0,8},{8,0},{1,9},{9,1},{2,10},{10,2},{3,11},{11,3},{4,12},{12,4},... | collective-permute-start | bytes 6291464 | tf_op jit(solution)/shard_map/ppermute | solution.py:499
  598.7 89.8 %collective-permute-start.28 = (bf16[512,2048]{1,0:T(8,128)(2,1)}, bf16[512,2048]{1,0:T(8,128)(2,1)}, u32[]{:S(2)}, u32[]{:S(2)}) collective-permute-start(bf16[512,2048]{1,0:T(8,128)(2,1)} %get-tuple-element.134), channel_id=1, source_target_pairs={{0,16},{16,0},{1,17},{17,1},{2,18},{18,2},{3,19},{19,3},{4,20},{20... | collective-permute-start | bytes 6291464 | tf_op jit(solution)/shard_map/ppermute | solution.py:499
  708.6 29.7 %collective-permute-start.29 = (bf16[1024,1536]{1,0:T(8,128)(2,1)}, bf16[1024,1536]{1,0:T(8,128)(2,1)}, u32[]{:S(2)}, u32[]{:S(2)}) collective-permute-start(bf16[1024,1536]{1,0:T(8,128)(2,1)} %convolution_convert_fusion), channel_id=1, source_target_pairs={{0,4},{4,0},{1,5},{5,1},{2,6},{6,2},{3,7},{7,3},{8,12},{12,8},{9,1... | collective-permute-start | bytes 9437192 | tf_op jit(solution)/shard_map/ppermute | solution.py:499
  711.1 25.6 %collective-permute-start.39 = (bf16[2048,256]{1,0:T(8,128)(2,1)S(1)}, bf16[2048,256]{1,0:T(8,128)(2,1)S(1)}, u32[]{:S(2)}, u32[]{:S(2)}) collective-permute-start(bf16[2048,256]{1,0:T(8,128)(2,1)S(1)} %slice.159), channel_id=1, source_target_pairs={{0,16},{16,0},{1,17},{17,1},{2,18},{18,2},{3,19},{19,3},{4,20},{20... | collective-permute-start | bytes 3145736 | tf_op jit(solution)/shard_map/ppermute | solution.py:499
  712.7 25.6 %copy-start.20 = (bf16[1024,2048]{1,0:T(8,128)(2,1)S(1)}, bf16[1024,2048]{1,0:T(8,128)(2,1)}, u32[]{:S(2)}) copy-start(bf16[1024,2048]{1,0:T(8,128)(2,1)} %get-tuple-element.122) | copy-start | bytes 12582916
  715.8 22.5 %copy-start.18 = (bf16[1024,1536]{1,0:T(8,128)(2,1)S(1)}, bf16[1024,1536]{1,0:T(8,128)(2,1)}, u32[]{:S(2)}) copy-start(bf16[1024,1536]{1,0:T(8,128)(2,1)} %shard_map.187.refs_0_) | copy-start | bytes 9437188
  715.9 29.6 %collective-permute-start.37 = (bf16[256,2048]{1,0:T(8,128)(2,1)S(1)}, bf16[256,2048]{1,0:T(8,128)(2,1)S(1)}, u32[]{:S(2)}, u32[]{:S(2)}) collective-permute-start(bf16[256,2048]{1,0:T(8,128)(2,1)S(1)} %constant_dynamic-slice_fusion.1), channel_id=1, source_target_pairs={{0,8},{8,0},{1,9},{9,1},{2,10},{10,2},{3,11},{11,3},{4,12},{12,4},... | collective-permute-start | bytes 3145736 | tf_op jit(solution)/shard_map/ppermute | solution.py:499
  743.9 13.7 %collective-permute-start.32 = (bf16[512,512]{1,0:T(8,128)(2,1)S(1)}, bf16[512,512]{1,0:T(8,128)(2,1)S(1)}, u32[]{:S(2)}, u32[]{:S(2)}) collective-permute-start(bf16[512,512]{1,0:T(8,128)(2,1)S(1)} %pad_maximum_fusion.13), channel_id=1, source_target_pairs={{0,8},{8,0},{1,9},{9,1},{2,10},{10,2},{3,11},{11,3},{4,12},{12,4},... | collective-permute-start | bytes 1572872 | tf_op jit(solution)/shard_map/ppermute | solution.py:499
  747.3 12.1 %copy-start = (bf16[512,2048]{1,0:T(8,128)(2,1)S(1)}, bf16[512,2048]{1,0:T(8,128)(2,1)}, u32[]{:S(2)}) copy-start(bf16[512,2048]{1,0:T(8,128)(2,1)} %get-tuple-element.130) | copy-start | bytes 6291460
  747.4 31.2 %collective-permute-start.30 = (bf16[512,1024]{1,0:T(8,128)(2,1)S(1)}, bf16[512,1024]{1,0:T(8,128)(2,1)S(1)}, u32[]{:S(2)}, u32[]{:S(2)}) collective-permute-start(bf16[512,1024]{1,0:T(8,128)(2,1)S(1)} %slice.151), channel_id=1, source_target_pairs={{0,16},{16,0},{1,17},{17,1},{2,18},{18,2},{3,19},{19,3},{4,20},{20... | collective-permute-start | bytes 3145736 | tf_op jit(solution)/shard_map/ppermute | solution.py:499
  750.2 29.3 %collective-permute-start.34 = (bf16[512,1024]{1,0:T(8,128)(2,1)S(1)}, bf16[512,1024]{1,0:T(8,128)(2,1)S(1)}, u32[]{:S(2)}, u32[]{:S(2)}) collective-permute-start(bf16[512,1024]{1,0:T(8,128)(2,1)S(1)} %fusion.12), channel_id=1, source_target_pairs={{0,4},{4,0},{1,5},{5,1},{2,6},{6,2},{3,7},{7,3},{8,12},{12,8},{9,1... | collective-permute-start | bytes 3145736 | tf_op jit(solution)/shard_map/ppermute | solution.py:499
  757.8 19.8 %collective-permute-start.33 = (bf16[256,512]{1,0:T(8,128)(2,1)S(1)}, bf16[256,512]{1,0:T(8,128)(2,1)S(1)}, u32[]{:S(2)}, u32[]{:S(2)}) collective-permute-start(bf16[256,512]{1,0:T(8,128)(2,1)S(1)} %slice.157), channel_id=1, source_target_pairs={{0,16},{16,0},{1,17},{17,1},{2,18},{18,2},{3,19},{19,3},{4,20},{20... | collective-permute-start | bytes 786440 | tf_op jit(solution)/shard_map/ppermute | solution.py:499
  762.0 26.2 %collective-permute-start.38 = (bf16[256,2048]{1,0:T(8,128)(2,1)S(1)}, bf16[256,2048]{1,0:T(8,128)(2,1)S(1)}, u32[]{:S(2)}, u32[]{:S(2)}) collective-permute-start(bf16[256,2048]{1,0:T(8,128)(2,1)S(1)} %constant_dynamic-slice_fusion), channel_id=1, source_target_pairs={{0,8},{8,0},{1,9},{9,1},{2,10},{10,2},{3,11},{11,3},{4,12},{12,4},... | collective-permute-start | bytes 3145736 | tf_op jit(solution)/shard_map/ppermute | solution.py:499
  778.9 20.4 %collective-permute-start.31 = (bf16[256,1024]{1,0:T(8,128)(2,1)S(1)}, bf16[256,1024]{1,0:T(8,128)(2,1)S(1)}, u32[]{:S(2)}, u32[]{:S(2)}) collective-permute-start(bf16[256,1024]{1,0:T(8,128)(2,1)S(1)} %constant_dynamic-slice_fusion.7), channel_id=1, source_target_pairs={{0,8},{8,0},{1,9},{9,1},{2,10},{10,2},{3,11},{11,3},{4,12},{12,4},... | collective-permute-start | bytes 1572872 | tf_op jit(solution)/shard_map/ppermute | solution.py:499
  780.8 12.4 %collective-permute-start.35 = (bf16[512,512]{1,0:T(8,128)(2,1)S(1)}, bf16[512,512]{1,0:T(8,128)(2,1)S(1)}, u32[]{:S(2)}, u32[]{:S(2)}) collective-permute-start(bf16[512,512]{1,0:T(8,128)(2,1)S(1)} %slice.145), channel_id=1, source_target_pairs={{0,16},{16,0},{1,17},{17,1},{2,18},{18,2},{3,19},{19,3},{4,20},{20... | collective-permute-start | bytes 1572872 | tf_op jit(solution)/shard_map/ppermute | solution.py:499
  793.4 9.3 %collective-permute-start.36 = (bf16[512,256]{1,0:T(8,128)(2,1)S(1)}, bf16[512,256]{1,0:T(8,128)(2,1)S(1)}, u32[]{:S(2)}, u32[]{:S(2)}) collective-permute-start(bf16[512,256]{1,0:T(8,128)(2,1)S(1)} %constant_dynamic-slice_fusion.2), channel_id=1, source_target_pairs={{0,8},{8,0},{1,9},{9,1},{2,10},{10,2},{3,11},{11,3},{4,12},{12,4},... | collective-permute-start | bytes 786440 | tf_op jit(solution)/shard_map/ppermute | solution.py:499
  (7 other events, 27.9 us)
Sparse Core Ops, SparseCore 0:
  9.6 83.4 all-gather.13
  105.0 27.2 all-gather.7
  155.2 81.3 all-gather.15
  299.2 75.3 reduce-scatter.3
  379.6 81.4 all-gather.9
  504.4 75.2 reduce-scatter.5
  585.1 81.2 all-gather.11
  708.7 75.4 reduce-scatter.7

commit v4 on v3

--- a/solution.py
+++ b/solution.py
@@ -609,9 +609,9 @@
     heads_full = links.gather_x(jnp.concatenate([w_query, w_key, w_value], axis=1), 0)
     heads_full = links.gather_y(heads_full, 0)
     gate_full = links.gather_x(w_gate, 0)
+    down_full = links.gather_x(after(w_down, gate_full), 1)
     heads_full, gate_full = tied(heads_full, gate_full)
     heads_full = links.gather_core(heads_full)
-    down_full = links.gather_x(after(w_down, gate_full), 1)
     up_full = links.gather_y_first(w_up, 0)
     states, tables, scale, down_full, up_full = tied(states, tables, scale, down_full, up_full)
     out_full = lax.all_gather(after(w_out, states), line, axis=0, tiled=True)

time: 825 us -> 816 us (0.989)
  waiting for transfers between devices: 453 us -> 441 us
    ppermute x38, waiting for transfers between devices: 256 us -> 241 us  [swap(): return lax.ppermute(values, axis, SWAP)]
where the time goes in v4:
time: 816 us; the launch traced here: 808 us
  waiting for transfers between devices  441 us (54%)
  Pallas kernels  172 us (21%)
  matrix products  59.4 us (7%)
  other arithmetic  44.6 us (5%)
  starting transfers between devices  44.3 us (5%)
  local copies, waits for them, and re-layouts  27.2 us (3%)
  between operations  19 us (2%)
    ppermute x38, waiting for transfers between devices, swap(): return lax.ppermute(values, axis, SWAP)  241 us
    pallas_call x13, Pallas kernels, kernel_call(): pl.pallas_call(body, grid=grid, in_specs=ins, out_specs=[spec for _, spec...  172 us
    reduce_scatter x3, waiting for transfers between devices, line_out(): return lax.psum_scatter(partial, line, scatter_dimension=0, tiled=True)  103 us
    all_gather x3, waiting for transfers between devices, line_in(): return lax.all_gather(values, line, axis=0, tiled=True)  82.5 us
    dot_general x10, matrix products, dot_tn(): lax.dot_general(left, right, (((0,), (0,)), ((), ())), preferred_element_...  59.4 us
    ppermute x38, starting transfers between devices, swap(): return lax.ppermute(values, axis, SWAP)  38.9 us
  transfers between devices with their start and end apart: 48, of which 28 were waited for; matrix products, arithmetic and copies ran while one was open for 15% of the time, Pallas kernels for 11%

profile of v4, /device:TPU:0, one launch (start us, length us, event | category | flops | bytes accessed | tf_op | source)
XLA Modules:
  0.0 807.9 jit_solution(3635159001491261340)
XLA Ops:
  11.0 3.0 collective-permute-start.6
  14.0 18.4 %collective-permute-done.6 = bf16[256,1536]{1,0:T(8,128)(2,1)} collective-permute-done((bf16[256,1536]{1,0:T(8,128)(2,1)S(1)}, bf16[256,1536]{1,0:T(8,128)(2,1)}, u32[]{:S(2)}, u32[]{:S(2)}) %collective-permute-start.6) | collective-permute-done | bytes 786464 | tf_op jit(solution)/shard_map/ppermute | solution.py:499
  35.8 2.1 collective-permute-start.7
  38.7 2.0 collective-permute-start.5
  40.7 13.4 %collective-permute-done.3 = bf16[256,2048]{1,0:T(8,128)(2,1)} collective-permute-done((bf16[256,2048]{1,0:T(8,128)(2,1)}, bf16[256,2048]{1,0:T(8,128)(2,1)}, u32[]{:S(2)}, u32[]{:S(2)}) %collective-permute-start.3) | collective-permute-done | bytes 1048608 | tf_op jit(solution)/shard_map/ppermute | solution.py:499
  57.4 16.1 %collective-permute-done.7 = bf16[512,1536]{1,0:T(8,128)(2,1)} collective-permute-done((bf16[512,1536]{1,0:T(8,128)(2,1)}, bf16[512,1536]{1,0:T(8,128)(2,1)}, u32[]{:S(2)}, u32[]{:S(2)}) %collective-permute-start.7) | collective-permute-done | bytes 1572896 | tf_op jit(solution)/shard_map/ppermute | solution.py:499
  73.5 3.3 pad_maximum_fusion.3.refs_0_.refs_1_
  76.8 2.1 collective-permute-start.1
  83.7 9.7 %collective-permute-done.5 = bf16[256,2048]{1,0:T(8,128)(2,1)S(1)} collective-permute-done((bf16[256,2048]{1,0:T(8,128)(2,1)}, bf16[256,2048]{1,0:T(8,128)(2,1)S(1)}, u32[]{:S(2)}, u32[]{:S(2)}) %collective-permute-start.5) | collective-permute-done | bytes 1048608 | tf_op jit(solution)/shard_map/ppermute | solution.py:499
  99.5 13.9 %shard_map.177 = (bf16[1024,2048]{1,0:T(8,128)(2,1)}, bf16[1024,512]{1,0:T(8,128)(2,1)}, bf16[1024,512]{1,0:T(8,128)(2,1)}, bf16[1024,512]{1,0:T(8,128)(2,1)}) custom-call(s32[8]{0:T(128)S(1)} %fusion.22.from_ref, bf16[1024,2048]{1,0:T(8,128)(2,1)} %bitcast.25, bf16[1024,1536]{1,0:T(8,128)(2,1)} %pad_maximum_fusion.3.refs_0_.refs_1_, ...), custom_call_target="tpu_custom_call" | custom-call | flops 6442450944 | bytes 18874400 | tf_op jit(solution)/shard_map/pallas_call | solution.py:64
  113.3 11.0 %shard_map.178 = (bf16[1024,512]{1,0:T(8,128)(2,1)}, f32[1024,512]{1,0:T(8,128)}) custom-call(bf16[1024,512]{1,0:T(8,128)(2,1)} %get-tuple-element.78.q_ref, bf16[1024,512]{1,0:T(8,128)(2,1)} %get-tuple-element.79.k_ref, bf16[1024,512]{1,0:T(8,128)(2,1)} %get-tuple-element.80.v_ref), custom_call_target="tpu_custom_call" | custom-call | flops 1610612736 | bytes 6291456 | tf_op jit(solution)/shard_map/pallas_call | solution.py:64
  124.3 17.6 %collective-permute-done.9 = bf16[512,2048]{1,0:T(8,128)(2,1)} collective-permute-done((bf16[512,2048]{1,0:T(8,128)(2,1)}, bf16[512,2048]{1,0:T(8,128)(2,1)}, u32[]{:S(2)}, u32[]{:S(2)}) %collective-permute-start.9) | collective-permute-done | bytes 2097184 | tf_op jit(solution)/shard_map/ppermute | solution.py:499
  143.8 2.3 pad_maximum_fusion.refs_2_.refs_4_
  148.5 24.3 %collective-permute-done.11 = bf16[2048,256]{1,0:T(8,128)(2,1)S(1)} collective-permute-done((bf16[2048,256]{1,0:T(8,128)(2,1)}, bf16[2048,256]{1,0:T(8,128)(2,1)S(1)}, u32[]{:S(2)}, u32[]{:S(2)}) %collective-permute-start.11) | collective-permute-done | bytes 1048608 | tf_op jit(solution)/shard_map/ppermute | solution.py:499
  175.1 38.2 %collective-permute-done.13 = bf16[2048,512]{1,0:T(8,128)(2,1)S(1)} collective-permute-done((bf16[2048,512]{1,0:T(8,128)(2,1)}, bf16[2048,512]{1,0:T(8,128)(2,1)S(1)}, u32[]{:S(2)}, u32[]{:S(2)}) %collective-permute-start.13) | collective-permute-done | bytes 2097184 | tf_op jit(solution)/shard_map/ppermute | solution.py:499
  213.4 2.6 pad_maximum_fusion.2.refs_1_.refs_0_
  216.2 2.3 pad_maximum_fusion.1.refs_0_
  218.6 9.0 %all-gather.16.cloned.1.call-done = bf16[4096,512]{1,0:T(8,128)(2,1)} async-done(((bf16[1024,512]{1,0:T(8,128)(2,1)}), bf16[4096,512]{1,0:T(8,128)(2,1)}) %all-gather.16.cloned.1.call-update) | async-done | bytes 4194320 | tf_op jit(solution)/shard_map/all_gather | solution.py:628
  230.6 4.4 collective-permute-done.14.refs_1_
  235.1 16.8 %shard_map.179 = (f32[1024,2048]{1,0:T(8,128)}, bf16[1024,2048]{1,0:T(8,128)(2,1)}) custom-call(s32[8]{0:T(128)S(1)} %fusion.22.from_ref, bf16[1024,2048]{1,0:T(8,128)(2,1)} %bitcast.26, bf16[4,1024,512]{2,1,0:T(8,128)(2,1)} %bitcast.27, bf16[2048,1024]{1,0:T(8,128)(2,1)} %pad_maximum_fusion.1.refs_0_, bf16[2048,1024]{1,0:T(8,128)(2,1)} %collective-permute-done.14.refs_1_), custom_call_target="tpu_custom_call" | custom-call | flops 8589934592 | bytes 29360160 | tf_op jit(solution)/shard_map/pallas_call | solution.py:64
  252.1 23.5 %shard_map.180 = (bf16[1024,2048]{1,0:T(8,128)(2,1)}, bf16[1024,2048]{1,0:T(8,128)(2,1)}, bf16[1024,2048]{1,0:T(8,128)(2,1)}) custom-call(bf16[1024,2048]{1,0:T(8,128)(2,1)} %get-tuple-element.111.x_ref, bf16[1024,2048]{1,0:T(8,128)(2,1)} %copy-done.13, bf16[1024,2048]{1,0:T(8,128)(2,1)} %collective-permute-done.15.refs_1_.refs_3_, ...), custom_call_target="tpu_custom_call" | custom-call | flops 17179869184 | bytes 33554432 | tf_op jit(solution)/shard_map/pallas_call | solution.py:64
  275.7 14.4 %shard_map.181 = bf16[1024,2048]{1,0:T(8,128)(2,1)} custom-call(bf16[1024,2048]{1,0:T(8,128)(2,1)} %get-tuple-element.112.refs_0_, bf16[2048,1024]{1,0:T(8,128)(2,1)} %pad_maximum_fusion.2.refs_1_.refs_0_, bf16[2048,1024]{1,0:T(8,128)(2,1)} %collective-permute-done.17.refs_2_.refs_1_), custom_call_target="tpu_custom_call" | custom-call | flops 8589934592 | bytes 16777216 | tf_op jit(solution)/shard_map/pallas_call | solution.py:64
  290.1 3.1 constant_dynamic-slice_fusion.14.r_ref
  293.3 72.3 %reduce-scatter.4.cloned.1.call-done.part_ref = bf16[256,2048]{1,0:T(8,128)(2,1)} async-done(((bf16[1024,2048]{1,0:T(8,128)(2,1)}), bf16[256,2048]{1,0:T(8,128)(2,1)}) %reduce-scatter.4.cloned.1.call-update) | async-done | bytes 1048592 | tf_op jit(solution)/shard_map/reduce_scatter | solution.py:597
  365.6 4.9 shard_map.182
  374.4 2.1 collective-permute-done.18
  378.8 2.2 collective-permute-done.19
  384.3 2.2 collective-permute-done.21
  386.5 2.9 collective-permute-start.22
  390.1 2.7 collective-permute-done.22
  393.9 58.2 %all-gather.10.cloned.1.call-done.y_ref = bf16[1024,2048]{1,0:T(8,128)(2,1)} async-done(((bf16[256,2048]{1,0:T(8,128)(2,1)}), bf16[1024,2048]{1,0:T(8,128)(2,1)}) %all-gather.10.cloned.1.call-update) | async-done | bytes 4194320 | tf_op jit(solution)/shard_map/all_gather | solution.py:594
  452.1 18.2 %shard_map.183 = (bf16[1024,2048]{1,0:T(8,128)(2,1)}, bf16[1024,2048]{1,0:T(8,128)(2,1)}) custom-call(bf16[1024,2048]{1,0:T(8,128)(2,1)} %all-gather.10.cloned.1.call-done.y_ref, bf16[2048,1024]{1,0:T(8,128)(2,1)} %pad_maximum_fusion.2.refs_1_.refs_0_, bf16[2048,1024]{1,0:T(8,128)(2,1)} %collective-permute-done.17.refs_2_.refs_1_, ...), custom_call_target="tpu_custom_call" | custom-call | flops 8589934592 | bytes 29360128 | tf_op jit(solution)/shard_map/pallas_call | solution.py:64
  470.3 24.9 %shard_map.184 = bf16[1024,2048]{1,0:T(8,128)(2,1)} custom-call(bf16[1024,2048]{1,0:T(8,128)(2,1)} %get-tuple-element.109.refs_0_, bf16[1024,2048]{1,0:T(8,128)(2,1)} %get-tuple-element.110.refs_1_, bf16[1024,2048]{1,0:T(8,128)(2,1)} %copy-done.13, bf16[1024,2048]{1,0:T(8,128)(2,1)} %collective-permute-done.15.refs_1_.refs_3_, ...), custom_call_target="tpu_custom_call" | custom-call | flops 17179869184 | bytes 29360128 | tf_op jit(solution)/shard_map/pallas_call | solution.py:64
  495.3 7.5 convolution_convert_fusion.3
  502.9 5.1 convolution_convert_fusion.1
  508.6 7.1 convolution_convert_fusion.2
  515.8 9.6 %add_convert_fusion.2 = bf16[1024,2048]{1,0:T(8,128)(2,1)} fusion(bf16[1024,2048]{1,0:T(8,128)(2,1)S(1)} %collective-permute-done.23, bf16[1024,2048]{1,0:T(8,128)(2,1)} %get-tuple-element.109.refs_0_, bf16[1024,2048]{1,0:T(8,128)(2,1)} %get-tuple-element.111.x_ref), kind=kOutput, calls=%fused_computation.2 | convolution fusion | flops 4301258752 | bytes 14680064 | tf_op jit(solution)/shard_map/dot_general | solution.py:55
  525.4 8.0 add_convert_fusion
  533.4 6.5 add_convert_fusion.1
  539.9 30.8 %reduce-scatter.6.cloned.1.call-done.part_ref = bf16[256,2048]{1,0:T(8,128)(2,1)} async-done(((bf16[1024,2048]{1,0:T(8,128)(2,1)}), bf16[256,2048]{1,0:T(8,128)(2,1)}) %reduce-scatter.6.cloned.1.call-update) | async-done | bytes 1048592 | tf_op jit(solution)/shard_map/reduce_scatter | solution.py:597
  570.7 5.2 shard_map.185
  576.0 5.0 fusion.29
  587.0 2.6 fusion.27
  590.2 2.3 constant_dynamic-slice_fusion.9.refs_0_
  592.5 2.3 constant_dynamic-slice_fusion.8.refs_1_
  596.1 33.7 %collective-permute-done.26 = bf16[512,2048]{1,0:T(8,128)(2,1)} collective-permute-done((bf16[512,2048]{1,0:T(8,128)(2,1)}, bf16[512,2048]{1,0:T(8,128)(2,1)}, u32[]{:S(2)}, u32[]{:S(2)}) %collective-permute-start.26) | collective-permute-done | bytes 2097184 | tf_op jit(solution)/shard_map/ppermute | solution.py:499
  629.8 3.2 collective-permute-done.27
  633.0 24.4 %all-gather.12.cloned.1.call-done.left_ref = bf16[1024,2048]{1,0:T(8,128)(2,1)} async-done(((bf16[256,2048]{1,0:T(8,128)(2,1)}), bf16[1024,2048]{1,0:T(8,128)(2,1)}) %all-gather.12.cloned.1.call-update) | async-done | bytes 4194320 | tf_op jit(solution)/shard_map/all_gather | solution.py:594
  657.4 6.1 shard_map.186.g_ref
  663.5 15.9 %shard_map.187.refs_0_ = bf16[1024,1536]{1,0:T(8,128)(2,1)} custom-call(bf16[1024,512]{1,0:T(8,128)(2,1)} %get-tuple-element.78.q_ref, bf16[1024,512]{1,0:T(8,128)(2,1)} %get-tuple-element.79.k_ref, bf16[1024,512]{1,0:T(8,128)(2,1)} %get-tuple-element.80.v_ref, bf16[1024,512]{1,0:T(8,128)(2,1)} %shard_map.186.g_ref, f32[1024,512]{1,0:T(8,128)} %get-tuple-element.119.lse_ref, ...), custom_call_target="tpu_custom_call" | custom-call | flops 3221225472 | bytes 10485760 | tf_op jit(solution)/shard_map/pallas_call | solution.py:64
  679.4 12.5 %shard_map.188 = bf16[1024,2048]{1,0:T(8,128)(2,1)} custom-call(bf16[1024,1536]{1,0:T(8,128)(2,1)} %shard_map.187.refs_0_, bf16[1024,1536]{1,0:T(8,128)(2,1)} %pad_maximum_fusion.3.refs_0_.refs_1_, bf16[1024,1536]{1,0:T(8,128)(2,1)} %collective-permute-done.8.refs_1_.refs_2_), custom_call_target="tpu_custom_call" | custom-call | flops 6442450944 | bytes 13631488 | tf_op jit(solution)/shard_map/pallas_call | solution.py:64
  691.8 7.7 convolution_convert_fusion
  699.6 2.5 add_convert_fusion.4
  703.7 3.0 add_convert_fusion.6
  708.5 19.3 %collective-permute-done.39 = bf16[2048,256]{1,0:T(8,128)(2,1)S(1)} collective-permute-done((bf16[2048,256]{1,0:T(8,128)(2,1)S(1)}, bf16[2048,256]{1,0:T(8,128)(2,1)S(1)}, u32[]{:S(2)}, u32[]{:S(2)}) %collective-permute-start.39) | collective-permute-done | bytes 1048608 | tf_op jit(solution)/shard_map/ppermute | solution.py:499
  729.3 5.4 add_convert_fusion.3
  741.2 7.4 collective-permute-done.32
  750.4 2.4 add_convert_fusion.5
  754.5 14.1 %collective-permute-done.33 = bf16[256,512]{1,0:T(8,128)(2,1)S(1)} collective-permute-done((bf16[256,512]{1,0:T(8,128)(2,1)S(1)}, bf16[256,512]{1,0:T(8,128)(2,1)S(1)}, u32[]{:S(2)}, u32[]{:S(2)}) %collective-permute-start.33) | collective-permute-done | bytes 262176 | tf_op jit(solution)/shard_map/ppermute | solution.py:499
  773.4 5.7 collective-permute-done.38
  780.8 3.4 collective-permute-done.35
  785.9 4.4 collective-permute-done.31
  791.5 2.2 collective-permute-done.36
  794.5 4.9 shard_map.189
  (181 shorter events, 74.8 us)
Async XLA Ops:
  7.2 89.3 %all-gather.14.cloned.1.call-start = ((), (), s32[]{:S(2)}) async-start(), calls=%async_computation.9 | async-start | bytes 5242880 | tf_op jit(solution)/shard_map/all_gather | solution.py:594
  7.9 46.2 %copy-start.11 = (bf16[256,2048]{1,0:T(8,128)(2,1)S(1)}, bf16[256,2048]{1,0:T(8,128)(2,1)}, u32[]{:S(2)}) copy-start(bf16[256,2048]{1,0:T(8,128)(2,1)} %param.17) | copy-start | bytes 3145732
  7.9 138.5 %all-gather.8.cloned.1.call-start = ((), (), s32[]{:S(2)}) async-start(), calls=%async_computation.3 | async-start | bytes 1310720 | tf_op jit(solution)/shard_map/all_gather | solution.py:617
  11.0 21.5 %collective-permute-start.6 = (bf16[256,1536]{1,0:T(8,128)(2,1)S(1)}, bf16[256,1536]{1,0:T(8,128)(2,1)}, u32[]{:S(2)}, u32[]{:S(2)}) collective-permute-start(bf16[256,1536]{1,0:T(8,128)(2,1)S(1)} %constant_dynamic-update-slice_fusion), channel_id=1, source_target_pairs={{0,8},{8,0},{1,9},{9,1},{2,10},{10,2},{3,11},{11,3},{4,12},{12,4},... | collective-permute-start | bytes 2359304 | tf_op jit(solution)/shard_map/ppermute | solution.py:499
  14.0 40.1 %collective-permute-start.3 = (bf16[256,2048]{1,0:T(8,128)(2,1)}, bf16[256,2048]{1,0:T(8,128)(2,1)}, u32[]{:S(2)}, u32[]{:S(2)}) collective-permute-start(bf16[256,2048]{1,0:T(8,128)(2,1)} %param.17), channel_id=1, source_target_pairs={{0,8},{8,0},{1,9},{9,1},{2,10},{10,2},{3,11},{11,3},{4,12},{12,4},... | collective-permute-start | bytes 3145736 | tf_op jit(solution)/shard_map/ppermute | solution.py:499
  35.8 37.7 %collective-permute-start.7 = (bf16[512,1536]{1,0:T(8,128)(2,1)}, bf16[512,1536]{1,0:T(8,128)(2,1)}, u32[]{:S(2)}, u32[]{:S(2)}) collective-permute-start(bf16[512,1536]{1,0:T(8,128)(2,1)} %pad_maximum_fusion.10), channel_id=1, source_target_pairs={{0,16},{16,0},{1,17},{17,1},{2,18},{18,2},{3,19},{19,3},{4,20},{20... | collective-permute-start | bytes 4718600 | tf_op jit(solution)/shard_map/ppermute | solution.py:499
  38.6 38.2 %collective-permute-start = (f32[8,128]{1,0:T(8,128)S(1)}, f32[8,128]{1,0:T(8,128)S(1)}, u32[]{:S(2)}, u32[]{:S(2)}) collective-permute-start(f32[8,128]{1,0:T(8,128)S(1)} %broadcast_in_dim.14), channel_id=1, source_target_pairs={{0,16},{16,0},{1,17},{17,1},{2,18},{18,2},{3,19},{19,3},{4,20},{20... | collective-permute-start | bytes 12296 | tf_op jit(solution)/shard_map/ppermute | solution.py:499
  38.7 54.7 %collective-permute-start.5 = (bf16[256,2048]{1,0:T(8,128)(2,1)}, bf16[256,2048]{1,0:T(8,128)(2,1)S(1)}, u32[]{:S(2)}, u32[]{:S(2)}) collective-permute-start(bf16[256,2048]{1,0:T(8,128)(2,1)} %param.18), channel_id=1, source_target_pairs={{0,16},{16,0},{1,17},{17,1},{2,18},{18,2},{3,19},{19,3},{4,20},{20... | collective-permute-start | bytes 3145736 | tf_op jit(solution)/shard_map/ppermute | solution.py:499
  40.7 14.9 %copy-start.12 = (bf16[2048,256]{1,0:T(8,128)(2,1)S(1)}, bf16[2048,256]{1,0:T(8,128)(2,1)}, u32[]{:S(2)}) copy-start(bf16[2048,256]{1,0:T(8,128)(2,1)} %param.19) | copy-start | bytes 3145732
  40.7 32.9 %copy-start.5 = (bf16[256,1536]{1,0:T(8,128)(2,1)S(1)}, bf16[256,1536]{1,0:T(8,128)(2,1)}, u32[]{:S(2)}) copy-start(bf16[256,1536]{1,0:T(8,128)(2,1)} %copy-done.4) | copy-start | bytes 2359300
  55.6 37.7 %copy-start.15 = (bf16[256,2048]{1,0:T(8,128)(2,1)S(1)}, bf16[256,2048]{1,0:T(8,128)(2,1)}, u32[]{:S(2)}) copy-start(bf16[256,2048]{1,0:T(8,128)(2,1)} %param.18) | copy-start | bytes 3145732
  55.6 39.2 %collective-permute-start.4 = (bf16[2048,256]{1,0:T(8,128)(2,1)S(1)}, bf16[2048,256]{1,0:T(8,128)(2,1)S(1)}, u32[]{:S(2)}, u32[]{:S(2)}) collective-permute-start(bf16[2048,256]{1,0:T(8,128)(2,1)S(1)} %copy-done.12), channel_id=1, source_target_pairs={{0,8},{8,0},{1,9},{9,1},{2,10},{10,2},{3,11},{11,3},{4,12},{12,4},... | collective-permute-start | bytes 3145736 | tf_op jit(solution)/shard_map/ppermute | solution.py:499
  76.8 22.6 %collective-permute-start.8 = (bf16[1024,1536]{1,0:T(8,128)(2,1)}, bf16[1024,1536]{1,0:T(8,128)(2,1)}, u32[]{:S(2)}, u32[]{:S(2)}) collective-permute-start(bf16[1024,1536]{1,0:T(8,128)(2,1)} %pad_maximum_fusion.3.refs_0_.refs_1_), channel_id=1, source_target_pairs={{0,4},{4,0},{1,5},{5,1},{2,6},{6,2},{3,7},{7,3},{8,12},{12,8},{9,1... | collective-permute-start | bytes 9437192 | tf_op jit(solution)/shard_map/ppermute | solution.py:499
  76.8 4.0 collective-permute-start.1
  80.9 1.6 collective-permute-start.2
  96.4 45.4 %collective-permute-start.9 = (bf16[512,2048]{1,0:T(8,128)(2,1)}, bf16[512,2048]{1,0:T(8,128)(2,1)}, u32[]{:S(2)}, u32[]{:S(2)}) collective-permute-start(bf16[512,2048]{1,0:T(8,128)(2,1)} %pad_maximum_fusion.6), channel_id=1, source_target_pairs={{0,8},{8,0},{1,9},{9,1},{2,10},{10,2},{3,11},{11,3},{4,12},{12,4},... | collective-permute-start | bytes 6291464 | tf_op jit(solution)/shard_map/ppermute | solution.py:499
  97.9 48.3 %collective-permute-start.10 = (bf16[512,2048]{1,0:T(8,128)(2,1)S(1)}, bf16[512,2048]{1,0:T(8,128)(2,1)}, u32[]{:S(2)}, u32[]{:S(2)}) collective-permute-start(bf16[512,2048]{1,0:T(8,128)(2,1)S(1)} %pad_maximum_fusion.4), channel_id=1, source_target_pairs={{0,16},{16,0},{1,17},{17,1},{2,18},{18,2},{3,19},{19,3},{4,20},{20... | collective-permute-start | bytes 6291464 | tf_op jit(solution)/shard_map/ppermute | solution.py:499
  99.4 128.2 %all-gather.16.cloned.1.call-start = ((), (), s32[]{:S(2)}) async-start(), calls=%async_computation.10 | async-start | bytes 5242880 | tf_op jit(solution)/shard_map/all_gather | solution.py:628
  113.3 28.5 %copy-start.3 = (bf16[512,2048]{1,0:T(8,128)(2,1)S(1)}, bf16[512,2048]{1,0:T(8,128)(2,1)}, u32[]{:S(2)}) copy-start(bf16[512,2048]{1,0:T(8,128)(2,1)} %pad_maximum_fusion.6) | copy-start | bytes 6291460
  146.1 219.4 %reduce-scatter.4.cloned.1.call-start = ((), (), s32[]{:S(2)}) async-start(), calls=%async_computation.4 | async-start | bytes 5242880 | tf_op jit(solution)/shard_map/reduce_scatter | solution.py:597
  146.4 66.9 %copy-start.2 = (bf16[2048,512]{1,0:T(8,128)(2,1)S(1)}, bf16[2048,512]{1,0:T(8,128)(2,1)}, u32[]{:S(2)}) copy-start(bf16[2048,512]{1,0:T(8,128)(2,1)} %pad_maximum_fusion.5) | copy-start | bytes 6291460
  146.4 26.4 %collective-permute-start.11 = (bf16[2048,256]{1,0:T(8,128)(2,1)}, bf16[2048,256]{1,0:T(8,128)(2,1)S(1)}, u32[]{:S(2)}, u32[]{:S(2)}) collective-permute-start(bf16[2048,256]{1,0:T(8,128)(2,1)} %all-gather.8.cloned.1.call-done), channel_id=1, source_target_pairs={{0,16},{16,0},{1,17},{17,1},{2,18},{18,2},{3,19},{19,3},{4,20},{20... | collective-permute-start | bytes 3145736 | tf_op jit(solution)/shard_map/ppermute | solution.py:499
  147.4 66.0 %collective-permute-start.13 = (bf16[2048,512]{1,0:T(8,128)(2,1)}, bf16[2048,512]{1,0:T(8,128)(2,1)S(1)}, u32[]{:S(2)}, u32[]{:S(2)}) collective-permute-start(bf16[2048,512]{1,0:T(8,128)(2,1)} %pad_maximum_fusion.5), channel_id=1, source_target_pairs={{0,16},{16,0},{1,17},{17,1},{2,18},{18,2},{3,19},{19,3},{4,20},{20... | collective-permute-start | bytes 6291464 | tf_op jit(solution)/shard_map/ppermute | solution.py:499
  174.2 41.8 %copy-start.10 = (bf16[2048,256]{1,0:T(8,128)(2,1)S(1)}, bf16[2048,256]{1,0:T(8,128)(2,1)}, u32[]{:S(2)}) copy-start(bf16[2048,256]{1,0:T(8,128)(2,1)} %all-gather.8.cloned.1.call-done) | copy-start | bytes 3145732
  174.2 41.7 %collective-permute-start.12 = (bf16[2048,512]{1,0:T(8,128)(2,1)S(1)}, bf16[2048,512]{1,0:T(8,128)(2,1)S(1)}, u32[]{:S(2)}, u32[]{:S(2)}) collective-permute-start(bf16[2048,512]{1,0:T(8,128)(2,1)S(1)} %pad_maximum_fusion.7), channel_id=1, source_target_pairs={{0,8},{8,0},{1,9},{9,1},{2,10},{10,2},{3,11},{11,3},{4,12},{12,4},... | collective-permute-start | bytes 6291464 | tf_op jit(solution)/shard_map/ppermute | solution.py:499
  227.6 7.5 collective-permute-start.14
  229.7 22.2 %copy-start.13 = (bf16[1024,2048]{1,0:T(8,128)(2,1)}, bf16[1024,2048]{1,0:T(8,128)(2,1)S(1)}, u32[]{:S(2)}) copy-start(bf16[1024,2048]{1,0:T(8,128)(2,1)S(1)} %constant_dynamic-update-slice_fusion.3.refs_0_.refs_2_) | copy-start | bytes 12582916
  229.7 22.2 %copy-start.7 = (bf16[2048,1024]{1,0:T(8,128)(2,1)S(1)}, bf16[2048,1024]{1,0:T(8,128)(2,1)}, u32[]{:S(2)}) copy-start(bf16[2048,1024]{1,0:T(8,128)(2,1)} %pad_maximum_fusion.2.refs_1_.refs_0_) | copy-start | bytes 12582916
  229.7 22.4 %collective-permute-start.15 = (bf16[1024,2048]{1,0:T(8,128)(2,1)S(1)}, bf16[1024,2048]{1,0:T(8,128)(2,1)}, u32[]{:S(2)}, u32[]{:S(2)}) collective-permute-start(bf16[1024,2048]{1,0:T(8,128)(2,1)S(1)} %constant_dynamic-update-slice_fusion.3.refs_0_.refs_2_), channel_id=1, source_target_pairs={{0,4},{4,0},{1,5},{5,1},{2,6},{6,2},{3,7},{7,3},{8,12},{12,8},{9,1... | collective-permute-start | bytes 12582920 | tf_op jit(solution)/shard_map/ppermute | solution.py:499
  230.5 21.6 %collective-permute-start.16 = (bf16[1024,2048]{1,0:T(8,128)(2,1)S(1)}, bf16[1024,2048]{1,0:T(8,128)(2,1)}, u32[]{:S(2)}, u32[]{:S(2)}) collective-permute-start(bf16[1024,2048]{1,0:T(8,128)(2,1)S(1)} %copy-done.6), channel_id=1, source_target_pairs={{0,4},{4,0},{1,5},{5,1},{2,6},{6,2},{3,7},{7,3},{8,12},{12,8},{9,1... | collective-permute-start | bytes 12582920 | tf_op jit(solution)/shard_map/ppermute | solution.py:499
  251.9 23.8 %collective-permute-start.17 = (bf16[2048,1024]{1,0:T(8,128)(2,1)S(1)}, bf16[2048,1024]{1,0:T(8,128)(2,1)}, u32[]{:S(2)}, u32[]{:S(2)}) collective-permute-start(bf16[2048,1024]{1,0:T(8,128)(2,1)S(1)} %copy-done.7), channel_id=1, source_target_pairs={{0,4},{4,0},{1,5},{5,1},{2,6},{6,2},{3,7},{7,3},{8,12},{12,8},{9,1... | collective-permute-start | bytes 12582920 | tf_op jit(solution)/shard_map/ppermute | solution.py:499
  290.1 162.0 %all-gather.10.cloned.1.call-start = ((), (), s32[]{:S(2)}) async-start(), calls=%async_computation.5 | async-start | bytes 5242880 | tf_op jit(solution)/shard_map/all_gather | solution.py:594
  370.5 200.2 %reduce-scatter.6.cloned.1.call-start = ((), (), s32[]{:S(2)}) async-start(), calls=%async_computation.6 | async-start | bytes 5242880 | tf_op jit(solution)/shard_map/reduce_scatter | solution.py:597
  372.9 3.7 collective-permute-start.18
  377.2 3.7 collective-permute-start.19
  381.6 1.2 collective-permute-start.20
  382.8 3.7 collective-permute-start.21
  386.5 6.3 collective-permute-start.22
  495.2 162.1 %all-gather.12.cloned.1.call-start = ((), (), s32[]{:S(2)}) async-start(), calls=%async_computation.7 | async-start | bytes 5242880 | tf_op jit(solution)/shard_map/all_gather | solution.py:594
  495.3 7.7 copy-start.19
  495.3 7.7 copy-start.21
  502.8 12.9 %collective-permute-start.23 = (bf16[1024,2048]{1,0:T(8,128)(2,1)S(1)}, bf16[1024,2048]{1,0:T(8,128)(2,1)S(1)}, u32[]{:S(2)}, u32[]{:S(2)}) collective-permute-start(bf16[1024,2048]{1,0:T(8,128)(2,1)S(1)} %convolution_convert_fusion.3), channel_id=1, source_target_pairs={{0,4},{4,0},{1,5},{5,1},{2,6},{6,2},{3,7},{7,3},{8,12},{12,8},{9,1... | collective-permute-start | bytes 12582920 | tf_op jit(solution)/shard_map/ppermute | solution.py:499
  508.1 17.3 %collective-permute-start.25 = (bf16[1024,2048]{1,0:T(8,128)(2,1)S(1)}, bf16[1024,2048]{1,0:T(8,128)(2,1)S(1)}, u32[]{:S(2)}, u32[]{:S(2)}) collective-permute-start(bf16[1024,2048]{1,0:T(8,128)(2,1)S(1)} %convolution_convert_fusion.1), channel_id=1, source_target_pairs={{0,4},{4,0},{1,5},{5,1},{2,6},{6,2},{3,7},{7,3},{8,12},{12,8},{9,1... | collective-permute-start | bytes 12582920 | tf_op jit(solution)/shard_map/ppermute | solution.py:499
  515.7 17.7 %collective-permute-start.24 = (bf16[2048,1024]{1,0:T(8,128)(2,1)S(1)}, bf16[2048,1024]{1,0:T(8,128)(2,1)S(1)}, u32[]{:S(2)}, u32[]{:S(2)}) collective-permute-start(bf16[2048,1024]{1,0:T(8,128)(2,1)S(1)} %convolution_convert_fusion.2), channel_id=1, source_target_pairs={{0,4},{4,0},{1,5},{5,1},{2,6},{6,2},{3,7},{7,3},{8,12},{12,8},{9,1... | collective-permute-start | bytes 12582920 | tf_op jit(solution)/shard_map/ppermute | solution.py:499
  525.4 8.1 copy-start.22
  575.9 218.6 %reduce-scatter.8.cloned.1.call-start = ((), (), s32[]{:S(2)}) async-start(), calls=%async_computation.8 | async-start | bytes 5242880 | tf_op jit(solution)/shard_map/reduce_scatter | solution.py:597
  576.0 6.5 copy-start.9
  581.0 48.8 %collective-permute-start.26 = (bf16[512,2048]{1,0:T(8,128)(2,1)}, bf16[512,2048]{1,0:T(8,128)(2,1)}, u32[]{:S(2)}, u32[]{:S(2)}) collective-permute-start(bf16[512,2048]{1,0:T(8,128)(2,1)} %get-tuple-element.138), channel_id=1, source_target_pairs={{0,16},{16,0},{1,17},{17,1},{2,18},{18,2},{3,19},{19,3},{4,20},{20... | collective-permute-start | bytes 6291464 | tf_op jit(solution)/shard_map/ppermute | solution.py:499
  585.5 47.4 %collective-permute-start.27 = (bf16[2048,512]{1,0:T(8,128)(2,1)}, bf16[2048,512]{1,0:T(8,128)(2,1)}, u32[]{:S(2)}, u32[]{:S(2)}) collective-permute-start(bf16[2048,512]{1,0:T(8,128)(2,1)} %pad_maximum_fusion.9), channel_id=1, source_target_pairs={{0,8},{8,0},{1,9},{9,1},{2,10},{10,2},{3,11},{11,3},{4,12},{12,4},... | collective-permute-start | bytes 6291464 | tf_op jit(solution)/shard_map/ppermute | solution.py:499
  589.6 89.7 %collective-permute-start.28 = (bf16[512,2048]{1,0:T(8,128)(2,1)}, bf16[512,2048]{1,0:T(8,128)(2,1)}, u32[]{:S(2)}, u32[]{:S(2)}) collective-permute-start(bf16[512,2048]{1,0:T(8,128)(2,1)} %get-tuple-element.134), channel_id=1, source_target_pairs={{0,16},{16,0},{1,17},{17,1},{2,18},{18,2},{3,19},{19,3},{4,20},{20... | collective-permute-start | bytes 6291464 | tf_op jit(solution)/shard_map/ppermute | solution.py:499
  699.5 29.7 %collective-permute-start.29 = (bf16[1024,1536]{1,0:T(8,128)(2,1)}, bf16[1024,1536]{1,0:T(8,128)(2,1)}, u32[]{:S(2)}, u32[]{:S(2)}) collective-permute-start(bf16[1024,1536]{1,0:T(8,128)(2,1)} %convolution_convert_fusion), channel_id=1, source_target_pairs={{0,4},{4,0},{1,5},{5,1},{2,6},{6,2},{3,7},{7,3},{8,12},{12,8},{9,1... | collective-permute-start | bytes 9437192 | tf_op jit(solution)/shard_map/ppermute | solution.py:499
  702.1 25.6 %collective-permute-start.39 = (bf16[2048,256]{1,0:T(8,128)(2,1)S(1)}, bf16[2048,256]{1,0:T(8,128)(2,1)S(1)}, u32[]{:S(2)}, u32[]{:S(2)}) collective-permute-start(bf16[2048,256]{1,0:T(8,128)(2,1)S(1)} %slice.159), channel_id=1, source_target_pairs={{0,16},{16,0},{1,17},{17,1},{2,18},{18,2},{3,19},{19,3},{4,20},{20... | collective-permute-start | bytes 3145736 | tf_op jit(solution)/shard_map/ppermute | solution.py:499
  703.7 25.6 %copy-start.20 = (bf16[1024,2048]{1,0:T(8,128)(2,1)S(1)}, bf16[1024,2048]{1,0:T(8,128)(2,1)}, u32[]{:S(2)}) copy-start(bf16[1024,2048]{1,0:T(8,128)(2,1)} %get-tuple-element.122) | copy-start | bytes 12582916
  706.7 22.5 %copy-start.18 = (bf16[1024,1536]{1,0:T(8,128)(2,1)S(1)}, bf16[1024,1536]{1,0:T(8,128)(2,1)}, u32[]{:S(2)}) copy-start(bf16[1024,1536]{1,0:T(8,128)(2,1)} %shard_map.187.refs_0_) | copy-start | bytes 9437188
  706.9 29.6 %collective-permute-start.37 = (bf16[256,2048]{1,0:T(8,128)(2,1)S(1)}, bf16[256,2048]{1,0:T(8,128)(2,1)S(1)}, u32[]{:S(2)}, u32[]{:S(2)}) collective-permute-start(bf16[256,2048]{1,0:T(8,128)(2,1)S(1)} %constant_dynamic-slice_fusion.1), channel_id=1, source_target_pairs={{0,8},{8,0},{1,9},{9,1},{2,10},{10,2},{3,11},{11,3},{4,12},{12,4},... | collective-permute-start | bytes 3145736 | tf_op jit(solution)/shard_map/ppermute | solution.py:499
  734.9 13.7 %collective-permute-start.32 = (bf16[512,512]{1,0:T(8,128)(2,1)S(1)}, bf16[512,512]{1,0:T(8,128)(2,1)S(1)}, u32[]{:S(2)}, u32[]{:S(2)}) collective-permute-start(bf16[512,512]{1,0:T(8,128)(2,1)S(1)} %pad_maximum_fusion.13), channel_id=1, source_target_pairs={{0,8},{8,0},{1,9},{9,1},{2,10},{10,2},{3,11},{11,3},{4,12},{12,4},... | collective-permute-start | bytes 1572872 | tf_op jit(solution)/shard_map/ppermute | solution.py:499
  738.3 12.1 %copy-start = (bf16[512,2048]{1,0:T(8,128)(2,1)S(1)}, bf16[512,2048]{1,0:T(8,128)(2,1)}, u32[]{:S(2)}) copy-start(bf16[512,2048]{1,0:T(8,128)(2,1)} %get-tuple-element.130) | copy-start | bytes 6291460
  738.3 31.2 %collective-permute-start.30 = (bf16[512,1024]{1,0:T(8,128)(2,1)S(1)}, bf16[512,1024]{1,0:T(8,128)(2,1)S(1)}, u32[]{:S(2)}, u32[]{:S(2)}) collective-permute-start(bf16[512,1024]{1,0:T(8,128)(2,1)S(1)} %slice.151), channel_id=1, source_target_pairs={{0,16},{16,0},{1,17},{17,1},{2,18},{18,2},{3,19},{19,3},{4,20},{20... | collective-permute-start | bytes 3145736 | tf_op jit(solution)/shard_map/ppermute | solution.py:499
  741.1 29.3 %collective-permute-start.34 = (bf16[512,1024]{1,0:T(8,128)(2,1)S(1)}, bf16[512,1024]{1,0:T(8,128)(2,1)S(1)}, u32[]{:S(2)}, u32[]{:S(2)}) collective-permute-start(bf16[512,1024]{1,0:T(8,128)(2,1)S(1)} %fusion.12), channel_id=1, source_target_pairs={{0,4},{4,0},{1,5},{5,1},{2,6},{6,2},{3,7},{7,3},{8,12},{12,8},{9,1... | collective-permute-start | bytes 3145736 | tf_op jit(solution)/shard_map/ppermute | solution.py:499
  748.8 19.8 %collective-permute-start.33 = (bf16[256,512]{1,0:T(8,128)(2,1)S(1)}, bf16[256,512]{1,0:T(8,128)(2,1)S(1)}, u32[]{:S(2)}, u32[]{:S(2)}) collective-permute-start(bf16[256,512]{1,0:T(8,128)(2,1)S(1)} %slice.157), channel_id=1, source_target_pairs={{0,16},{16,0},{1,17},{17,1},{2,18},{18,2},{3,19},{19,3},{4,20},{20... | collective-permute-start | bytes 786440 | tf_op jit(solution)/shard_map/ppermute | solution.py:499
  752.9 26.2 %collective-permute-start.38 = (bf16[256,2048]{1,0:T(8,128)(2,1)S(1)}, bf16[256,2048]{1,0:T(8,128)(2,1)S(1)}, u32[]{:S(2)}, u32[]{:S(2)}) collective-permute-start(bf16[256,2048]{1,0:T(8,128)(2,1)S(1)} %constant_dynamic-slice_fusion), channel_id=1, source_target_pairs={{0,8},{8,0},{1,9},{9,1},{2,10},{10,2},{3,11},{11,3},{4,12},{12,4},... | collective-permute-start | bytes 3145736 | tf_op jit(solution)/shard_map/ppermute | solution.py:499
  769.9 20.4 %collective-permute-start.31 = (bf16[256,1024]{1,0:T(8,128)(2,1)S(1)}, bf16[256,1024]{1,0:T(8,128)(2,1)S(1)}, u32[]{:S(2)}, u32[]{:S(2)}) collective-permute-start(bf16[256,1024]{1,0:T(8,128)(2,1)S(1)} %constant_dynamic-slice_fusion.7), channel_id=1, source_target_pairs={{0,8},{8,0},{1,9},{9,1},{2,10},{10,2},{3,11},{11,3},{4,12},{12,4},... | collective-permute-start | bytes 1572872 | tf_op jit(solution)/shard_map/ppermute | solution.py:499
  771.8 12.4 %collective-permute-start.35 = (bf16[512,512]{1,0:T(8,128)(2,1)S(1)}, bf16[512,512]{1,0:T(8,128)(2,1)S(1)}, u32[]{:S(2)}, u32[]{:S(2)}) collective-permute-start(bf16[512,512]{1,0:T(8,128)(2,1)S(1)} %slice.145), channel_id=1, source_target_pairs={{0,16},{16,0},{1,17},{17,1},{2,18},{18,2},{3,19},{19,3},{4,20},{20... | collective-permute-start | bytes 1572872 | tf_op jit(solution)/shard_map/ppermute | solution.py:499
  784.3 9.3 %collective-permute-start.36 = (bf16[512,256]{1,0:T(8,128)(2,1)S(1)}, bf16[512,256]{1,0:T(8,128)(2,1)S(1)}, u32[]{:S(2)}, u32[]{:S(2)}) collective-permute-start(bf16[512,256]{1,0:T(8,128)(2,1)S(1)} %constant_dynamic-slice_fusion.2), channel_id=1, source_target_pairs={{0,8},{8,0},{1,9},{9,1},{2,10},{10,2},{3,11},{11,3},{4,12},{12,4},... | collective-permute-start | bytes 786440 | tf_op jit(solution)/shard_map/ppermute | solution.py:499
  (7 other events, 28.0 us)
Sparse Core Ops, SparseCore 0:
  9.6 83.4 all-gather.13
  99.5 27.2 all-gather.7
  146.3 81.2 all-gather.15
  290.2 75.3 reduce-scatter.3
  370.6 81.4 all-gather.9
  495.3 75.2 reduce-scatter.5
  576.1 81.2 all-gather.11
  699.7 75.4 reduce-scatter.7

commit v5 on v4

--- a/solution.py
+++ b/solution.py
@@ -318,7 +318,7 @@
 
 
 def over_out(lefts, rights, transposed):
-    size = 256
+    size = 512 if len(lefts) == 1 else 256
     free = 0 if transposed else 1
     steps = rights[0][0].shape[free] // size
     count = steps * len(rights[0])

time: 816 us -> 814 us (level)
  no operation moved by 1% of the time
where the time goes in v5:
time: 814 us; the launch traced here: 806 us
  waiting for transfers between devices  441 us (54%)
  Pallas kernels  171 us (21%)
  matrix products  59.6 us (7%)
  other arithmetic  44.6 us (5%)
  starting transfers between devices  44.3 us (5%)
  local copies, waits for them, and re-layouts  27.2 us (3%)
  between operations  19 us (2%)
    ppermute x38, waiting for transfers between devices, swap(): return lax.ppermute(values, axis, SWAP)  241 us
    pallas_call x13, Pallas kernels, kernel_call(): pl.pallas_call(body, grid=grid, in_specs=ins, out_specs=[spec for _, spec...  171 us
    reduce_scatter x3, waiting for transfers between devices, line_out(): return lax.psum_scatter(partial, line, scatter_dimension=0, tiled=True)  103 us
    all_gather x3, waiting for transfers between devices, line_in(): return lax.all_gather(values, line, axis=0, tiled=True)  82.5 us
    dot_general x10, matrix products, dot_tn(): lax.dot_general(left, right, (((0,), (0,)), ((), ())), preferred_element_...  59.6 us
    ppermute x38, starting transfers between devices, swap(): return lax.ppermute(values, axis, SWAP)  39 us
  transfers between devices with their start and end apart: 48, of which 28 were waited for; matrix products, arithmetic and copies ran while one was open for 15% of the time, Pallas kernels for 11%

profile of v5, /device:TPU:0, one launch (start us, length us, event | category | flops | bytes accessed | tf_op | source)
XLA Modules:
  0.0 806.2 jit_solution(2644417651626606335)
XLA Ops:
  11.0 3.0 collective-permute-start.6
  14.0 18.4 %collective-permute-done.6 = bf16[256,1536]{1,0:T(8,128)(2,1)} collective-permute-done((bf16[256,1536]{1,0:T(8,128)(2,1)S(1)}, bf16[256,1536]{1,0:T(8,128)(2,1)}, u32[]{:S(2)}, u32[]{:S(2)}) %collective-permute-start.6) | collective-permute-done | bytes 786464 | tf_op jit(solution)/shard_map/ppermute | solution.py:499
  35.8 2.1 collective-permute-start.7
  38.7 2.0 collective-permute-start.5
  40.7 13.4 %collective-permute-done.3 = bf16[256,2048]{1,0:T(8,128)(2,1)} collective-permute-done((bf16[256,2048]{1,0:T(8,128)(2,1)}, bf16[256,2048]{1,0:T(8,128)(2,1)}, u32[]{:S(2)}, u32[]{:S(2)}) %collective-permute-start.3) | collective-permute-done | bytes 1048608 | tf_op jit(solution)/shard_map/ppermute | solution.py:499
  57.4 16.1 %collective-permute-done.7 = bf16[512,1536]{1,0:T(8,128)(2,1)} collective-permute-done((bf16[512,1536]{1,0:T(8,128)(2,1)}, bf16[512,1536]{1,0:T(8,128)(2,1)}, u32[]{:S(2)}, u32[]{:S(2)}) %collective-permute-start.7) | collective-permute-done | bytes 1572896 | tf_op jit(solution)/shard_map/ppermute | solution.py:499
  73.5 3.3 pad_maximum_fusion.3.refs_0_.refs_1_
  76.8 2.1 collective-permute-start.1
  83.7 9.7 %collective-permute-done.5 = bf16[256,2048]{1,0:T(8,128)(2,1)S(1)} collective-permute-done((bf16[256,2048]{1,0:T(8,128)(2,1)}, bf16[256,2048]{1,0:T(8,128)(2,1)S(1)}, u32[]{:S(2)}, u32[]{:S(2)}) %collective-permute-start.5) | collective-permute-done | bytes 1048608 | tf_op jit(solution)/shard_map/ppermute | solution.py:499
  99.5 13.9 %shard_map.177 = (bf16[1024,2048]{1,0:T(8,128)(2,1)}, bf16[1024,512]{1,0:T(8,128)(2,1)}, bf16[1024,512]{1,0:T(8,128)(2,1)}, bf16[1024,512]{1,0:T(8,128)(2,1)}) custom-call(s32[8]{0:T(128)S(1)} %fusion.22.from_ref, bf16[1024,2048]{1,0:T(8,128)(2,1)} %bitcast.25, bf16[1024,1536]{1,0:T(8,128)(2,1)} %pad_maximum_fusion.3.refs_0_.refs_1_, ...), custom_call_target="tpu_custom_call" | custom-call | flops 6442450944 | bytes 18874400 | tf_op jit(solution)/shard_map/pallas_call | solution.py:64
  113.3 11.0 %shard_map.178 = (bf16[1024,512]{1,0:T(8,128)(2,1)}, f32[1024,512]{1,0:T(8,128)}) custom-call(bf16[1024,512]{1,0:T(8,128)(2,1)} %get-tuple-element.78.q_ref, bf16[1024,512]{1,0:T(8,128)(2,1)} %get-tuple-element.79.k_ref, bf16[1024,512]{1,0:T(8,128)(2,1)} %get-tuple-element.80.v_ref), custom_call_target="tpu_custom_call" | custom-call | flops 1610612736 | bytes 6291456 | tf_op jit(solution)/shard_map/pallas_call | solution.py:64
  124.3 17.6 %collective-permute-done.9 = bf16[512,2048]{1,0:T(8,128)(2,1)} collective-permute-done((bf16[512,2048]{1,0:T(8,128)(2,1)}, bf16[512,2048]{1,0:T(8,128)(2,1)}, u32[]{:S(2)}, u32[]{:S(2)}) %collective-permute-start.9) | collective-permute-done | bytes 2097184 | tf_op jit(solution)/shard_map/ppermute | solution.py:499
  143.8 2.3 pad_maximum_fusion.refs_2_.refs_4_
  148.5 24.3 %collective-permute-done.11 = bf16[2048,256]{1,0:T(8,128)(2,1)S(1)} collective-permute-done((bf16[2048,256]{1,0:T(8,128)(2,1)}, bf16[2048,256]{1,0:T(8,128)(2,1)S(1)}, u32[]{:S(2)}, u32[]{:S(2)}) %collective-permute-start.11) | collective-permute-done | bytes 1048608 | tf_op jit(solution)/shard_map/ppermute | solution.py:499
  175.1 38.2 %collective-permute-done.13 = bf16[2048,512]{1,0:T(8,128)(2,1)S(1)} collective-permute-done((bf16[2048,512]{1,0:T(8,128)(2,1)}, bf16[2048,512]{1,0:T(8,128)(2,1)S(1)}, u32[]{:S(2)}, u32[]{:S(2)}) %collective-permute-start.13) | collective-permute-done | bytes 2097184 | tf_op jit(solution)/shard_map/ppermute | solution.py:499
  213.4 2.6 pad_maximum_fusion.2.refs_1_.refs_0_
  216.2 2.3 pad_maximum_fusion.1.refs_0_
  218.6 9.0 %all-gather.16.cloned.1.call-done = bf16[4096,512]{1,0:T(8,128)(2,1)} async-done(((bf16[1024,512]{1,0:T(8,128)(2,1)}), bf16[4096,512]{1,0:T(8,128)(2,1)}) %all-gather.16.cloned.1.call-update) | async-done | bytes 4194320 | tf_op jit(solution)/shard_map/all_gather | solution.py:628
  230.6 4.4 collective-permute-done.14.refs_1_
  235.1 16.8 %shard_map.179 = (f32[1024,2048]{1,0:T(8,128)}, bf16[1024,2048]{1,0:T(8,128)(2,1)}) custom-call(s32[8]{0:T(128)S(1)} %fusion.22.from_ref, bf16[1024,2048]{1,0:T(8,128)(2,1)} %bitcast.26, bf16[4,1024,512]{2,1,0:T(8,128)(2,1)} %bitcast.27, bf16[2048,1024]{1,0:T(8,128)(2,1)} %pad_maximum_fusion.1.refs_0_, bf16[2048,1024]{1,0:T(8,128)(2,1)} %collective-permute-done.14.refs_1_), custom_call_target="tpu_custom_call" | custom-call | flops 8589934592 | bytes 29360160 | tf_op jit(solution)/shard_map/pallas_call | solution.py:64
  252.1 23.5 %shard_map.180 = (bf16[1024,2048]{1,0:T(8,128)(2,1)}, bf16[1024,2048]{1,0:T(8,128)(2,1)}, bf16[1024,2048]{1,0:T(8,128)(2,1)}) custom-call(bf16[1024,2048]{1,0:T(8,128)(2,1)} %get-tuple-element.111.x_ref, bf16[1024,2048]{1,0:T(8,128)(2,1)} %copy-done.13, bf16[1024,2048]{1,0:T(8,128)(2,1)} %collective-permute-done.15.refs_1_.refs_3_, ...), custom_call_target="tpu_custom_call" | custom-call | flops 17179869184 | bytes 33554432 | tf_op jit(solution)/shard_map/pallas_call | solution.py:64
  275.7 14.0 %shard_map.181 = bf16[1024,2048]{1,0:T(8,128)(2,1)} custom-call(bf16[1024,2048]{1,0:T(8,128)(2,1)} %get-tuple-element.112.refs_0_, bf16[2048,1024]{1,0:T(8,128)(2,1)} %pad_maximum_fusion.2.refs_1_.refs_0_, bf16[2048,1024]{1,0:T(8,128)(2,1)} %collective-permute-done.17.refs_2_.refs_1_), custom_call_target="tpu_custom_call" | custom-call | flops 8589934592 | bytes 16777216 | tf_op jit(solution)/shard_map/pallas_call | solution.py:64
  289.8 3.1 constant_dynamic-slice_fusion.14.r_ref
  292.9 72.3 %reduce-scatter.4.cloned.1.call-done.part_ref = bf16[256,2048]{1,0:T(8,128)(2,1)} async-done(((bf16[1024,2048]{1,0:T(8,128)(2,1)}), bf16[256,2048]{1,0:T(8,128)(2,1)}) %reduce-scatter.4.cloned.1.call-update) | async-done | bytes 1048592 | tf_op jit(solution)/shard_map/reduce_scatter | solution.py:597
  365.2 4.9 shard_map.182
  374.1 2.1 collective-permute-done.18
  378.4 2.1 collective-permute-done.19
  383.9 2.2 collective-permute-done.21
  386.1 2.9 collective-permute-start.22
  389.7 2.7 collective-permute-done.22
  393.5 58.2 %all-gather.10.cloned.1.call-done.y_ref = bf16[1024,2048]{1,0:T(8,128)(2,1)} async-done(((bf16[256,2048]{1,0:T(8,128)(2,1)}), bf16[1024,2048]{1,0:T(8,128)(2,1)}) %all-gather.10.cloned.1.call-update) | async-done | bytes 4194320 | tf_op jit(solution)/shard_map/all_gather | solution.py:594
  451.7 18.2 %shard_map.183 = (bf16[1024,2048]{1,0:T(8,128)(2,1)}, bf16[1024,2048]{1,0:T(8,128)(2,1)}) custom-call(bf16[1024,2048]{1,0:T(8,128)(2,1)} %all-gather.10.cloned.1.call-done.y_ref, bf16[2048,1024]{1,0:T(8,128)(2,1)} %pad_maximum_fusion.2.refs_1_.refs_0_, bf16[2048,1024]{1,0:T(8,128)(2,1)} %collective-permute-done.17.refs_2_.refs_1_, ...), custom_call_target="tpu_custom_call" | custom-call | flops 8589934592 | bytes 29360128 | tf_op jit(solution)/shard_map/pallas_call | solution.py:64
  469.9 24.9 %shard_map.184 = bf16[1024,2048]{1,0:T(8,128)(2,1)} custom-call(bf16[1024,2048]{1,0:T(8,128)(2,1)} %get-tuple-element.109.refs_0_, bf16[1024,2048]{1,0:T(8,128)(2,1)} %get-tuple-element.110.refs_1_, bf16[1024,2048]{1,0:T(8,128)(2,1)} %copy-done.13, bf16[1024,2048]{1,0:T(8,128)(2,1)} %collective-permute-done.15.refs_1_.refs_3_, ...), custom_call_target="tpu_custom_call" | custom-call | flops 17179869184 | bytes 29360128 | tf_op jit(solution)/shard_map/pallas_call | solution.py:64
  494.9 7.5 convolution_convert_fusion.3
  502.6 5.1 convolution_convert_fusion.1
  508.2 7.1 convolution_convert_fusion.2
  515.4 9.6 %add_convert_fusion.2 = bf16[1024,2048]{1,0:T(8,128)(2,1)} fusion(bf16[1024,2048]{1,0:T(8,128)(2,1)S(1)} %collective-permute-done.23, bf16[1024,2048]{1,0:T(8,128)(2,1)} %get-tuple-element.109.refs_0_, bf16[1024,2048]{1,0:T(8,128)(2,1)} %get-tuple-element.111.x_ref), kind=kOutput, calls=%fused_computation.2 | convolution fusion | flops 4301258752 | bytes 14680064 | tf_op jit(solution)/shard_map/dot_general | solution.py:55
  525.0 8.0 add_convert_fusion
  533.0 6.7 add_convert_fusion.1
  539.7 30.6 %reduce-scatter.6.cloned.1.call-done.part_ref = bf16[256,2048]{1,0:T(8,128)(2,1)} async-done(((bf16[1024,2048]{1,0:T(8,128)(2,1)}), bf16[256,2048]{1,0:T(8,128)(2,1)}) %reduce-scatter.6.cloned.1.call-update) | async-done | bytes 1048592 | tf_op jit(solution)/shard_map/reduce_scatter | solution.py:597
  570.3 5.2 shard_map.185
  575.6 5.0 fusion.29
  586.6 2.6 fusion.27
  589.8 2.3 constant_dynamic-slice_fusion.9.refs_0_
  592.1 2.3 constant_dynamic-slice_fusion.8.refs_1_
  595.8 33.7 %collective-permute-done.26 = bf16[512,2048]{1,0:T(8,128)(2,1)} collective-permute-done((bf16[512,2048]{1,0:T(8,128)(2,1)}, bf16[512,2048]{1,0:T(8,128)(2,1)}, u32[]{:S(2)}, u32[]{:S(2)}) %collective-permute-start.26) | collective-permute-done | bytes 2097184 | tf_op jit(solution)/shard_map/ppermute | solution.py:499
  629.4 3.2 collective-permute-done.27
  632.6 24.4 %all-gather.12.cloned.1.call-done.left_ref = bf16[1024,2048]{1,0:T(8,128)(2,1)} async-done(((bf16[256,2048]{1,0:T(8,128)(2,1)}), bf16[1024,2048]{1,0:T(8,128)(2,1)}) %all-gather.12.cloned.1.call-update) | async-done | bytes 4194320 | tf_op jit(solution)/shard_map/all_gather | solution.py:594
  657.0 5.9 shard_map.186.g_ref
  662.9 15.9 %shard_map.187.refs_0_ = bf16[1024,1536]{1,0:T(8,128)(2,1)} custom-call(bf16[1024,512]{1,0:T(8,128)(2,1)} %get-tuple-element.78.q_ref, bf16[1024,512]{1,0:T(8,128)(2,1)} %get-tuple-element.79.k_ref, bf16[1024,512]{1,0:T(8,128)(2,1)} %get-tuple-element.80.v_ref, bf16[1024,512]{1,0:T(8,128)(2,1)} %shard_map.186.g_ref, f32[1024,512]{1,0:T(8,128)} %get-tuple-element.119.lse_ref, ...), custom_call_target="tpu_custom_call" | custom-call | flops 3221225472 | bytes 10485760 | tf_op jit(solution)/shard_map/pallas_call | solution.py:64
  678.8 11.4 %shard_map.188 = bf16[1024,2048]{1,0:T(8,128)(2,1)} custom-call(bf16[1024,1536]{1,0:T(8,128)(2,1)} %shard_map.187.refs_0_, bf16[1024,1536]{1,0:T(8,128)(2,1)} %pad_maximum_fusion.3.refs_0_.refs_1_, bf16[1024,1536]{1,0:T(8,128)(2,1)} %collective-permute-done.8.refs_1_.refs_2_), custom_call_target="tpu_custom_call" | custom-call | flops 6442450944 | bytes 13631488 | tf_op jit(solution)/shard_map/pallas_call | solution.py:64
  690.2 7.7 convolution_convert_fusion
  697.9 2.5 add_convert_fusion.4
  702.0 3.0 add_convert_fusion.6
  706.8 19.3 %collective-permute-done.39 = bf16[2048,256]{1,0:T(8,128)(2,1)S(1)} collective-permute-done((bf16[2048,256]{1,0:T(8,128)(2,1)S(1)}, bf16[2048,256]{1,0:T(8,128)(2,1)S(1)}, u32[]{:S(2)}, u32[]{:S(2)}) %collective-permute-start.39) | collective-permute-done | bytes 1048608 | tf_op jit(solution)/shard_map/ppermute | solution.py:499
  727.6 5.4 add_convert_fusion.3
  739.5 7.4 collective-permute-done.32
  748.7 2.4 add_convert_fusion.5
  752.8 14.1 %collective-permute-done.33 = bf16[256,512]{1,0:T(8,128)(2,1)S(1)} collective-permute-done((bf16[256,512]{1,0:T(8,128)(2,1)S(1)}, bf16[256,512]{1,0:T(8,128)(2,1)S(1)}, u32[]{:S(2)}, u32[]{:S(2)}) %collective-permute-start.33) | collective-permute-done | bytes 262176 | tf_op jit(solution)/shard_map/ppermute | solution.py:499
  771.7 5.7 collective-permute-done.38
  779.1 3.4 collective-permute-done.35
  784.2 4.4 collective-permute-done.31
  789.8 2.2 collective-permute-done.36
  792.8 4.9 shard_map.189
  (181 shorter events, 74.9 us)
Async XLA Ops:
  7.2 89.3 %all-gather.14.cloned.1.call-start = ((), (), s32[]{:S(2)}) async-start(), calls=%async_computation.9 | async-start | bytes 5242880 | tf_op jit(solution)/shard_map/all_gather | solution.py:594
  7.9 46.2 %copy-start.11 = (bf16[256,2048]{1,0:T(8,128)(2,1)S(1)}, bf16[256,2048]{1,0:T(8,128)(2,1)}, u32[]{:S(2)}) copy-start(bf16[256,2048]{1,0:T(8,128)(2,1)} %param.17) | copy-start | bytes 3145732
  7.9 138.5 %all-gather.8.cloned.1.call-start = ((), (), s32[]{:S(2)}) async-start(), calls=%async_computation.3 | async-start | bytes 1310720 | tf_op jit(solution)/shard_map/all_gather | solution.py:617
  11.0 21.5 %collective-permute-start.6 = (bf16[256,1536]{1,0:T(8,128)(2,1)S(1)}, bf16[256,1536]{1,0:T(8,128)(2,1)}, u32[]{:S(2)}, u32[]{:S(2)}) collective-permute-start(bf16[256,1536]{1,0:T(8,128)(2,1)S(1)} %constant_dynamic-update-slice_fusion), channel_id=1, source_target_pairs={{0,8},{8,0},{1,9},{9,1},{2,10},{10,2},{3,11},{11,3},{4,12},{12,4},... | collective-permute-start | bytes 2359304 | tf_op jit(solution)/shard_map/ppermute | solution.py:499
  14.0 40.1 %collective-permute-start.3 = (bf16[256,2048]{1,0:T(8,128)(2,1)}, bf16[256,2048]{1,0:T(8,128)(2,1)}, u32[]{:S(2)}, u32[]{:S(2)}) collective-permute-start(bf16[256,2048]{1,0:T(8,128)(2,1)} %param.17), channel_id=1, source_target_pairs={{0,8},{8,0},{1,9},{9,1},{2,10},{10,2},{3,11},{11,3},{4,12},{12,4},... | collective-permute-start | bytes 3145736 | tf_op jit(solution)/shard_map/ppermute | solution.py:499
  35.8 37.7 %collective-permute-start.7 = (bf16[512,1536]{1,0:T(8,128)(2,1)}, bf16[512,1536]{1,0:T(8,128)(2,1)}, u32[]{:S(2)}, u32[]{:S(2)}) collective-permute-start(bf16[512,1536]{1,0:T(8,128)(2,1)} %pad_maximum_fusion.10), channel_id=1, source_target_pairs={{0,16},{16,0},{1,17},{17,1},{2,18},{18,2},{3,19},{19,3},{4,20},{20... | collective-permute-start | bytes 4718600 | tf_op jit(solution)/shard_map/ppermute | solution.py:499
  38.6 38.2 %collective-permute-start = (f32[8,128]{1,0:T(8,128)S(1)}, f32[8,128]{1,0:T(8,128)S(1)}, u32[]{:S(2)}, u32[]{:S(2)}) collective-permute-start(f32[8,128]{1,0:T(8,128)S(1)} %broadcast_in_dim.14), channel_id=1, source_target_pairs={{0,16},{16,0},{1,17},{17,1},{2,18},{18,2},{3,19},{19,3},{4,20},{20... | collective-permute-start | bytes 12296 | tf_op jit(solution)/shard_map/ppermute | solution.py:499
  38.7 54.7 %collective-permute-start.5 = (bf16[256,2048]{1,0:T(8,128)(2,1)}, bf16[256,2048]{1,0:T(8,128)(2,1)S(1)}, u32[]{:S(2)}, u32[]{:S(2)}) collective-permute-start(bf16[256,2048]{1,0:T(8,128)(2,1)} %param.18), channel_id=1, source_target_pairs={{0,16},{16,0},{1,17},{17,1},{2,18},{18,2},{3,19},{19,3},{4,20},{20... | collective-permute-start | bytes 3145736 | tf_op jit(solution)/shard_map/ppermute | solution.py:499
  40.7 14.9 %copy-start.12 = (bf16[2048,256]{1,0:T(8,128)(2,1)S(1)}, bf16[2048,256]{1,0:T(8,128)(2,1)}, u32[]{:S(2)}) copy-start(bf16[2048,256]{1,0:T(8,128)(2,1)} %param.19) | copy-start | bytes 3145732
  40.7 32.9 %copy-start.5 = (bf16[256,1536]{1,0:T(8,128)(2,1)S(1)}, bf16[256,1536]{1,0:T(8,128)(2,1)}, u32[]{:S(2)}) copy-start(bf16[256,1536]{1,0:T(8,128)(2,1)} %copy-done.4) | copy-start | bytes 2359300
  55.6 37.7 %copy-start.15 = (bf16[256,2048]{1,0:T(8,128)(2,1)S(1)}, bf16[256,2048]{1,0:T(8,128)(2,1)}, u32[]{:S(2)}) copy-start(bf16[256,2048]{1,0:T(8,128)(2,1)} %param.18) | copy-start | bytes 3145732
  55.6 39.2 %collective-permute-start.4 = (bf16[2048,256]{1,0:T(8,128)(2,1)S(1)}, bf16[2048,256]{1,0:T(8,128)(2,1)S(1)}, u32[]{:S(2)}, u32[]{:S(2)}) collective-permute-start(bf16[2048,256]{1,0:T(8,128)(2,1)S(1)} %copy-done.12), channel_id=1, source_target_pairs={{0,8},{8,0},{1,9},{9,1},{2,10},{10,2},{3,11},{11,3},{4,12},{12,4},... | collective-permute-start | bytes 3145736 | tf_op jit(solution)/shard_map/ppermute | solution.py:499
  76.8 22.6 %collective-permute-start.8 = (bf16[1024,1536]{1,0:T(8,128)(2,1)}, bf16[1024,1536]{1,0:T(8,128)(2,1)}, u32[]{:S(2)}, u32[]{:S(2)}) collective-permute-start(bf16[1024,1536]{1,0:T(8,128)(2,1)} %pad_maximum_fusion.3.refs_0_.refs_1_), channel_id=1, source_target_pairs={{0,4},{4,0},{1,5},{5,1},{2,6},{6,2},{3,7},{7,3},{8,12},{12,8},{9,1... | collective-permute-start | bytes 9437192 | tf_op jit(solution)/shard_map/ppermute | solution.py:499
  76.8 4.0 collective-permute-start.1
  80.9 1.6 collective-permute-start.2
  96.4 45.4 %collective-permute-start.9 = (bf16[512,2048]{1,0:T(8,128)(2,1)}, bf16[512,2048]{1,0:T(8,128)(2,1)}, u32[]{:S(2)}, u32[]{:S(2)}) collective-permute-start(bf16[512,2048]{1,0:T(8,128)(2,1)} %pad_maximum_fusion.6), channel_id=1, source_target_pairs={{0,8},{8,0},{1,9},{9,1},{2,10},{10,2},{3,11},{11,3},{4,12},{12,4},... | collective-permute-start | bytes 6291464 | tf_op jit(solution)/shard_map/ppermute | solution.py:499
  97.9 48.3 %collective-permute-start.10 = (bf16[512,2048]{1,0:T(8,128)(2,1)S(1)}, bf16[512,2048]{1,0:T(8,128)(2,1)}, u32[]{:S(2)}, u32[]{:S(2)}) collective-permute-start(bf16[512,2048]{1,0:T(8,128)(2,1)S(1)} %pad_maximum_fusion.4), channel_id=1, source_target_pairs={{0,16},{16,0},{1,17},{17,1},{2,18},{18,2},{3,19},{19,3},{4,20},{20... | collective-permute-start | bytes 6291464 | tf_op jit(solution)/shard_map/ppermute | solution.py:499
  99.4 128.2 %all-gather.16.cloned.1.call-start = ((), (), s32[]{:S(2)}) async-start(), calls=%async_computation.10 | async-start | bytes 5242880 | tf_op jit(solution)/shard_map/all_gather | solution.py:628
  113.3 28.5 %copy-start.3 = (bf16[512,2048]{1,0:T(8,128)(2,1)S(1)}, bf16[512,2048]{1,0:T(8,128)(2,1)}, u32[]{:S(2)}) copy-start(bf16[512,2048]{1,0:T(8,128)(2,1)} %pad_maximum_fusion.6) | copy-start | bytes 6291460
  146.1 219.0 %reduce-scatter.4.cloned.1.call-start = ((), (), s32[]{:S(2)}) async-start(), calls=%async_computation.4 | async-start | bytes 5242880 | tf_op jit(solution)/shard_map/reduce_scatter | solution.py:597
  146.4 66.9 %copy-start.2 = (bf16[2048,512]{1,0:T(8,128)(2,1)S(1)}, bf16[2048,512]{1,0:T(8,128)(2,1)}, u32[]{:S(2)}) copy-start(bf16[2048,512]{1,0:T(8,128)(2,1)} %pad_maximum_fusion.5) | copy-start | bytes 6291460
  146.4 26.4 %collective-permute-start.11 = (bf16[2048,256]{1,0:T(8,128)(2,1)}, bf16[2048,256]{1,0:T(8,128)(2,1)S(1)}, u32[]{:S(2)}, u32[]{:S(2)}) collective-permute-start(bf16[2048,256]{1,0:T(8,128)(2,1)} %all-gather.8.cloned.1.call-done), channel_id=1, source_target_pairs={{0,16},{16,0},{1,17},{17,1},{2,18},{18,2},{3,19},{19,3},{4,20},{20... | collective-permute-start | bytes 3145736 | tf_op jit(solution)/shard_map/ppermute | solution.py:499
  147.4 66.0 %collective-permute-start.13 = (bf16[2048,512]{1,0:T(8,128)(2,1)}, bf16[2048,512]{1,0:T(8,128)(2,1)S(1)}, u32[]{:S(2)}, u32[]{:S(2)}) collective-permute-start(bf16[2048,512]{1,0:T(8,128)(2,1)} %pad_maximum_fusion.5), channel_id=1, source_target_pairs={{0,16},{16,0},{1,17},{17,1},{2,18},{18,2},{3,19},{19,3},{4,20},{20... | collective-permute-start | bytes 6291464 | tf_op jit(solution)/shard_map/ppermute | solution.py:499
  174.2 41.8 %copy-start.10 = (bf16[2048,256]{1,0:T(8,128)(2,1)S(1)}, bf16[2048,256]{1,0:T(8,128)(2,1)}, u32[]{:S(2)}) copy-start(bf16[2048,256]{1,0:T(8,128)(2,1)} %all-gather.8.cloned.1.call-done) | copy-start | bytes 3145732
  174.2 41.7 %collective-permute-start.12 = (bf16[2048,512]{1,0:T(8,128)(2,1)S(1)}, bf16[2048,512]{1,0:T(8,128)(2,1)S(1)}, u32[]{:S(2)}, u32[]{:S(2)}) collective-permute-start(bf16[2048,512]{1,0:T(8,128)(2,1)S(1)} %pad_maximum_fusion.7), channel_id=1, source_target_pairs={{0,8},{8,0},{1,9},{9,1},{2,10},{10,2},{3,11},{11,3},{4,12},{12,4},... | collective-permute-start | bytes 6291464 | tf_op jit(solution)/shard_map/ppermute | solution.py:499
  227.6 7.5 collective-permute-start.14
  229.7 22.2 %copy-start.13 = (bf16[1024,2048]{1,0:T(8,128)(2,1)}, bf16[1024,2048]{1,0:T(8,128)(2,1)S(1)}, u32[]{:S(2)}) copy-start(bf16[1024,2048]{1,0:T(8,128)(2,1)S(1)} %constant_dynamic-update-slice_fusion.3.refs_0_.refs_2_) | copy-start | bytes 12582916
  229.7 22.2 %copy-start.7 = (bf16[2048,1024]{1,0:T(8,128)(2,1)S(1)}, bf16[2048,1024]{1,0:T(8,128)(2,1)}, u32[]{:S(2)}) copy-start(bf16[2048,1024]{1,0:T(8,128)(2,1)} %pad_maximum_fusion.2.refs_1_.refs_0_) | copy-start | bytes 12582916
  229.7 22.4 %collective-permute-start.15 = (bf16[1024,2048]{1,0:T(8,128)(2,1)S(1)}, bf16[1024,2048]{1,0:T(8,128)(2,1)}, u32[]{:S(2)}, u32[]{:S(2)}) collective-permute-start(bf16[1024,2048]{1,0:T(8,128)(2,1)S(1)} %constant_dynamic-update-slice_fusion.3.refs_0_.refs_2_), channel_id=1, source_target_pairs={{0,4},{4,0},{1,5},{5,1},{2,6},{6,2},{3,7},{7,3},{8,12},{12,8},{9,1... | collective-permute-start | bytes 12582920 | tf_op jit(solution)/shard_map/ppermute | solution.py:499
  230.5 21.6 %collective-permute-start.16 = (bf16[1024,2048]{1,0:T(8,128)(2,1)S(1)}, bf16[1024,2048]{1,0:T(8,128)(2,1)}, u32[]{:S(2)}, u32[]{:S(2)}) collective-permute-start(bf16[1024,2048]{1,0:T(8,128)(2,1)S(1)} %copy-done.6), channel_id=1, source_target_pairs={{0,4},{4,0},{1,5},{5,1},{2,6},{6,2},{3,7},{7,3},{8,12},{12,8},{9,1... | collective-permute-start | bytes 12582920 | tf_op jit(solution)/shard_map/ppermute | solution.py:499
  251.9 23.8 %collective-permute-start.17 = (bf16[2048,1024]{1,0:T(8,128)(2,1)S(1)}, bf16[2048,1024]{1,0:T(8,128)(2,1)}, u32[]{:S(2)}, u32[]{:S(2)}) collective-permute-start(bf16[2048,1024]{1,0:T(8,128)(2,1)S(1)} %copy-done.7), channel_id=1, source_target_pairs={{0,4},{4,0},{1,5},{5,1},{2,6},{6,2},{3,7},{7,3},{8,12},{12,8},{9,1... | collective-permute-start | bytes 12582920 | tf_op jit(solution)/shard_map/ppermute | solution.py:499
  289.7 162.0 %all-gather.10.cloned.1.call-start = ((), (), s32[]{:S(2)}) async-start(), calls=%async_computation.5 | async-start | bytes 5242880 | tf_op jit(solution)/shard_map/all_gather | solution.py:594
  370.1 200.2 %reduce-scatter.6.cloned.1.call-start = ((), (), s32[]{:S(2)}) async-start(), calls=%async_computation.6 | async-start | bytes 5242880 | tf_op jit(solution)/shard_map/reduce_scatter | solution.py:597
  372.5 3.7 collective-permute-start.18
  376.8 3.7 collective-permute-start.19
  381.2 1.2 collective-permute-start.20
  382.4 3.7 collective-permute-start.21
  386.1 6.3 collective-permute-start.22
  494.8 162.1 %all-gather.12.cloned.1.call-start = ((), (), s32[]{:S(2)}) async-start(), calls=%async_computation.7 | async-start | bytes 5242880 | tf_op jit(solution)/shard_map/all_gather | solution.py:594
  494.9 7.7 copy-start.19
  494.9 7.7 copy-start.21
  502.5 12.9 %collective-permute-start.23 = (bf16[1024,2048]{1,0:T(8,128)(2,1)S(1)}, bf16[1024,2048]{1,0:T(8,128)(2,1)S(1)}, u32[]{:S(2)}, u32[]{:S(2)}) collective-permute-start(bf16[1024,2048]{1,0:T(8,128)(2,1)S(1)} %convolution_convert_fusion.3), channel_id=1, source_target_pairs={{0,4},{4,0},{1,5},{5,1},{2,6},{6,2},{3,7},{7,3},{8,12},{12,8},{9,1... | collective-permute-start | bytes 12582920 | tf_op jit(solution)/shard_map/ppermute | solution.py:499
  507.7 17.3 %collective-permute-start.25 = (bf16[1024,2048]{1,0:T(8,128)(2,1)S(1)}, bf16[1024,2048]{1,0:T(8,128)(2,1)S(1)}, u32[]{:S(2)}, u32[]{:S(2)}) collective-permute-start(bf16[1024,2048]{1,0:T(8,128)(2,1)S(1)} %convolution_convert_fusion.1), channel_id=1, source_target_pairs={{0,4},{4,0},{1,5},{5,1},{2,6},{6,2},{3,7},{7,3},{8,12},{12,8},{9,1... | collective-permute-start | bytes 12582920 | tf_op jit(solution)/shard_map/ppermute | solution.py:499
  515.3 17.7 %collective-permute-start.24 = (bf16[2048,1024]{1,0:T(8,128)(2,1)S(1)}, bf16[2048,1024]{1,0:T(8,128)(2,1)S(1)}, u32[]{:S(2)}, u32[]{:S(2)}) collective-permute-start(bf16[2048,1024]{1,0:T(8,128)(2,1)S(1)} %convolution_convert_fusion.2), channel_id=1, source_target_pairs={{0,4},{4,0},{1,5},{5,1},{2,6},{6,2},{3,7},{7,3},{8,12},{12,8},{9,1... | collective-permute-start | bytes 12582920 | tf_op jit(solution)/shard_map/ppermute | solution.py:499
  525.0 8.1 copy-start.22
  575.6 217.3 %reduce-scatter.8.cloned.1.call-start = ((), (), s32[]{:S(2)}) async-start(), calls=%async_computation.8 | async-start | bytes 5242880 | tf_op jit(solution)/shard_map/reduce_scatter | solution.py:597
  575.6 6.5 copy-start.9
  580.6 48.8 %collective-permute-start.26 = (bf16[512,2048]{1,0:T(8,128)(2,1)}, bf16[512,2048]{1,0:T(8,128)(2,1)}, u32[]{:S(2)}, u32[]{:S(2)}) collective-permute-start(bf16[512,2048]{1,0:T(8,128)(2,1)} %get-tuple-element.138), channel_id=1, source_target_pairs={{0,16},{16,0},{1,17},{17,1},{2,18},{18,2},{3,19},{19,3},{4,20},{20... | collective-permute-start | bytes 6291464 | tf_op jit(solution)/shard_map/ppermute | solution.py:499
  585.2 47.4 %collective-permute-start.27 = (bf16[2048,512]{1,0:T(8,128)(2,1)}, bf16[2048,512]{1,0:T(8,128)(2,1)}, u32[]{:S(2)}, u32[]{:S(2)}) collective-permute-start(bf16[2048,512]{1,0:T(8,128)(2,1)} %pad_maximum_fusion.9), channel_id=1, source_target_pairs={{0,8},{8,0},{1,9},{9,1},{2,10},{10,2},{3,11},{11,3},{4,12},{12,4},... | collective-permute-start | bytes 6291464 | tf_op jit(solution)/shard_map/ppermute | solution.py:499
  589.3 89.5 %collective-permute-start.28 = (bf16[512,2048]{1,0:T(8,128)(2,1)}, bf16[512,2048]{1,0:T(8,128)(2,1)}, u32[]{:S(2)}, u32[]{:S(2)}) collective-permute-start(bf16[512,2048]{1,0:T(8,128)(2,1)} %get-tuple-element.134), channel_id=1, source_target_pairs={{0,16},{16,0},{1,17},{17,1},{2,18},{18,2},{3,19},{19,3},{4,20},{20... | collective-permute-start | bytes 6291464 | tf_op jit(solution)/shard_map/ppermute | solution.py:499
  697.8 29.7 %collective-permute-start.29 = (bf16[1024,1536]{1,0:T(8,128)(2,1)}, bf16[1024,1536]{1,0:T(8,128)(2,1)}, u32[]{:S(2)}, u32[]{:S(2)}) collective-permute-start(bf16[1024,1536]{1,0:T(8,128)(2,1)} %convolution_convert_fusion), channel_id=1, source_target_pairs={{0,4},{4,0},{1,5},{5,1},{2,6},{6,2},{3,7},{7,3},{8,12},{12,8},{9,1... | collective-permute-start | bytes 9437192 | tf_op jit(solution)/shard_map/ppermute | solution.py:499
  700.4 25.6 %collective-permute-start.39 = (bf16[2048,256]{1,0:T(8,128)(2,1)S(1)}, bf16[2048,256]{1,0:T(8,128)(2,1)S(1)}, u32[]{:S(2)}, u32[]{:S(2)}) collective-permute-start(bf16[2048,256]{1,0:T(8,128)(2,1)S(1)} %slice.159), channel_id=1, source_target_pairs={{0,16},{16,0},{1,17},{17,1},{2,18},{18,2},{3,19},{19,3},{4,20},{20... | collective-permute-start | bytes 3145736 | tf_op jit(solution)/shard_map/ppermute | solution.py:499
  702.0 25.6 %copy-start.20 = (bf16[1024,2048]{1,0:T(8,128)(2,1)S(1)}, bf16[1024,2048]{1,0:T(8,128)(2,1)}, u32[]{:S(2)}) copy-start(bf16[1024,2048]{1,0:T(8,128)(2,1)} %get-tuple-element.122) | copy-start | bytes 12582916
  705.1 22.5 %copy-start.18 = (bf16[1024,1536]{1,0:T(8,128)(2,1)S(1)}, bf16[1024,1536]{1,0:T(8,128)(2,1)}, u32[]{:S(2)}) copy-start(bf16[1024,1536]{1,0:T(8,128)(2,1)} %shard_map.187.refs_0_) | copy-start | bytes 9437188
  705.2 29.6 %collective-permute-start.37 = (bf16[256,2048]{1,0:T(8,128)(2,1)S(1)}, bf16[256,2048]{1,0:T(8,128)(2,1)S(1)}, u32[]{:S(2)}, u32[]{:S(2)}) collective-permute-start(bf16[256,2048]{1,0:T(8,128)(2,1)S(1)} %constant_dynamic-slice_fusion.1), channel_id=1, source_target_pairs={{0,8},{8,0},{1,9},{9,1},{2,10},{10,2},{3,11},{11,3},{4,12},{12,4},... | collective-permute-start | bytes 3145736 | tf_op jit(solution)/shard_map/ppermute | solution.py:499
  733.2 13.7 %collective-permute-start.32 = (bf16[512,512]{1,0:T(8,128)(2,1)S(1)}, bf16[512,512]{1,0:T(8,128)(2,1)S(1)}, u32[]{:S(2)}, u32[]{:S(2)}) collective-permute-start(bf16[512,512]{1,0:T(8,128)(2,1)S(1)} %pad_maximum_fusion.13), channel_id=1, source_target_pairs={{0,8},{8,0},{1,9},{9,1},{2,10},{10,2},{3,11},{11,3},{4,12},{12,4},... | collective-permute-start | bytes 1572872 | tf_op jit(solution)/shard_map/ppermute | solution.py:499
  736.6 12.1 %copy-start = (bf16[512,2048]{1,0:T(8,128)(2,1)S(1)}, bf16[512,2048]{1,0:T(8,128)(2,1)}, u32[]{:S(2)}) copy-start(bf16[512,2048]{1,0:T(8,128)(2,1)} %get-tuple-element.130) | copy-start | bytes 6291460
  736.6 31.2 %collective-permute-start.30 = (bf16[512,1024]{1,0:T(8,128)(2,1)S(1)}, bf16[512,1024]{1,0:T(8,128)(2,1)S(1)}, u32[]{:S(2)}, u32[]{:S(2)}) collective-permute-start(bf16[512,1024]{1,0:T(8,128)(2,1)S(1)} %slice.151), channel_id=1, source_target_pairs={{0,16},{16,0},{1,17},{17,1},{2,18},{18,2},{3,19},{19,3},{4,20},{20... | collective-permute-start | bytes 3145736 | tf_op jit(solution)/shard_map/ppermute | solution.py:499
  739.5 29.3 %collective-permute-start.34 = (bf16[512,1024]{1,0:T(8,128)(2,1)S(1)}, bf16[512,1024]{1,0:T(8,128)(2,1)S(1)}, u32[]{:S(2)}, u32[]{:S(2)}) collective-permute-start(bf16[512,1024]{1,0:T(8,128)(2,1)S(1)} %fusion.12), channel_id=1, source_target_pairs={{0,4},{4,0},{1,5},{5,1},{2,6},{6,2},{3,7},{7,3},{8,12},{12,8},{9,1... | collective-permute-start | bytes 3145736 | tf_op jit(solution)/shard_map/ppermute | solution.py:499
  747.1 19.8 %collective-permute-start.33 = (bf16[256,512]{1,0:T(8,128)(2,1)S(1)}, bf16[256,512]{1,0:T(8,128)(2,1)S(1)}, u32[]{:S(2)}, u32[]{:S(2)}) collective-permute-start(bf16[256,512]{1,0:T(8,128)(2,1)S(1)} %slice.157), channel_id=1, source_target_pairs={{0,16},{16,0},{1,17},{17,1},{2,18},{18,2},{3,19},{19,3},{4,20},{20... | collective-permute-start | bytes 786440 | tf_op jit(solution)/shard_map/ppermute | solution.py:499
  751.2 26.2 %collective-permute-start.38 = (bf16[256,2048]{1,0:T(8,128)(2,1)S(1)}, bf16[256,2048]{1,0:T(8,128)(2,1)S(1)}, u32[]{:S(2)}, u32[]{:S(2)}) collective-permute-start(bf16[256,2048]{1,0:T(8,128)(2,1)S(1)} %constant_dynamic-slice_fusion), channel_id=1, source_target_pairs={{0,8},{8,0},{1,9},{9,1},{2,10},{10,2},{3,11},{11,3},{4,12},{12,4},... | collective-permute-start | bytes 3145736 | tf_op jit(solution)/shard_map/ppermute | solution.py:499
  768.2 20.4 %collective-permute-start.31 = (bf16[256,1024]{1,0:T(8,128)(2,1)S(1)}, bf16[256,1024]{1,0:T(8,128)(2,1)S(1)}, u32[]{:S(2)}, u32[]{:S(2)}) collective-permute-start(bf16[256,1024]{1,0:T(8,128)(2,1)S(1)} %constant_dynamic-slice_fusion.7), channel_id=1, source_target_pairs={{0,8},{8,0},{1,9},{9,1},{2,10},{10,2},{3,11},{11,3},{4,12},{12,4},... | collective-permute-start | bytes 1572872 | tf_op jit(solution)/shard_map/ppermute | solution.py:499
  770.1 12.4 %collective-permute-start.35 = (bf16[512,512]{1,0:T(8,128)(2,1)S(1)}, bf16[512,512]{1,0:T(8,128)(2,1)S(1)}, u32[]{:S(2)}, u32[]{:S(2)}) collective-permute-start(bf16[512,512]{1,0:T(8,128)(2,1)S(1)} %slice.145), channel_id=1, source_target_pairs={{0,16},{16,0},{1,17},{17,1},{2,18},{18,2},{3,19},{19,3},{4,20},{20... | collective-permute-start | bytes 1572872 | tf_op jit(solution)/shard_map/ppermute | solution.py:499
  782.7 9.3 %collective-permute-start.36 = (bf16[512,256]{1,0:T(8,128)(2,1)S(1)}, bf16[512,256]{1,0:T(8,128)(2,1)S(1)}, u32[]{:S(2)}, u32[]{:S(2)}) collective-permute-start(bf16[512,256]{1,0:T(8,128)(2,1)S(1)} %constant_dynamic-slice_fusion.2), channel_id=1, source_target_pairs={{0,8},{8,0},{1,9},{9,1},{2,10},{10,2},{3,11},{11,3},{4,12},{12,4},... | collective-permute-start | bytes 786440 | tf_op jit(solution)/shard_map/ppermute | solution.py:499
  (7 other events, 28.0 us)
Sparse Core Ops, SparseCore 0:
  9.6 83.4 all-gather.13
  99.5 27.2 all-gather.7
  146.3 81.2 all-gather.15
  289.8 75.2 reduce-scatter.3
  370.2 81.4 all-gather.9
  495.0 75.2 reduce-scatter.5
  575.7 81.2 all-gather.11
  698.0 75.4 reduce-scatter.7
